TPU v7x, 32 devices: a whole 2x2x4 slice. The times are simulated.
32 devices in a mesh: groups: 2 (over x), gx: 16 (over z, y, core).
Axes of the slice: x: 2, y: 2, z: 4, core: 2. Of those that a mesh axis runs over, the one named last changes fastest.
Arguments:
- features: bfloat16 [128, 8, 8, 8, 128], P(('groups', 'gx')), parts along dimension 0, may hold values from -6 to 6
- fine_nbr: int32 [128, 27], P(('groups', 'gx')), parts along dimension 0, may hold values from -1 to 3, as said below
- fine_send: int32 [32, 2, 4], P(('groups', 'gx')), parts along dimension 0, may hold values from -1 to 3, as said below
- fine_parent: int32 [128], P(('groups', 'gx')), parts along dimension 0, may hold values from -1 to 127, as said below
- coarse_child: int32 [32, 8], P(('groups', 'gx')), parts along dimension 0, may hold values from -1 to 63, as said below
- coarse_nbr: int32 [32, 27], P(('groups', 'gx')), parts along dimension 0, may hold values from -1 to 15, as said below
- enc_fine_w: bfloat16 [27, 128, 128], replicated, may hold values from -0.15625 to 0.15625
- enc_coarse_w: bfloat16 [27, 128, 128], replicated, may hold values from -0.15625 to 0.15625
- dec_coarse_w: bfloat16 [27, 128, 128], replicated, may hold values from -0.15625 to 0.15625
- dec_fine_w: bfloat16 [27, 128, 128], replicated, may hold values from -0.15625 to 0.15625
Outputs:
- fine_out: bfloat16 [128, 8, 8, 8, 128], P(('groups', 'gx')), parts along dimension 0
There are 2 independent parts, one for each index of `groups`. A program takes and returns all parts, laid end to end along the dimension named above; an argument that names none is the same for every part. Nothing has to cross between parts.
Inputs may be any that keep to these rules, and one draw needn't show every extreme that they name: `fine_nbr`: entry t of a fine slot on gx device d names the slot, on device d + dx, of the brick at brick offset (dx, dy, dz), or is -1 where there is none. A slot whose entry 13 is -1 holds no brick and all its entries are -1; entry 13 of a brick is its own slot. Adjacency is symmetric. `fine_send`: on device d, entry s of row 0 is s when slot s holds a brick with a neighbour on device d + 1, else -1; row 1 likewise for device d - 1. `fine_parent`: 8 g + o for a brick whose parent is coarse slot g at octant o, -1 for slots without a brick. Coarse slot g is held by gx device g, which lies in the same aligned group of four gx devices as the child's device. `coarse_child`: entry o of coarse slot g is the fine slot f with fine_parent[f] = 8 g + o, or -1 where there is none. `coarse_nbr`: entry t (taps ordered as for fine_nbr) is the coarse slot of the neighbouring coarse brick, or -1 where there is none; entry 13 is the brick's own slot; every neighbour is held by a gx device of the same or an adjacent aligned group of four, and neighbours with dx = 0 by a device of the same aligned group of four.
All inputs are finite; a program needn't handle non-finite values.
Results may differ from a plain program's by a relative error of at most 0.01.
Values may be sent and summed in bfloat16 or wider, within the bound.
No kernel may reach another device: no remote copies, remote signals or barrier semaphores. Data moves between devices by JAX's collectives and lax.ppermute only.
A program may use at most 128 MiB of HBM per device.

v0:
```python
import functools

import jax
import jax.numpy as jnp
from jax import lax
from jax.experimental import pallas as pl
from jax.experimental.pallas import tpu as pltpu
from jax.sharding import PartitionSpec as P

LANES = 4
OFFSETS = (-1, 0, 1)
BF16 = jnp.bfloat16
F32 = jnp.float32
VMEM = pl.BlockSpec(memory_space=pltpu.VMEM)
SMEM = pl.BlockSpec(memory_space=pltpu.SMEM)
PARAMS = pltpu.CompilerParams(vmem_limit_bytes=60 << 20)


def tap(dx, dy, dz):
    return 9 * (dx + 1) + 3 * (dy + 1) + dz + 1


def z_shifts(center, below, above):
    edge = center.shape[1]
    z = lax.broadcasted_iota(jnp.int32, center.shape, 1)
    down = jnp.where(z == 0, pltpu.roll(below, 1, 1), pltpu.roll(center, 1, 1))
    up = jnp.where(z == edge - 1, pltpu.roll(above, edge - 1, 1), pltpu.roll(center, edge - 1, 1))
    return down, center, up


def columns(fetch, edge):
    parts = []
    for dy in OFFSETS:
        triple = [fetch(dy, dz) for dz in (0, -1, 1)]
        planes, rows, _, width = triple[0].shape
        flat = [v.reshape(planes * rows, edge, width) for v in triple]
        parts.append([s.reshape(planes, rows, edge, width) for s in z_shifts(*flat)])
    return [jnp.concatenate([part[k] for part in parts], axis=1) for k in range(3)]


def y_rows(load, dy, edge):
    if dy == 0:
        value = load(0, edge * edge)
    elif dy < 0:
        value = load(edge * edge - 2 * edge, 2 * edge)[:, edge:]
    else:
        value = load(0, 2 * edge)[:, :edge]
    planes, rows, width = value.shape
    return value.reshape(planes, rows // edge, edge, width)


def inner_kernel(nbr, x_ref, w_ref, out_ref, part_ref, even, odd):
    slots, edge, rows, width = x_ref.shape
    even[:, :, 0] = jnp.zeros_like(even[:, :, 0])
    even[:, :, edge + 1] = jnp.zeros_like(even[:, :, 0])
    odd[:, :, 0] = jnp.zeros_like(odd[:, :, 0])
    odd[:, :, edge + 1] = jnp.zeros_like(odd[:, :, 0])
    for b in range(slots):

        def fetch(dy, dz):
            slot = nbr[b, tap(0, dy, dz)]
            held = jnp.maximum(slot, 0)
            value = y_rows(lambda r, n: x_ref[held, :, r : r + n, :].astype(F32), dy, edge)
            return jnp.where(slot >= 0, value, 0.0)

        for k, full in enumerate(columns(fetch, edge)):
            even[b, k, 1 : edge + 1] = full.reshape(edge, rows + 2 * edge, width).astype(BF16)
            odd[b, k, 1 : edge + 1] = full[:, 1 : edge + 1].reshape(edge, rows, width).astype(BF16)
        taps = []
        for dx in range(3):
            for dy in OFFSETS:
                for k in range(3):
                    if dy == 0:
                        piece = odd[b, k, dx : dx + edge]
                    else:
                        first = (dy + 1) * edge
                        piece = even[b, k, dx : dx + edge, first : first + rows]
                    taps.append(piece.reshape(edge * rows, width))
        total = jnp.dot(jnp.concatenate(taps, axis=1), w_ref[...], preferred_element_type=F32)
        total = total.reshape(edge, rows, width)
        out_ref[b] = jnp.maximum(total, 0.0).astype(BF16)
        part_ref[b, 0] = total[0]
        part_ref[b, 1] = total[edge - 1]


def inner(x, nbr, weights):
    slots, edge, rows, width = x.shape
    return pl.pallas_call(
        inner_kernel,
        out_shape=(
            jax.ShapeDtypeStruct(x.shape, BF16),
            jax.ShapeDtypeStruct((slots, 2, rows, width), F32),
        ),
        in_specs=[SMEM, VMEM, VMEM],
        out_specs=(VMEM, VMEM),
        scratch_shapes=[
            pltpu.VMEM((slots, 3, edge + 2, rows + 2 * edge, width), BF16),
            pltpu.VMEM((slots, 3, edge + 2, rows, width), BF16),
        ],
        compiler_params=PARAMS,
        cost_estimate=pl.CostEstimate(
            flops=2 * slots * edge * rows * 27 * width * width,
            bytes_accessed=4 << 20,
            transcendentals=0,
        ),
        name="inner",
    )(nbr, x, weights)


def outer_planes(nbr, info, near_ref, far_ref, part_ref, w_ref, out_ref):
    slots, _, rows, width = part_ref.shape
    edge = rows // (rows // 8)
    is_odd = info[0, 0] == 1
    for side, dx in enumerate((-1, 1)):
        use_near = is_odd if side == 0 else jnp.logical_not(is_odd)
        bricks = []
        for b in range(slots):

            def fetch(dy, dz):
                slot = nbr[b, tap(dx, dy, dz)]
                held = jnp.maximum(slot, 0)

                def load(r, n):
                    near = near_ref[held, r : r + n, :].astype(F32)
                    far = far_ref[held, r : r + n, :].astype(F32)
                    return jnp.where(use_near, near, far)[None]

                return jnp.where(slot >= 0, y_rows(load, dy, edge), 0.0)

            shifted = columns(fetch, edge)
            taps = []
            for first in range(3):
                for k in range(3):
                    piece = shifted[k][0, first : first + edge]
                    taps.append(piece.reshape(rows, width).astype(BF16))
            bricks.append(jnp.concatenate(taps, axis=1))
        count = 9 * width
        start = 0 if side == 0 else 2 * count
        extra = jnp.dot(
            jnp.concatenate(bricks, axis=0),
            w_ref[start : start + count],
            preferred_element_type=F32,
        ).reshape(slots, rows, width)
        plane = 0 if side == 0 else out_ref.shape[1] - 1
        for b in range(slots):
            total = part_ref[b, side] + extra[b]
            out_ref[b, plane] = jnp.maximum(total, 0.0).astype(BF16)


def outer_kernel(nbr, info, near_ref, far_ref, part_ref, w_ref, main_ref, out_ref):
    out_ref[:, 1 : out_ref.shape[1] - 1] = main_ref[:, 1 : out_ref.shape[1] - 1]
    outer_planes(nbr, info, near_ref, far_ref, part_ref, w_ref, out_ref)


def outer(main, part, near, far, nbr, info, weights):
    return pl.pallas_call(
        outer_kernel,
        out_shape=jax.ShapeDtypeStruct(main.shape, BF16),
        in_specs=[SMEM, SMEM, VMEM, VMEM, VMEM, VMEM, VMEM],
        out_specs=VMEM,
        compiler_params=PARAMS,
        name="outer",
    )(nbr, info, near, far, part, weights, main)


def outer_pool_kernel(
    nbr, info, parent, near_ref, far_ref, part_ref, w_ref, main_ref, out_ref, pool_ref, rim_ref, sums
):
    slots, edge, rows, width = out_ref.shape
    half = edge // 2
    out_ref[:, 1 : edge - 1] = main_ref[:, 1 : edge - 1]
    outer_planes(nbr, info, near_ref, far_ref, part_ref, w_ref, out_ref)
    cells = half**3
    for b in range(slots):
        value = out_ref[b].astype(F32).reshape(half, 2, half, 2, edge, width)
        value = (value[:, 0, :, 0] + value[:, 0, :, 1]) + (value[:, 1, :, 0] + value[:, 1, :, 1])
        sums[b] = value.reshape(half * half * edge, width)
        low = sums[b, pl.ds(0, cells, stride=2), :]
        high = sums[b, pl.ds(1, cells, stride=2), :]
        pooled = (low + high) * 0.125
        pool_ref[b * cells : (b + 1) * cells, :] = pooled.astype(BF16)
        outer_x = (jnp.maximum(parent[0, b], 0) >> 2) & 1
        rim = jnp.where(outer_x == 0, pooled[: cells // 2], pooled[cells // 2 :])
        rim_ref[b * cells // 2 : (b + 1) * cells // 2, :] = rim.astype(BF16)


def outer_pool(main, part, near, far, nbr, info, parent, weights):
    slots, edge, rows, width = main.shape
    cells = (edge // 2) ** 3
    return pl.pallas_call(
        outer_pool_kernel,
        out_shape=(
            jax.ShapeDtypeStruct(main.shape, BF16),
            jax.ShapeDtypeStruct((slots * cells, width), BF16),
            jax.ShapeDtypeStruct((slots * cells // 2, width), BF16),
        ),
        in_specs=[SMEM, SMEM, SMEM, VMEM, VMEM, VMEM, VMEM, VMEM],
        out_specs=(VMEM, VMEM, VMEM),
        scratch_shapes=[pltpu.VMEM((slots, 2 * cells, width), F32)],
        compiler_params=PARAMS,
        name="outer_pool",
    )(nbr, info, parent, near, far, part, weights, main)


def source_row(rel, device, lane_y, lane_c):
    c = device & 1
    flip_y = ((device >> 1) & 1) ^ lane_y
    same = flip_y * 2 + (c ^ lane_c)
    below = 4 + 4 * lane_c + flip_y * 2 + (1 - c)
    above = 8 - 4 * lane_c + flip_y * 2 + c
    return jnp.where(rel == 0, same, jnp.where(rel < 0, below, above))


def coarse_kernel(coarse_slots, *refs):
    table, parent, info, send = refs[:4]
    blocks = refs[4:12]
    enc_ref, w1_ref, w2_ref, out_ref, near_ref, far_ref = refs[12:18]
    held, region, even, odd, mid, even2, odd2, spread, base_s, gone_s, row_s, there_s = refs[18:]
    slots, edge, rows, width = enc_ref.shape
    half = edge // 2
    plane = half * half
    cells = half * plane
    position = info[0, 1]
    group = position >> 2
    lane_y = (position >> 1) & 1
    lane_c = position & 1

    first = 0
    for ref in blocks:
        held[first : first + ref.shape[0]] = ref[...].astype(F32)
        first += ref.shape[0]
    full_rows = LANES * slots * cells
    zero_row = first
    held[zero_row : zero_row + cells] = jnp.zeros((cells, width), F32)

    def place(b, carry):
        own = parent[0, b]
        known = own >= 0
        own = jnp.maximum(own, 0)
        octant = own & 7
        brick = own >> 3
        bits = ((octant >> 2) & 1, (octant >> 1) & 1, octant & 1)
        home = source_row(0, brick // coarse_slots, lane_y, lane_c)
        home_slot = brick % coarse_slots
        sign = tuple(2 * bit - 1 for bit in bits)
        for cross in range(8):
            crossed = (cross >> 2, (cross >> 1) & 1, cross & 1)
            number = 13
            for scale, s, c in zip((9, 3, 1), sign, crossed):
                if c:
                    number = number + scale * s
            found = table[home, 8 * coarse_slots + home_slot * 27 + number]
            there_s[cross] = jnp.where(known & (found >= 0), 1, 0)
            found = jnp.maximum(found, 0)
            device = found // coarse_slots
            rel = (device >> 2) - group
            row_s[cross] = source_row(rel, device, lane_y, lane_c) * coarse_slots + found % coarse_slots
        for ex in OFFSETS:
            for ey in OFFSETS:
                for ez in OFFSETS:
                    cross = 0
                    flip = 0
                    for scale, bit, e in zip((4, 2, 1), bits, (ex, ey, ez)):
                        if e:
                            cross = cross + scale * (bit if e > 0 else 1 - bit)
                            flip += scale
                    there = there_s[cross] == 1
                    row = row_s[cross]
                    column = (row % coarse_slots) * 8 + (octant ^ flip)
                    row = row // coarse_slots
                    child = table[row, column]
                    valid = there & (child >= 0)
                    child = jnp.maximum(child, 0)
                    device = child // slots
                    slot = child % slots
                    rel = (device >> 2) - group
                    source = source_row(rel, device, lane_y, lane_c)
                    whole = (source * slots + slot) * cells + (2 * plane if ex < 0 else 0)
                    rim = full_rows + ((source - 4) * slots + slot) * (cells // 2)
                    base = jnp.where(rel == 0, whole, rim)
                    base = jnp.where(valid, base, zero_row)
                    base = pl.multiple_of(base, 16)
                    gone_s[b, tap(ex, ey, ez)] = jnp.where(there, 0, 1)
                    size = {-1: (0, half - 2, 2), 0: (2, 0, half), 1: (half + 2, 0, 2)}
                    x0, _, nx = size[ex]
                    y0, sy, ny = size[ey]
                    z0, sz, nz = size[ez]
                    for x in range(nx):
                        for y in range(ny):
                            at = base + (x * plane + (sy + y) * half + sz)
                            region[b, x0 + x, y0 + y, z0 : z0 + nz, :] = held[pl.ds(at, nz), :]
        return carry

    lax.fori_loop(0, slots, place, 0)

    def spread_taps(source, even_ref, odd_ref, b, size):
        value = source.reshape(-1, edge, width)
        for k in range(3):
            moved = value if k == 0 else pltpu.roll(value, edge - k, 1)
            moved = moved.reshape(size, size, edge, width)
            even_ref[b, k] = moved.reshape(size, size * edge, width).astype(BF16)
            inside = moved[:, 1 : size - 1]
            odd_ref[b, k] = inside.reshape(size, (size - 2) * edge, width).astype(BF16)

    def gather_taps(even_ref, odd_ref, size):
        inside = size - 2
        bricks = []
        for b in range(slots):
            taps = []
            for dx in range(3):
                for dy in range(3):
                    for k in range(3):
                        if dy == 1:
                            piece = odd_ref[b, k, dx : dx + inside]
                        else:
                            piece = even_ref[
                                b, k, dx : dx + inside, dy * edge : (dy + inside) * edge
                            ]
                        taps.append(piece.reshape(inside * inside * edge, width))
            bricks.append(jnp.concatenate(taps, axis=1))
        return jnp.concatenate(bricks, axis=0)

    for b in range(slots):
        spread_taps(region[b], even, odd, b, edge)
    inside = edge - 2
    coarse = jnp.dot(gather_taps(even, odd, edge), w1_ref[...], preferred_element_type=F32)
    coarse = jnp.maximum(coarse, 0.0).astype(BF16).astype(F32)
    mid[...] = coarse.reshape(slots, inside, inside, edge, width)

    def clear(b, carry):
        span = {-1: (0, 1), 0: (1, half), 1: (half + 1, 1)}
        for ex in OFFSETS:
            for ey in OFFSETS:
                for ez in OFFSETS:
                    if (ex, ey, ez) == (0, 0, 0):
                        continue

                    @pl.when(gone_s[b, tap(ex, ey, ez)] == 1)
                    def _():
                        x0, nx = span[ex]
                        y0, ny = span[ey]
                        z0, nz = span[ez]
                        mid[b, x0 : x0 + nx, y0 : y0 + ny, z0 : z0 + nz, :] = jnp.zeros(
                            (nx, ny, nz, width), F32
                        )

        return carry

    lax.fori_loop(0, slots, clear, 0)
    for b in range(slots):
        spread_taps(mid[b], even2, odd2, b, inside)
    fine = jnp.dot(gather_taps(even2, odd2, inside), w2_ref[...], preferred_element_type=F32)
    fine = jnp.maximum(fine, 0.0).astype(BF16).astype(F32)
    fine = fine.reshape(slots, plane * edge, width)
    is_odd = lane_c == 1
    for b in range(slots):
        value = jnp.where(parent[0, b] >= 0, fine[b], 0.0)
        spread[b, pl.ds(0, plane * edge, stride=2), :] = value
        spread[b, pl.ds(1, plane * edge, stride=2), :] = value
        up = spread[b].reshape(half, half, 2 * edge, width)[:, :, :edge]
        base = enc_ref[b].astype(F32).reshape(half, 2, half, 2, edge, width)
        total = base + up[:, None, :, None]
        total = total.reshape(edge, rows, width).astype(BF16)
        out_ref[b] = total
        last = jnp.where(send[0, b] == b, total[edge - 1], 0)
        head = jnp.where(send[1, b] == b, total[0], 0)
        near_ref[b] = jnp.where(is_odd, head, last)
        far_ref[b] = jnp.where(is_odd, last, head)


def coarse(table, parent, info, send, blocks, enc, w1, w2, coarse_slots):
    slots, edge, rows, width = enc.shape
    half = edge // 2
    inside = edge - 2
    total = sum(block.shape[0] for block in blocks)
    face = jax.ShapeDtypeStruct((slots, rows, width), BF16)
    return pl.pallas_call(
        functools.partial(coarse_kernel, coarse_slots),
        out_shape=(jax.ShapeDtypeStruct(enc.shape, BF16), face, face),
        in_specs=[SMEM] * 4 + [VMEM] * 11,
        out_specs=(VMEM, VMEM, VMEM),
        scratch_shapes=[
            pltpu.VMEM((total + half**3, width), F32),
            pltpu.VMEM((slots, edge, edge, edge, width), F32),
            pltpu.VMEM((slots, 3, edge, edge * edge, width), BF16),
            pltpu.VMEM((slots, 3, edge, inside * edge, width), BF16),
            pltpu.VMEM((slots, inside, inside, edge, width), F32),
            pltpu.VMEM((slots, 3, inside, inside * edge, width), BF16),
            pltpu.VMEM((slots, 3, inside, half * edge, width), BF16),
            pltpu.VMEM((slots, 2 * half * half * edge, width), F32),
            pltpu.SMEM((slots, 27), jnp.int32),
            pltpu.SMEM((slots, 27), jnp.int32),
            pltpu.SMEM((8,), jnp.int32),
            pltpu.SMEM((8,), jnp.int32),
        ],
        compiler_params=PARAMS,
        name="coarse",
    )(table, parent, info, send, *blocks, enc, w1, w2)


def per_device(
    features,
    fine_nbr,
    fine_send,
    fine_parent,
    coarse_child,
    coarse_nbr,
    enc_fine_w,
    enc_coarse_w,
    dec_coarse_w,
    dec_fine_w,
):
    slots, edge, _, _, width = features.shape
    coarse_slots = coarse_nbr.shape[0]
    size = lax.axis_size("gx")
    position = lax.axis_index("gx")
    is_odd = position % 2

    def swap(value, partner):
        pairs = [(i, partner(i)) for i in range(size) if 0 <= partner(i) < size]
        return lax.ppermute(value, "gx", pairs)

    def core(value):
        return swap(value, lambda i: i ^ 1)

    def next_chip(value):
        return swap(value, lambda i: i + 1 if i % 2 else i - 1)

    def across_y(value):
        return swap(value, lambda i: i ^ 2)

    def across_z(value):
        return swap(value, lambda i: i + 3 if i % 2 else i - 3)

    x = features.reshape(slots, edge, edge * edge, width)
    flat = [w.reshape(27 * width, width) for w in (enc_fine_w, enc_coarse_w, dec_coarse_w, dec_fine_w)]
    info = jnp.stack([is_odd, position]).astype(jnp.int32).reshape(1, 2)
    parent = fine_parent.reshape(1, slots)
    send = fine_send[0]
    listed = (send == jnp.arange(slots, dtype=jnp.int32)[None, :])[:, :, None, None]
    last = jnp.where(listed[0], x[:, edge - 1], jnp.zeros((), BF16))
    head = jnp.where(listed[1], x[:, 0], jnp.zeros((), BF16))
    far = next_chip(jnp.where(is_odd == 1, last, head))
    near = core(jnp.where(is_odd == 1, head, last))
    main, part = inner(x, fine_nbr, flat[0])
    enc, pooled, rim = outer_pool(main, part, near, far, fine_nbr, info, parent, flat[0])

    table = jnp.concatenate([coarse_child.reshape(1, -1), coarse_nbr.reshape(1, -1)], axis=1)
    table_c = core(table)
    rim_c = core(rim)
    pooled_c = core(pooled)
    chip_table = jnp.concatenate([table, table_c], axis=0)
    rim_z = across_z(jnp.concatenate([rim, rim_c], axis=0))
    table_z = across_z(chip_table)
    pooled_y = across_y(pooled)
    rim_zy = across_y(rim_z)
    table_y = across_y(chip_table)
    table_zy = across_y(table_z)
    pooled_yc = core(pooled_y)
    rim_zc = core(rim_z)
    rim_zyc = core(rim_zy)
    z_table = jnp.concatenate([table_z, table_zy], axis=0)
    tables = jnp.concatenate([chip_table, table_y, z_table, core(z_table)], axis=0)
    blocks = [pooled, pooled_c, pooled_y, pooled_yc, rim_z, rim_zy, rim_zc, rim_zyc]
    dec_in, near_face, far_face = coarse(
        tables, parent, info, send, blocks, enc, flat[1], flat[2], coarse_slots
    )
    far = next_chip(far_face)
    near = core(near_face)
    main, part = inner(dec_in, fine_nbr, flat[3])
    out = outer(main, part, near, far, fine_nbr, info, flat[3])
    return out.reshape(features.shape)


def solution(mesh):
    placed = (
        P(("groups", "gx"), None, None, None, None),
        P(("groups", "gx"), None),
        P(("groups", "gx"), None, None),
        P(("groups", "gx")),
        P(("groups", "gx"), None),
        P(("groups", "gx"), None),
        P(),
        P(),
        P(),
        P(),
    )
    return jax.shard_map(
        per_device,
        mesh=mesh,
        in_specs=placed,
        out_specs=P(("groups", "gx"), None, None, None, None),
        check_vma=False,
    )
```

profile of v0, /device:TPU:5, one launch (start us, length us, event | category | flops | bytes accessed | tf_op | source)
XLA Modules:
  0.0 62.1 jit_solution(8585406641411841572)
XLA Ops:
  0.0 0.7 %copy-done.12 = s32[1,2,4]{2,1,0:T(2,128)S(1)} copy-done((s32[1,2,4]{2,1,0:T(2,128)S(1)}, s32[1,2,4]{2,1,0:T(2,128)}, u32[]{:S(2)}) %copy-start.12) | copy-done | bytes 56
  0.7 1.1 %copy.15 = bf16[4,8,8,8,128]{4,3,2,0,1:T(8,128)(2,1)S(1)} copy(bf16[4,8,8,8,128]{4,3,2,1,0:T(8,128)(2,1)} %param.10) | data formatting | bytes 1048576 | tf_op args[0]
  1.8 0.1 broadcast_select_fusion
  1.9 3.7 %collective-permute-start.6 = (bf16[4,64,128]{2,1,0:T(8,128)(2,1)S(1)}, bf16[4,64,128]{2,1,0:T(8,128)(2,1)S(1)}, u32[]{:S(2)}, u32[]{:S(2)}) collective-permute-start(bf16[4,64,128]{2,1,0:T(8,128)(2,1)S(1)} %get-tuple-element.25), channel_id=1, source_target_pairs={{1,2},{2,1},{3,4},{4,3},{5,6},{6,5},{7,8},{8,7},{9,10},{10,9},{11,... | collective-permute-start | bytes 196616 | tf_op jit(solution)/shard_map/ppermute | solution.py:421
  5.6 0.1 collective-permute-start.5
  5.7 6.2 %inner.2 = (bf16[4,8,64,128]{3,2,1,0:T(8,128)(2,1)}, f32[4,2,64,128]{3,2,1,0:T(8,128)}) custom-call(s32[4,27]{1,0:T(4,128)} %nbr.7, bf16[4,8,64,128]{3,2,1,0:T(8,128)(2,1)} %bitcast.43, bf16[3456,128]{1,0:T(8,128)(2,1)} %bitcast.40), custom_call_target="tpu_custom_call" | custom-call | flops 1811939328 | bytes 4194304 | tf_op jit(solution)/shard_map/inner/pallas_call | solution.py:88
  11.9 0.6 add_bitcast_fusion.info.refs_2_
  12.5 0.0 collective-permute-done.6.far_ref
  12.5 0.0 collective-permute-done.5.near_ref
  12.5 0.6 copy-done.8
  13.1 0.0 copy-done.9
  13.2 2.8 %outer_pool.1 = (bf16[4,8,64,128]{3,2,1,0:T(8,128)(2,1)}, bf16[256,128]{1,0:T(8,128)(2,1)}, bf16[128,128]{1,0:T(8,128)(2,1)}) custom-call(s32[4,27]{1,0:T(4,128)} %nbr.7, s32[1,2]{1,0:T(1,128)} %add_bitcast_fusion.info.refs_2_, s32[1,4]{1,0:T(1,128)} %bitcast.44, bf16[4,64,128]{2,1,0:T(8,128)(2,1)} %copy-done.9, bf16[4,64,128]{2,1,0:T(8,128)(2,1)} %copy-done.8, ...), custom_call_target="tpu_custom_call" | custom-call | tf_op jit(solution)/shard_map/outer_pool/pallas_call | solution.py:190
  16.0 0.6 collective-permute-start.10
  16.6 1.1 %collective-permute-done.10 = bf16[128,128]{1,0:T(8,128)(2,1)S(1)} collective-permute-done((bf16[128,128]{1,0:T(8,128)(2,1)}, bf16[128,128]{1,0:T(8,128)(2,1)S(1)}, u32[]{:S(2)}, u32[]{:S(2)}) %collective-permute-start.10) | collective-permute-done | bytes 32800 | tf_op jit(solution)/shard_map/ppermute | solution.py:421
  17.6 0.8 %pad_maximum_fusion = bf16[256,128]{1,0:T(8,128)(2,1)S(1)} fusion(bf16[128,128]{1,0:T(8,128)(2,1)S(1)} %collective-permute-done.10, bf16[128,128]{1,0:T(8,128)(2,1)} %get-tuple-element.18), kind=kLoop, calls=%fused_computation.5 | loop fusion | flops 131072 | bytes 131072 | tf_op jit(solution)/shard_map/concatenate | solution.py:453
  18.4 3.4 %collective-permute-start.11 = (bf16[256,128]{1,0:T(8,128)(2,1)S(1)}, bf16[256,128]{1,0:T(8,128)(2,1)S(1)}, u32[]{:S(2)}, u32[]{:S(2)}) collective-permute-start(bf16[256,128]{1,0:T(8,128)(2,1)S(1)} %pad_maximum_fusion), channel_id=1, source_target_pairs={{1,4},{3,6},{4,1},{5,8},{6,3},{7,10},{8,5},{9,12},{10,7},{11,14},{... | collective-permute-start | bytes 196616 | tf_op jit(solution)/shard_map/ppermute | solution.py:421
  21.8 0.1 pad_add_fusion.2
  21.9 0.0 collective-permute-start
  21.9 0.3 collective-permute-start.8
  22.2 1.7 %collective-permute-done.11.refs_8_ = bf16[256,128]{1,0:T(8,128)(2,1)S(1)} collective-permute-done((bf16[256,128]{1,0:T(8,128)(2,1)S(1)}, bf16[256,128]{1,0:T(8,128)(2,1)S(1)}, u32[]{:S(2)}, u32[]{:S(2)}) %collective-permute-start.11) | collective-permute-done | bytes 65568 | tf_op jit(solution)/shard_map/ppermute | solution.py:421
  24.0 0.2 collective-permute-start.12
  24.2 0.0 collective-permute-done
  24.2 0.1 pad_add_fusion.1
  24.3 3.7 %collective-permute-start.2 = (s32[2,35]{1,0:T(2,128)S(1)}, s32[2,35]{1,0:T(2,128)S(1)}, u32[]{:S(2)}, u32[]{:S(2)}) collective-permute-start(s32[2,35]{1,0:T(2,128)S(1)} %pad_add_fusion.1), channel_id=1, source_target_pairs={{1,4},{3,6},{4,1},{5,8},{6,3},{7,10},{8,5},{9,12},{10,7},{11,14},{... | collective-permute-start | bytes 848 | tf_op jit(solution)/shard_map/ppermute | solution.py:421
  28.0 1.2 %collective-permute-done.2 = s32[2,35]{1,0:T(2,128)S(1)} collective-permute-done((s32[2,35]{1,0:T(2,128)S(1)}, s32[2,35]{1,0:T(2,128)S(1)}, u32[]{:S(2)}, u32[]{:S(2)}) %collective-permute-start.2) | collective-permute-done | bytes 312 | tf_op jit(solution)/shard_map/ppermute | solution.py:421
  29.2 1.2 %collective-permute-start.3 = (s32[2,35]{1,0:T(2,128)S(1)}, s32[2,35]{1,0:T(2,128)S(1)}, u32[]{:S(2)}, u32[]{:S(2)}) collective-permute-start(s32[2,35]{1,0:T(2,128)S(1)} %collective-permute-done.2), channel_id=1, source_target_pairs={{0,2},{1,3},{2,0},{3,1},{4,6},{5,7},{6,4},{7,5},{8,10},{9,11},{10,... | collective-permute-start | bytes 848 | tf_op jit(solution)/shard_map/ppermute | solution.py:421
  30.5 0.2 collective-permute-start.1
  30.7 0.0 collective-permute-start.7
  30.7 0.0 collective-permute-done.8.refs_6_
  30.7 0.5 collective-permute-start.9
  31.2 0.4 collective-permute-done.3
  31.7 0.5 collective-permute-start.14
  32.2 0.7 %collective-permute-done.1 = s32[2,35]{1,0:T(2,128)S(1)} collective-permute-done((s32[2,35]{1,0:T(2,128)S(1)}, s32[2,35]{1,0:T(2,128)S(1)}, u32[]{:S(2)}, u32[]{:S(2)}) %collective-permute-start.1) | collective-permute-done | bytes 312 | tf_op jit(solution)/shard_map/ppermute | solution.py:421
  32.9 1.2 %collective-permute-done.4 = s32[4,35]{1,0:T(4,128)S(1)} collective-permute-done((s32[4,35]{1,0:T(4,128)S(1)}, s32[4,35]{1,0:T(4,128)S(1)}, u32[]{:S(2)}, u32[]{:S(2)}) %collective-permute-start.4) | collective-permute-done | bytes 592 | tf_op jit(solution)/shard_map/ppermute | solution.py:421
  34.1 1.2 %concatenate.19.refs_0_ = s32[12,35]{1,0:T(8,128)} concatenate(s32[1,35]{1,0:T(1,128)S(1)} %pad_add_fusion.2, s32[1,35]{1,0:T(1,128)S(1)} %collective-permute-done, s32[2,35]{1,0:T(2,128)S(1)} %collective-permute-done.1, s32[2,35]{1,0:T(2,128)S(1)} %collective-permute-done.2, s32[2,35]{1,0:T(2,128)S(1)} %collective-permute-done.3, s32[4,35]{1,0:T(4,128)S(1)} %collective-permute-done.4), dimensions={0} | concatenate | bytes 3360 | tf_op jit(solution)/shard_map/concatenate | solution.py:463
  35.3 0.0 collective-permute-done.9.refs_7_
  35.4 0.5 copy-done.4
  35.9 0.0 copy-done.5
  35.9 0.0 copy-done.6
  36.0 0.0 copy-done.7
  36.0 11.0 %coarse.1 = (bf16[4,8,64,128]{3,2,1,0:T(8,128)(2,1)}, bf16[4,64,128]{2,1,0:T(8,128)(2,1)}, bf16[4,64,128]{2,1,0:T(8,128)(2,1)}) custom-call(s32[12,35]{1,0:T(8,128)} %concatenate.19.refs_0_, s32[1,4]{1,0:T(1,128)} %bitcast.45, s32[1,2]{1,0:T(1,128)} %add_bitcast_fusion.info.refs_2_, s32[2,4]{1,0:T(2,128)} %bitcast.46, ...), custom_call_target="tpu_custom_call" | custom-call | tf_op jit(solution)/shard_map/coarse/pallas_call | solution.py:377
  47.0 0.2 collective-permute-start.15
  47.2 5.3 %collective-permute-start.16 = (bf16[4,64,128]{2,1,0:T(8,128)(2,1)}, bf16[4,64,128]{2,1,0:T(8,128)(2,1)S(1)}, u32[]{:S(2)}, u32[]{:S(2)}) collective-permute-start(bf16[4,64,128]{2,1,0:T(8,128)(2,1)} %get-tuple-element.21), channel_id=1, source_target_pairs={{1,2},{2,1},{3,4},{4,3},{5,6},{6,5},{7,8},{8,7},{9,10},{10,9},{11,... | collective-permute-start | bytes 196616 | tf_op jit(solution)/shard_map/ppermute | solution.py:421
  52.5 6.2 %inner.3 = (bf16[4,8,64,128]{3,2,1,0:T(8,128)(2,1)}, f32[4,2,64,128]{3,2,1,0:T(8,128)}) custom-call(s32[4,27]{1,0:T(4,128)} %nbr.7, bf16[4,8,64,128]{3,2,1,0:T(8,128)(2,1)} %get-tuple-element.22.x_ref, bf16[3456,128]{1,0:T(8,128)(2,1)} %bitcast.38), custom_call_target="tpu_custom_call" | custom-call | flops 1811939328 | bytes 4194304 | tf_op jit(solution)/shard_map/inner/pallas_call | solution.py:88
  58.7 0.0 collective-permute-done.15.near_ref
  58.8 0.6 copy-done.10
  59.4 0.0 copy-done.11
  59.4 2.7 %outer.1 = bf16[4,8,64,128]{3,2,1,0:T(8,128)(2,1)} custom-call(s32[4,27]{1,0:T(4,128)} %nbr.7, s32[1,2]{1,0:T(1,128)} %add_bitcast_fusion.info.refs_2_, bf16[4,64,128]{2,1,0:T(8,128)(2,1)} %copy-done.10, bf16[4,64,128]{2,1,0:T(8,128)(2,1)} %copy-done.11, f32[4,2,64,128]{3,2,1,0:T(8,128)} %get-tuple-element.23.part_ref, bf16[3456,128]{1,0:T(8,128)(2,1)} %bitcast.39, ...), custom_call_target="tpu_custom_call" | custom-call | tf_op jit(solution)/shard_map/outer/pallas_call | solution.py:156
  (31 shorter events, 0.1 us)
Async XLA Ops:
  0.0 0.7 %copy-start.12 = (s32[1,2,4]{2,1,0:T(2,128)S(1)}, s32[1,2,4]{2,1,0:T(2,128)}, u32[]{:S(2)}) copy-start(s32[1,2,4]{2,1,0:T(2,128)} %param.12) | copy-start | bytes 100
  1.9 10.6 %collective-permute-start.6 = (bf16[4,64,128]{2,1,0:T(8,128)(2,1)S(1)}, bf16[4,64,128]{2,1,0:T(8,128)(2,1)S(1)}, u32[]{:S(2)}, u32[]{:S(2)}) collective-permute-start(bf16[4,64,128]{2,1,0:T(8,128)(2,1)S(1)} %get-tuple-element.25), channel_id=1, source_target_pairs={{1,2},{2,1},{3,4},{4,3},{5,6},{6,5},{7,8},{8,7},{9,10},{10,9},{11,... | collective-permute-start | bytes 196616 | tf_op jit(solution)/shard_map/ppermute | solution.py:421
  5.6 6.9 %collective-permute-start.5 = (bf16[4,64,128]{2,1,0:T(8,128)(2,1)S(1)}, bf16[4,64,128]{2,1,0:T(8,128)(2,1)S(1)}, u32[]{:S(2)}, u32[]{:S(2)}) collective-permute-start(bf16[4,64,128]{2,1,0:T(8,128)(2,1)S(1)} %get-tuple-element.26), channel_id=1, source_target_pairs={{0,1},{1,0},{2,3},{3,2},{4,5},{5,4},{6,7},{7,6},{8,9},{9,8},{10,11... | collective-permute-start | bytes 196616 | tf_op jit(solution)/shard_map/ppermute | solution.py:421
  12.5 0.6 copy-start.8
  12.5 0.6 %copy-start.9 = (bf16[4,64,128]{2,1,0:T(8,128)(2,1)}, bf16[4,64,128]{2,1,0:T(8,128)(2,1)S(1)}, u32[]{:S(2)}) copy-start(bf16[4,64,128]{2,1,0:T(8,128)(2,1)S(1)} %collective-permute-done.5.near_ref) | copy-start | bytes 196612
  16.0 5.8 %copy-start.13 = (s32[1,27]{1,0:T(1,128)S(1)}, s32[1,27]{1,0:T(1,128)}, u32[]{:S(2)}) copy-start(s32[1,27]{1,0:T(1,128)} %param.15) | copy-start | bytes 328
  16.0 5.8 %copy-start.14 = (s32[1,8]{1,0:T(1,128)S(1)}, s32[1,8]{1,0:T(1,128)}, u32[]{:S(2)}) copy-start(s32[1,8]{1,0:T(1,128)} %param.14) | copy-start | bytes 100
  16.0 5.9 %copy-start = (bf16[256,128]{1,0:T(8,128)(2,1)S(1)}, bf16[256,128]{1,0:T(8,128)(2,1)}, u32[]{:S(2)}) copy-start(bf16[256,128]{1,0:T(8,128)(2,1)} %get-tuple-element.17.refs_4_) | copy-start | bytes 196612
  16.0 1.6 %collective-permute-start.10 = (bf16[128,128]{1,0:T(8,128)(2,1)}, bf16[128,128]{1,0:T(8,128)(2,1)S(1)}, u32[]{:S(2)}, u32[]{:S(2)}) collective-permute-start(bf16[128,128]{1,0:T(8,128)(2,1)} %get-tuple-element.18), channel_id=1, source_target_pairs={{0,1},{1,0},{2,3},{3,2},{4,5},{5,4},{6,7},{7,6},{8,9},{9,8},{10,11... | collective-permute-start | bytes 98312 | tf_op jit(solution)/shard_map/ppermute | solution.py:421
  18.4 5.6 %collective-permute-start.11 = (bf16[256,128]{1,0:T(8,128)(2,1)S(1)}, bf16[256,128]{1,0:T(8,128)(2,1)S(1)}, u32[]{:S(2)}, u32[]{:S(2)}) collective-permute-start(bf16[256,128]{1,0:T(8,128)(2,1)S(1)} %pad_maximum_fusion), channel_id=1, source_target_pairs={{1,4},{3,6},{4,1},{5,8},{6,3},{7,10},{8,5},{9,12},{10,7},{11,14},{... | collective-permute-start | bytes 196616 | tf_op jit(solution)/shard_map/ppermute | solution.py:421
  21.9 2.3 %collective-permute-start = (s32[1,35]{1,0:T(1,128)S(1)}, s32[1,35]{1,0:T(1,128)S(1)}, u32[]{:S(2)}, u32[]{:S(2)}) collective-permute-start(s32[1,35]{1,0:T(1,128)S(1)} %pad_add_fusion.2), channel_id=1, source_target_pairs={{0,1},{1,0},{2,3},{3,2},{4,5},{5,4},{6,7},{7,6},{8,9},{9,8},{10,11... | collective-permute-start | bytes 428 | tf_op jit(solution)/shard_map/ppermute | solution.py:421
  21.9 8.8 %collective-permute-start.8 = (bf16[256,128]{1,0:T(8,128)(2,1)S(1)}, bf16[256,128]{1,0:T(8,128)(2,1)S(1)}, u32[]{:S(2)}, u32[]{:S(2)}) collective-permute-start(bf16[256,128]{1,0:T(8,128)(2,1)S(1)} %copy-done), channel_id=1, source_target_pairs={{0,2},{1,3},{2,0},{3,1},{4,6},{5,7},{6,4},{7,5},{8,10},{9,11},{10,... | collective-permute-start | bytes 196616 | tf_op jit(solution)/shard_map/ppermute | solution.py:421
  24.0 11.4 %copy-start.1 = (bf16[256,128]{1,0:T(8,128)(2,1)}, bf16[256,128]{1,0:T(8,128)(2,1)S(1)}, u32[]{:S(2)}) copy-start(bf16[256,128]{1,0:T(8,128)(2,1)S(1)} %collective-permute-done.11.refs_8_) | copy-start | bytes 196612
  24.0 7.7 %collective-permute-start.12 = (bf16[256,128]{1,0:T(8,128)(2,1)S(1)}, bf16[256,128]{1,0:T(8,128)(2,1)S(1)}, u32[]{:S(2)}, u32[]{:S(2)}) collective-permute-start(bf16[256,128]{1,0:T(8,128)(2,1)S(1)} %collective-permute-done.11.refs_8_), channel_id=1, source_target_pairs={{0,2},{1,3},{2,0},{3,1},{4,6},{5,7},{6,4},{7,5},{8,10},{9,11},{10,... | collective-permute-start | bytes 196616 | tf_op jit(solution)/shard_map/ppermute | solution.py:421
  24.3 5.0 %collective-permute-start.2 = (s32[2,35]{1,0:T(2,128)S(1)}, s32[2,35]{1,0:T(2,128)S(1)}, u32[]{:S(2)}, u32[]{:S(2)}) collective-permute-start(s32[2,35]{1,0:T(2,128)S(1)} %pad_add_fusion.1), channel_id=1, source_target_pairs={{1,4},{3,6},{4,1},{5,8},{6,3},{7,10},{8,5},{9,12},{10,7},{11,14},{... | collective-permute-start | bytes 848 | tf_op jit(solution)/shard_map/ppermute | solution.py:421
  29.2 2.4 %collective-permute-start.3 = (s32[2,35]{1,0:T(2,128)S(1)}, s32[2,35]{1,0:T(2,128)S(1)}, u32[]{:S(2)}, u32[]{:S(2)}) collective-permute-start(s32[2,35]{1,0:T(2,128)S(1)} %collective-permute-done.2), channel_id=1, source_target_pairs={{0,2},{1,3},{2,0},{3,1},{4,6},{5,7},{6,4},{7,5},{8,10},{9,11},{10,... | collective-permute-start | bytes 848 | tf_op jit(solution)/shard_map/ppermute | solution.py:421
  30.5 2.4 %collective-permute-start.1 = (s32[2,35]{1,0:T(2,128)S(1)}, s32[2,35]{1,0:T(2,128)S(1)}, u32[]{:S(2)}, u32[]{:S(2)}) collective-permute-start(s32[2,35]{1,0:T(2,128)S(1)} %pad_add_fusion.1), channel_id=1, source_target_pairs={{0,2},{1,3},{2,0},{3,1},{4,6},{5,7},{6,4},{7,5},{8,10},{9,11},{10,... | collective-permute-start | bytes 848 | tf_op jit(solution)/shard_map/ppermute | solution.py:421
  30.7 4.6 %collective-permute-start.7 = (bf16[256,128]{1,0:T(8,128)(2,1)S(1)}, bf16[256,128]{1,0:T(8,128)(2,1)S(1)}, u32[]{:S(2)}, u32[]{:S(2)}) collective-permute-start(bf16[256,128]{1,0:T(8,128)(2,1)S(1)} %copy-done), channel_id=1, source_target_pairs={{0,1},{1,0},{2,3},{3,2},{4,5},{5,4},{6,7},{7,6},{8,9},{9,8},{10,11... | collective-permute-start | bytes 196616 | tf_op jit(solution)/shard_map/ppermute | solution.py:421
  30.7 4.6 %copy-start.2 = (bf16[256,128]{1,0:T(8,128)(2,1)}, bf16[256,128]{1,0:T(8,128)(2,1)S(1)}, u32[]{:S(2)}) copy-start(bf16[256,128]{1,0:T(8,128)(2,1)S(1)} %collective-permute-done.8.refs_6_) | copy-start | bytes 196612
  30.7 4.6 %collective-permute-start.9 = (bf16[256,128]{1,0:T(8,128)(2,1)S(1)}, bf16[256,128]{1,0:T(8,128)(2,1)S(1)}, u32[]{:S(2)}, u32[]{:S(2)}) collective-permute-start(bf16[256,128]{1,0:T(8,128)(2,1)S(1)} %collective-permute-done.8.refs_6_), channel_id=1, source_target_pairs={{0,1},{1,0},{2,3},{3,2},{4,5},{5,4},{6,7},{7,6},{8,9},{9,8},{10,11... | collective-permute-start | bytes 196616 | tf_op jit(solution)/shard_map/ppermute | solution.py:421
  31.7 3.6 %collective-permute-start.13 = (bf16[256,128]{1,0:T(8,128)(2,1)S(1)}, bf16[256,128]{1,0:T(8,128)(2,1)S(1)}, u32[]{:S(2)}, u32[]{:S(2)}) collective-permute-start(bf16[256,128]{1,0:T(8,128)(2,1)S(1)} %collective-permute-done.11.refs_8_), channel_id=1, source_target_pairs={{0,1},{1,0},{2,3},{3,2},{4,5},{5,4},{6,7},{7,6},{8,9},{9,8},{10,11... | collective-permute-start | bytes 196616 | tf_op jit(solution)/shard_map/ppermute | solution.py:421
  31.7 3.7 %copy-start.3 = (bf16[256,128]{1,0:T(8,128)(2,1)}, bf16[256,128]{1,0:T(8,128)(2,1)S(1)}, u32[]{:S(2)}) copy-start(bf16[256,128]{1,0:T(8,128)(2,1)S(1)} %collective-permute-done.12.refs_9_) | copy-start | bytes 196612
  31.7 3.7 %collective-permute-start.14 = (bf16[256,128]{1,0:T(8,128)(2,1)S(1)}, bf16[256,128]{1,0:T(8,128)(2,1)S(1)}, u32[]{:S(2)}, u32[]{:S(2)}) collective-permute-start(bf16[256,128]{1,0:T(8,128)(2,1)S(1)} %collective-permute-done.12.refs_9_), channel_id=1, source_target_pairs={{0,1},{1,0},{2,3},{3,2},{4,5},{5,4},{6,7},{7,6},{8,9},{9,8},{10,11... | collective-permute-start | bytes 196616 | tf_op jit(solution)/shard_map/ppermute | solution.py:421
  32.9 1.2 %collective-permute-start.4 = (s32[4,35]{1,0:T(4,128)S(1)}, s32[4,35]{1,0:T(4,128)S(1)}, u32[]{:S(2)}, u32[]{:S(2)}) collective-permute-start(s32[4,35]{1,0:T(4,128)S(1)} %pad_add_fusion), channel_id=1, source_target_pairs={{0,1},{1,0},{2,3},{3,2},{4,5},{5,4},{6,7},{7,6},{8,9},{9,8},{10,11... | collective-permute-start | bytes 1688 | tf_op jit(solution)/shard_map/ppermute | solution.py:421
  35.3 0.6 %copy-start.4 = (bf16[256,128]{1,0:T(8,128)(2,1)}, bf16[256,128]{1,0:T(8,128)(2,1)S(1)}, u32[]{:S(2)}) copy-start(bf16[256,128]{1,0:T(8,128)(2,1)S(1)} %collective-permute-done.7.refs_5_) | copy-start | bytes 196612
  35.3 0.6 %copy-start.5 = (bf16[256,128]{1,0:T(8,128)(2,1)}, bf16[256,128]{1,0:T(8,128)(2,1)S(1)}, u32[]{:S(2)}) copy-start(bf16[256,128]{1,0:T(8,128)(2,1)S(1)} %collective-permute-done.9.refs_7_) | copy-start | bytes 196612
  35.3 0.6 %copy-start.6 = (bf16[256,128]{1,0:T(8,128)(2,1)}, bf16[256,128]{1,0:T(8,128)(2,1)S(1)}, u32[]{:S(2)}) copy-start(bf16[256,128]{1,0:T(8,128)(2,1)S(1)} %collective-permute-done.13.refs_10_) | copy-start | bytes 196612
  35.3 0.6 %copy-start.7 = (bf16[256,128]{1,0:T(8,128)(2,1)}, bf16[256,128]{1,0:T(8,128)(2,1)S(1)}, u32[]{:S(2)}) copy-start(bf16[256,128]{1,0:T(8,128)(2,1)S(1)} %collective-permute-done.14.refs_11_) | copy-start | bytes 196612
  47.0 11.7 %collective-permute-start.15 = (bf16[4,64,128]{2,1,0:T(8,128)(2,1)}, bf16[4,64,128]{2,1,0:T(8,128)(2,1)S(1)}, u32[]{:S(2)}, u32[]{:S(2)}) collective-permute-start(bf16[4,64,128]{2,1,0:T(8,128)(2,1)} %get-tuple-element.20), channel_id=1, source_target_pairs={{0,1},{1,0},{2,3},{3,2},{4,5},{5,4},{6,7},{7,6},{8,9},{9,8},{10,11... | collective-permute-start | bytes 196616 | tf_op jit(solution)/shard_map/ppermute | solution.py:421
  47.2 11.5 %collective-permute-start.16 = (bf16[4,64,128]{2,1,0:T(8,128)(2,1)}, bf16[4,64,128]{2,1,0:T(8,128)(2,1)S(1)}, u32[]{:S(2)}, u32[]{:S(2)}) collective-permute-start(bf16[4,64,128]{2,1,0:T(8,128)(2,1)} %get-tuple-element.21), channel_id=1, source_target_pairs={{1,2},{2,1},{3,4},{4,3},{5,6},{6,5},{7,8},{8,7},{9,10},{10,9},{11,... | collective-permute-start | bytes 196616 | tf_op jit(solution)/shard_map/ppermute | solution.py:421
  58.7 0.6 copy-start.10
  58.8 0.6 %copy-start.11 = (bf16[4,64,128]{2,1,0:T(8,128)(2,1)}, bf16[4,64,128]{2,1,0:T(8,128)(2,1)S(1)}, u32[]{:S(2)}) copy-start(bf16[4,64,128]{2,1,0:T(8,128)(2,1)S(1)} %collective-permute-done.16.far_ref) | copy-start | bytes 196612
where the time goes:
time: 62.6 us; the launch traced here: 62.1 us
  Pallas kernels  29.1 us (46%)
  starting transfers between devices  20 us (32%)
  waiting for transfers between devices  6.38 us (10%)
  local copies, waits for them, and re-layouts  4.89 us (8%)
  other arithmetic  1.6 us (3%)
    ppermute x17, starting transfers between devices, swap(): return lax.ppermute(value, 'gx', pairs)  20 us
    pallas_call x2, Pallas kernels, inner(): pl.pallas_call(inner_kernel, out_shape=(jax.ShapeDtypeStruct(x.shape, BF1...  12.5 us
    pallas_call x1, Pallas kernels, coarse(): pl.pallas_call(functools.partial(coarse_kernel, coarse_slots), out_shape=...  11 us
    ppermute x17, waiting for transfers between devices, swap(): return lax.ppermute(value, 'gx', pairs)  6.38 us
    unnamed x31, local copies, waits for them, and re-layouts  3.66 us
    pallas_call x1, Pallas kernels, outer_pool(): pl.pallas_call(outer_pool_kernel, out_shape=(jax.ShapeDtypeStruct(main.sh...  2.83 us
    pallas_call x1, Pallas kernels, outer(): pl.pallas_call(outer_kernel, out_shape=jax.ShapeDtypeStruct(main.shape, B...  2.74 us
  transfers between devices with their start and end apart: 17, of which 6 were waited for; matrix products, arithmetic and copies ran while one was open for 3% of the time, Pallas kernels for 20%

commit v1 on v0

v1 whole, which is shorter than its diff:
```python
import functools

import jax
import jax.numpy as jnp
from jax import lax
from jax.experimental import pallas as pl
from jax.experimental.pallas import tpu as pltpu
from jax.sharding import PartitionSpec as P

LANES = 4
GROUP = 1
CONV_GROUP = 4
TILE = 16
OFFSETS = (-1, 0, 1)
BF16 = jnp.bfloat16
F32 = jnp.float32
VMEM = pl.BlockSpec(memory_space=pltpu.VMEM)
SMEM = pl.BlockSpec(memory_space=pltpu.SMEM)
PARAMS = pltpu.CompilerParams(vmem_limit_bytes=16 << 20)


def tap(dx, dy, dz):
    return 9 * (dx + 1) + 3 * (dy + 1) + dz + 1


def z_shifts(center, below, above):
    edge = center.shape[1]
    z = lax.broadcasted_iota(jnp.int32, center.shape, 1)
    down = jnp.where(z == 0, pltpu.roll(below, 1, 1), pltpu.roll(center, 1, 1))
    up = jnp.where(z == edge - 1, pltpu.roll(above, edge - 1, 1), pltpu.roll(center, edge - 1, 1))
    return down, center, up


def columns(fetch, edge):
    parts = []
    for dy in OFFSETS:
        triple = [fetch(dy, dz) for dz in (0, -1, 1)]
        planes, rows, _, width = triple[0].shape
        flat = [v.reshape(planes * rows, edge, width) for v in triple]
        parts.append([s.reshape(planes, rows, edge, width) for s in z_shifts(*flat)])
    return [jnp.concatenate([part[k] for part in parts], axis=1) for k in range(3)]


def y_rows(load, dy, edge):
    if dy == 0:
        value = load(0, edge * edge)
    elif dy < 0:
        value = load(edge * edge - 2 * edge, 2 * edge)[:, edge:]
    else:
        value = load(0, 2 * edge)[:, :edge]
    planes, rows, width = value.shape
    return value.reshape(planes, rows // edge, edge, width)


def pair_weights(w_ref, dxs, width):
    zero = jnp.zeros((3 * width, width), BF16)
    blocks = []
    for dx in dxs:
        for j in range(4):
            sides = []
            for p in range(2):
                dy = j - p
                first = (9 * dx + 3 * dy) * width
                sides.append(w_ref[first : first + 3 * width] if 0 <= dy < 3 else zero)
            blocks.append(jnp.concatenate(sides, axis=1))
    return jnp.concatenate(blocks, axis=0)


def pair_rows(full, j, pairs):
    planes, _, edge, width = full.shape
    picked = jnp.concatenate([full[:, j + 2 * i : j + 2 * i + 1] for i in range(pairs)], axis=1)
    return picked.reshape(planes, pairs * edge, width).astype(BF16)


def unpair(total, planes, pairs, edge, width):
    sides = [
        total[:, p * width : (p + 1) * width].reshape(planes, pairs, 1, edge, width) for p in range(2)
    ]
    return jnp.concatenate(sides, axis=2).reshape(planes, 2 * pairs * edge, width)


def inner_kernel(nbr, x_ref, w_ref, out_ref, part_ref, cols):
    slots, edge, rows, width = x_ref.shape
    pairs = edge // 2
    empty = jnp.zeros((slots, 4, 3, pairs * edge, width), BF16)
    cols[:, :, :, 0] = empty
    cols[:, :, :, edge + 1] = empty
    weights = pair_weights(w_ref, range(3), width)
    for group in range(0, slots, GROUP):
        bricks = []
        for b in range(group, group + GROUP):

            def fetch(dy, dz):
                slot = nbr[b, tap(0, dy, dz)]
                held = jnp.maximum(slot, 0)
                value = y_rows(lambda r, n: x_ref[held, :, r : r + n, :].astype(F32), dy, edge)
                return jnp.where(slot >= 0, value, 0.0)

            for k, full in enumerate(columns(fetch, edge)):
                for j in range(4):
                    cols[b, j, k, 1 : edge + 1] = pair_rows(full, j, pairs)
            taps = []
            for dx in range(3):
                for j in range(4):
                    for k in range(3):
                        taps.append(
                            cols[b, j, k, dx : dx + edge].reshape(edge * pairs * edge, width)
                        )
            bricks.append(jnp.concatenate(taps, axis=1))
        totals = jnp.dot(
            jnp.concatenate(bricks, axis=0), weights, preferred_element_type=F32
        )
        count = edge * pairs * edge
        for i in range(GROUP):
            b = group + i
            total = unpair(totals[i * count : (i + 1) * count], edge, pairs, edge, width)
            out_ref[b] = jnp.maximum(total, 0.0).astype(BF16)
            part_ref[b, 0] = total[0]
            part_ref[b, 1] = total[edge - 1]


def inner(x, nbr, weights):
    slots, edge, rows, width = x.shape
    return pl.pallas_call(
        inner_kernel,
        out_shape=(
            jax.ShapeDtypeStruct(x.shape, BF16),
            jax.ShapeDtypeStruct((slots, 2, rows, width), F32),
        ),
        in_specs=[SMEM, VMEM, VMEM],
        out_specs=(VMEM, VMEM),
        scratch_shapes=[
            pltpu.VMEM((slots, 4, 3, edge + 2, rows // 2, width), BF16),
        ],
        compiler_params=PARAMS,
        cost_estimate=pl.CostEstimate(
            flops=2 * slots * edge * rows * 27 * width * width,
            bytes_accessed=4 << 20,
            transcendentals=0,
        ),
        name="inner",
    )(nbr, x, weights)


def outer_planes(nbr, info, near_ref, far_ref, part_ref, w_ref, out_ref):
    slots, _, rows, width = part_ref.shape
    edge = out_ref.shape[1]
    pairs = edge // 2
    is_odd = info[0, 0] == 1
    for side, dx in enumerate((-1, 1)):
        use_near = is_odd if side == 0 else jnp.logical_not(is_odd)
        bricks = []
        for b in range(slots):

            def fetch(dy, dz):
                slot = nbr[b, tap(dx, dy, dz)]
                held = jnp.maximum(slot, 0)

                def load(r, n):
                    near = near_ref[held, r : r + n, :].astype(F32)
                    far = far_ref[held, r : r + n, :].astype(F32)
                    return jnp.where(use_near, near, far)[None]

                return jnp.where(slot >= 0, y_rows(load, dy, edge), 0.0)

            shifted = columns(fetch, edge)
            taps = []
            for j in range(4):
                for k in range(3):
                    taps.append(pair_rows(shifted[k], j, pairs).reshape(rows // 2, width))
            bricks.append(jnp.concatenate(taps, axis=1))
        extra = jnp.dot(
            jnp.concatenate(bricks, axis=0),
            pair_weights(w_ref, [dx + 1], width),
            preferred_element_type=F32,
        )
        extra = unpair(extra, slots, pairs, edge, width)
        plane = 0 if side == 0 else out_ref.shape[1] - 1
        for b in range(slots):
            total = part_ref[b, side] + extra[b]
            out_ref[b, plane] = jnp.maximum(total, 0.0).astype(BF16)


def outer_kernel(nbr, info, near_ref, far_ref, part_ref, w_ref, main_ref, out_ref):
    out_ref[:, 1 : out_ref.shape[1] - 1] = main_ref[:, 1 : out_ref.shape[1] - 1]
    outer_planes(nbr, info, near_ref, far_ref, part_ref, w_ref, out_ref)


def outer(main, part, near, far, nbr, info, weights):
    return pl.pallas_call(
        outer_kernel,
        out_shape=jax.ShapeDtypeStruct(main.shape, BF16),
        in_specs=[SMEM, SMEM, VMEM, VMEM, VMEM, VMEM, VMEM],
        out_specs=VMEM,
        compiler_params=PARAMS,
        name="outer",
    )(nbr, info, near, far, part, weights, main)


def outer_pool_kernel(
    nbr, info, parent, near_ref, far_ref, part_ref, w_ref, main_ref, code_ref, out_ref, pool_ref, rim_ref, sums
):
    slots, edge, rows, width = out_ref.shape
    half = edge // 2
    out_ref[:, 1 : edge - 1] = main_ref[:, 1 : edge - 1]
    outer_planes(nbr, info, near_ref, far_ref, part_ref, w_ref, out_ref)
    cells = half**3
    pool_ref[slots * cells :] = code_ref[...]
    rim_ref[slots * cells // 2 :] = code_ref[...]
    for b in range(slots):
        value = out_ref[b].astype(F32).reshape(half, 2, half, 2, edge, width)
        value = (value[:, 0, :, 0] + value[:, 0, :, 1]) + (value[:, 1, :, 0] + value[:, 1, :, 1])
        sums[b] = value.reshape(half * half * edge, width)
        low = sums[b, pl.ds(0, cells, stride=2), :]
        high = sums[b, pl.ds(1, cells, stride=2), :]
        pooled = (low + high) * 0.125
        pool_ref[b * cells : (b + 1) * cells, :] = pooled.astype(BF16)
        outer_x = (jnp.maximum(parent[0, b], 0) >> 2) & 1
        rim = jnp.where(outer_x == 0, pooled[: cells // 2], pooled[cells // 2 :])
        rim_ref[b * cells // 2 : (b + 1) * cells // 2, :] = rim.astype(BF16)


def outer_pool(main, part, near, far, nbr, info, parent, weights, codes):
    slots, edge, rows, width = main.shape
    cells = (edge // 2) ** 3
    return pl.pallas_call(
        outer_pool_kernel,
        out_shape=(
            jax.ShapeDtypeStruct(main.shape, BF16),
            jax.ShapeDtypeStruct((slots * cells + TILE, width), BF16),
            jax.ShapeDtypeStruct((slots * cells // 2 + TILE, width), BF16),
        ),
        in_specs=[SMEM, SMEM, SMEM, VMEM, VMEM, VMEM, VMEM, VMEM, VMEM],
        out_specs=(VMEM, VMEM, VMEM),
        scratch_shapes=[pltpu.VMEM((slots, 2 * cells, width), F32)],
        compiler_params=PARAMS,
        name="outer_pool",
    )(nbr, info, parent, near, far, part, weights, main, codes)


def source_row(rel, device, lane_y, lane_c):
    c = device & 1
    flip_y = ((device >> 1) & 1) ^ lane_y
    same = flip_y * 2 + (c ^ lane_c)
    below = 4 + 4 * lane_c + flip_y * 2 + (1 - c)
    above = 8 - 4 * lane_c + flip_y * 2 + c
    return jnp.where(rel == 0, same, jnp.where(rel < 0, below, above))


def x_pair_weights(w_ref, width):
    count = 9 * width
    zero = jnp.zeros((count, width), BF16)
    blocks = []
    for j in range(4):
        sides = [w_ref[(j - p) * count : (j - p + 1) * count] if 0 <= j - p < 3 else zero for p in range(2)]
        blocks.append(jnp.concatenate(sides, axis=1))
    return jnp.concatenate(blocks, axis=0)


def valid_conv(values, weights, cols, edge, width):
    size = values[0].shape[0]
    inside = size - 2
    pairs = inside // 2
    even, odd = cols
    bricks = []
    for b, value in enumerate(values):
        flat = value.reshape(size * size, edge, width)
        for k in range(3):
            moved = flat if k == 0 else pltpu.roll(flat, edge - k, 1)
            moved = moved.reshape(size, size, edge, width)
            even[b, k] = moved.reshape(size, size * edge, width).astype(BF16)
            odd[b, k] = moved[:, 1 : size - 1].reshape(size, inside * edge, width).astype(BF16)
        taps = []
        for j in range(4):
            for dy in range(3):
                for k in range(3):
                    if dy == 1:
                        planes = [odd[b, k, j + 2 * i] for i in range(pairs)]
                    else:
                        rows = slice(dy * edge, (dy + inside) * edge)
                        planes = [even[b, k, j + 2 * i, rows] for i in range(pairs)]
                    taps.append(jnp.concatenate(planes, axis=0))
        bricks.append(jnp.concatenate(taps, axis=1))
    rows = inside * edge
    outs = []
    for first in range(0, len(values), CONV_GROUP):
        picked = bricks[first : first + CONV_GROUP]
        total = jnp.dot(jnp.concatenate(picked, axis=0), weights, preferred_element_type=F32)
        total = jnp.maximum(total, 0.0).astype(BF16).astype(F32)
        for i in range(len(picked)):
            one = total[i * pairs * rows : (i + 1) * pairs * rows]
            sides = [one[:, p * width : (p + 1) * width].reshape(pairs, 1, rows, width) for p in range(2)]
            outs.append(jnp.concatenate(sides, axis=1).reshape(inside, inside, edge, width))
    return outs


def coarse_kernel(
    coarse_slots, parent, info, send, own_ref, core_ref, big_ref, bigc_ref, enc_ref, w1_ref, w2_ref,
    out_ref, near_ref, far_ref, held, codes, even, odd, even2, odd2, spread, table, row_s, there_s, sem,
):
    slots, edge, rows, width = enc_ref.shape
    half = edge // 2
    plane = half * half
    cells = half * plane
    position = info[0, 1]
    lane_y = (position >> 1) & 1
    lane_c = position & 1
    whole_rows = slots * cells
    rim_rows = whole_rows // 2
    rim_at = [0, rim_rows + TILE, 2 * rim_rows + whole_rows + 3 * TILE]
    rim_at.append(rim_at[2] + rim_rows + TILE)
    whole_at = 2 * (rim_rows + TILE)
    places = [(own_ref, 0, whole_rows), (core_ref, 0, whole_rows)]
    places += [(ref, whole_at, whole_rows) for ref in (big_ref, bigc_ref)]
    places += [(ref, at, rim_rows) for ref in (big_ref, bigc_ref) for at in rim_at]
    for i, (ref, at, count) in enumerate(places):
        line = ref[at + count : at + count + TILE].astype(F32)[:1]
        codes[i : i + 1] = line.astype(jnp.int32)
    copy = pltpu.make_async_copy(codes, table, sem)
    copy.start()
    first = 0
    for ref, at, count in places:
        held[first : first + count] = ref[at : at + count]
        first += count
    zero_row = first
    held[zero_row:] = jnp.zeros((cells, width), BF16)
    full_rows = LANES * whole_rows
    copy.wait()

    row_of = lax.broadcasted_iota(jnp.int32, (1, edge, width), 1)
    from_above = (row_of & 2) == 0
    center = (row_of >= 2) & (row_of < half + 2)
    regions = []
    masks = []
    for b in range(slots):
        own = parent[0, b]
        known = own >= 0
        own = jnp.maximum(own, 0)
        octant = own & 7
        brick = own >> 3
        bits = ((octant >> 2) & 1, (octant >> 1) & 1, octant & 1)
        home = source_row(0, brick // coarse_slots, lane_y, lane_c)
        home_slot = brick % coarse_slots
        sign = tuple(2 * bit - 1 for bit in bits)
        for cross in range(8):
            crossed = (cross >> 2, (cross >> 1) & 1, cross & 1)
            number = 13
            for scale, s, c in zip((9, 3, 1), sign, crossed):
                if c:
                    number = number + scale * s
            found = table[home, 8 * coarse_slots + home_slot * 27 + number] - 1
            there = known & (found >= 0)
            there_s[b, cross] = jnp.where(there, 1, 0)
            found = jnp.maximum(found, 0)
            rel = found // (LANES * coarse_slots) - 1
            lane = found // coarse_slots % LANES
            start = found % coarse_slots * 8
            row = source_row(rel, lane, lane_y, lane_c)
            row_s[b, cross] = jnp.where(there, (rel + 1) * 65536 + row * 1024 + start, -1)

        def base_of(ex, ey, ez):
            cross = 0
            flip = 0
            for scale, bit, e in zip((4, 2, 1), bits, (ex, ey, ez)):
                if e:
                    cross = cross + scale * (bit if e > 0 else 1 - bit)
                    flip += scale
            entry = row_s[b, cross]
            there = entry >= 0
            entry = jnp.maximum(entry, 0)
            rel = (entry >> 16) - 1
            child = table[(entry >> 10) & 63, (entry & 1023) + (octant ^ flip)] - 1
            valid = there & (child >= 0)
            child = jnp.maximum(child, 0)
            source = source_row(rel, child // slots, lane_y, lane_c)
            slot = child % slots
            whole = (source * slots + slot) * cells + (2 * plane if ex < 0 else 0)
            rim = full_rows + ((source - LANES) * slots + slot) * (cells // 2)
            base = jnp.where(rel == 0, whole, rim)
            return pl.multiple_of(jnp.where(valid, base, zero_row), TILE)

        x_parts = []
        for ex in OFFSETS:
            planes = half if ex == 0 else 2
            y_parts = []
            for ey in OFFSETS:
                picked = []
                for ez in OFFSETS:
                    value = held[pl.ds(base_of(ex, ey, ez), planes * plane), :].astype(F32)
                    value = value.reshape(planes, 2, edge, width)
                    if ey < 0:
                        value = value[:, 1:]
                    elif ey > 0:
                        value = value[:, :1]
                    picked.append(value.reshape(-1, edge, width))
                sides = jnp.where(from_above, picked[2], picked[0])
                first_y = jnp.where(center, pltpu.roll(picked[1], 2, 1), pltpu.roll(sides, edge - 2, 1))
                second_y = jnp.where(center, pltpu.roll(picked[1], edge - 2, 1), pltpu.roll(sides, 2, 1))
                shape = (planes, -1, 1, edge, width)
                both = jnp.concatenate([first_y.reshape(shape), second_y.reshape(shape)], axis=2)
                y_parts.append(both.reshape(planes, -1, edge, width))
            x_parts.append(jnp.concatenate(y_parts, axis=1))
        regions.append(jnp.concatenate(x_parts, axis=0))
        at_edge = jnp.where(bits[2] == 1, half + 1, 0)
        kinds = []
        for ex in OFFSETS:
            for ey in OFFSETS:
                cross = 0
                for scale, bit, e in zip((4, 2), bits, (ex, ey)):
                    if e:
                        cross = cross + scale * (bit if e > 0 else 1 - bit)
                kinds.append(jnp.where(row_of == at_edge, there_s[b, cross + 1], there_s[b, cross]) == 1)
        masks.append(kinds)

    mids = []
    for value, kinds in zip(valid_conv(regions, x_pair_weights(w1_ref, width), (even, odd), edge, width), masks):
        spans = ((0, 1), (1, half + 1), (half + 1, half + 2))
        x_parts = []
        for i, (x0, x1) in enumerate(spans):
            y_parts = []
            for n, (y0, y1) in enumerate(spans):
                y_parts.append(jnp.where(kinds[3 * i + n][None], value[x0:x1, y0:y1], 0.0))
            x_parts.append(jnp.concatenate(y_parts, axis=1))
        mids.append(jnp.concatenate(x_parts, axis=0))
    fines = valid_conv(mids, x_pair_weights(w2_ref, width), (even2, odd2), edge, width)
    is_odd = lane_c == 1
    for b in range(slots):
        value = jnp.where(parent[0, b] >= 0, fines[b], 0.0).reshape(plane * edge, width)
        spread[b, pl.ds(0, plane * edge, stride=2), :] = value
        spread[b, pl.ds(1, plane * edge, stride=2), :] = value
        up = spread[b].reshape(half, half, 2 * edge, width)[:, :, :edge]
        base = enc_ref[b].astype(F32).reshape(half, 2, half, 2, edge, width)
        total = base + up[:, None, :, None]
        total = total.reshape(edge, rows, width).astype(BF16)
        out_ref[b] = total
        last = jnp.where(send[0, b] == b, total[edge - 1], 0)
        head = jnp.where(send[1, b] == b, total[0], 0)
        near_ref[b] = jnp.where(is_odd, head, last)
        far_ref[b] = jnp.where(is_odd, last, head)


def coarse(parent, info, send, blocks, enc, w1, w2, coarse_slots):
    slots, edge, rows, width = enc.shape
    half = edge // 2
    inside = edge - 2
    total = 2 * LANES * slots * half**3 + half**3
    face = jax.ShapeDtypeStruct((slots, rows, width), BF16)
    return pl.pallas_call(
        functools.partial(coarse_kernel, coarse_slots),
        out_shape=(jax.ShapeDtypeStruct(enc.shape, BF16), face, face),
        in_specs=[SMEM] * 3 + [VMEM] * 7,
        out_specs=(VMEM, VMEM, VMEM),
        scratch_shapes=[
            pltpu.VMEM((total, width), BF16),
            pltpu.VMEM((TILE, width), jnp.int32),
            pltpu.VMEM((slots, 3, edge, edge * edge, width), BF16),
            pltpu.VMEM((slots, 3, edge, inside * edge, width), BF16),
            pltpu.VMEM((slots, 3, inside, inside * edge, width), BF16),
            pltpu.VMEM((slots, 3, inside, half * edge, width), BF16),
            pltpu.VMEM((slots, 2 * half * half * edge, width), F32),
            pltpu.SMEM((TILE, width), jnp.int32),
            pltpu.SMEM((slots, 8), jnp.int32),
            pltpu.SMEM((slots, 8), jnp.int32),
            pltpu.SemaphoreType.DMA,
        ],
        compiler_params=PARAMS,
        name="coarse",
    )(parent, info, send, *blocks, enc, w1, w2)


def encode(coarse_child, coarse_nbr, position, slots, width):
    coarse_slots = coarse_nbr.shape[0]
    child = jnp.where(coarse_child >= 0, coarse_child % (LANES * slots) + 1, 0)
    first = (position // LANES - 1) * LANES * coarse_slots
    neighbour = jnp.where(coarse_nbr >= 0, coarse_nbr - first + 1, 0)
    line = jnp.concatenate([child.reshape(1, -1), neighbour.reshape(1, -1)], axis=1)
    line = jnp.pad(line, ((0, TILE - 1), (0, width - line.shape[1])))
    return line.astype(BF16)


def per_device(
    features,
    fine_nbr,
    fine_send,
    fine_parent,
    coarse_child,
    coarse_nbr,
    enc_fine_w,
    enc_coarse_w,
    dec_coarse_w,
    dec_fine_w,
):
    slots, edge, _, _, width = features.shape
    coarse_slots = coarse_nbr.shape[0]
    size = lax.axis_size("gx")
    position = lax.axis_index("gx")
    is_odd = position % 2

    def swap(value, partner):
        pairs = [(i, partner(i)) for i in range(size) if 0 <= partner(i) < size]
        return lax.ppermute(value, "gx", pairs)

    def core(value):
        return swap(value, lambda i: i ^ 1)

    def next_chip(value):
        return swap(value, lambda i: i + 1 if i % 2 else i - 1)

    def across_y(value):
        return swap(value, lambda i: i ^ 2)

    def across_z(value):
        return swap(value, lambda i: i + 3 if i % 2 else i - 3)

    x = features.reshape(slots, edge, edge * edge, width)
    flat = [w.reshape(27 * width, width) for w in (enc_fine_w, enc_coarse_w, dec_coarse_w, dec_fine_w)]
    info = jnp.stack([is_odd, position]).astype(jnp.int32).reshape(1, 2)
    parent = fine_parent.reshape(1, slots)
    send = fine_send[0]
    listed = (send == jnp.arange(slots, dtype=jnp.int32)[None, :])[:, :, None, None]
    last = jnp.where(listed[0], x[:, edge - 1], jnp.zeros((), BF16))
    head = jnp.where(listed[1], x[:, 0], jnp.zeros((), BF16))
    far = next_chip(jnp.where(is_odd == 1, last, head))
    near = core(jnp.where(is_odd == 1, head, last))
    codes = encode(coarse_child, coarse_nbr, position, slots, width)
    main, part = inner(x, fine_nbr, flat[0])
    enc, pooled, rim = outer_pool(main, part, near, far, fine_nbr, info, parent, flat[0], codes)

    rim_c = core(rim)
    pooled_c = core(pooled)
    rim_z = across_z(jnp.concatenate([rim, rim_c], axis=0))
    crossed = across_y(jnp.concatenate([pooled, rim_z], axis=0))
    big = jnp.concatenate([rim_z, crossed], axis=0)
    blocks = [pooled, pooled_c, big, core(big)]
    dec_in, near_face, far_face = coarse(
        parent, info, send, blocks, enc, flat[1], flat[2], coarse_slots
    )
    far = next_chip(far_face)
    near = core(near_face)
    main, part = inner(dec_in, fine_nbr, flat[3])
    out = outer(main, part, near, far, fine_nbr, info, flat[3])
    return out.reshape(features.shape)


def solution(mesh):
    placed = (
        P(("groups", "gx"), None, None, None, None),
        P(("groups", "gx"), None),
        P(("groups", "gx"), None, None),
        P(("groups", "gx")),
        P(("groups", "gx"), None),
        P(("groups", "gx"), None),
        P(),
        P(),
        P(),
        P(),
    )
    return jax.shard_map(
        per_device,
        mesh=mesh,
        in_specs=placed,
        out_specs=P(("groups", "gx"), None, None, None, None),
        check_vma=False,
    )
```

time: 62.6 us -> 45.6 us (0.73)
  Pallas kernels: 29.1 us -> 16.6 us
  starting transfers between devices: 20 us -> 14 us
  waiting for transfers between devices: 6.38 us -> 8.03 us
    ppermute x17 -> x9, starting transfers between devices: 20 us -> 14 us  [swap(): return lax.ppermute(value, 'gx', pairs)]
    pallas_call x2, Pallas kernels: 12.5 us -> 6.95 us  [inner(): pl.pallas_call(inner_kernel, out_shape=(jax.ShapeDtypeStruct(x.shape, BF1...]
    pallas_call x1, Pallas kernels: 11 us -> 6.71 us  [coarse(): pl.pallas_call(functools.partial(coarse_kernel, coarse_slots), out_shape=...]
    unnamed x31 -> x22, local copies, waits for them, and re-layouts: 3.66 us -> 5.43 us
    pallas_call x1, Pallas kernels: 2.83 us -> 1.09 us  [outer_pool(): pl.pallas_call(outer_pool_kernel, out_shape=(jax.ShapeDtypeStruct(main.sh...]
    ppermute x17 -> x9, waiting for transfers between devices: 6.38 us -> 8.03 us  [swap(): return lax.ppermute(value, 'gx', pairs)]
    concatenate x1, local copies, waits for them, and re-layouts: 1.22 us -> 0.02 us  [per_device(): big = jnp.concatenate([rim_z, crossed], axis=0)]
    pallas_call x1, Pallas kernels: 2.74 us -> 1.9 us  [outer(): pl.pallas_call(outer_kernel, out_shape=jax.ShapeDtypeStruct(main.shape, B...]
  transfers between devices with their start and end apart: 17 -> 9, of which waited for: 6 -> 4; matrix products, arithmetic and copies ran while one was open for 3% -> 0% of each run, Pallas kernels for 20% -> 15%
where the time goes in v1:
time: 45.6 us; the launch traced here: 45.3 us
  Pallas kernels  16.6 us (36%)
  starting transfers between devices  14 us (31%)
  waiting for transfers between devices  8.03 us (18%)
  local copies, waits for them, and re-layouts  5.46 us (12%)
  other arithmetic  1.04 us (2%)
    ppermute x9, starting transfers between devices, swap(): return lax.ppermute(value, 'gx', pairs)  14 us
    ppermute x9, waiting for transfers between devices, swap(): return lax.ppermute(value, 'gx', pairs)  8.03 us
    pallas_call x2, Pallas kernels, inner(): pl.pallas_call(inner_kernel, out_shape=(jax.ShapeDtypeStruct(x.shape, BF1...  6.95 us
    pallas_call x1, Pallas kernels, coarse(): pl.pallas_call(functools.partial(coarse_kernel, coarse_slots), out_shape=...  6.71 us
    unnamed x22, local copies, waits for them, and re-layouts  5.43 us
    pallas_call x1, Pallas kernels, outer(): pl.pallas_call(outer_kernel, out_shape=jax.ShapeDtypeStruct(main.shape, B...  1.9 us
    pallas_call x1, Pallas kernels, outer_pool(): pl.pallas_call(outer_pool_kernel, out_shape=(jax.ShapeDtypeStruct(main.sh...  1.09 us
  transfers between devices with their start and end apart: 9, of which 4 were waited for; matrix products, arithmetic and copies ran while one was open for 0% of the time, Pallas kernels for 15%

profile of v1, /device:TPU:5, one launch (start us, length us, event | category | flops | bytes accessed | tf_op | source)
XLA Modules:
  0.0 45.3 jit_solution(14335112696226718786)
XLA Ops:
  0.0 0.0 copy-start.3
  0.0 0.8 %iota_compare_fusion.2 = pred[2,4]{1,0:T(4,128)(4,1)S(1)} fusion(s32[1,2,4]{2,1,0:T(2,128)} %param.12), kind=kLoop, calls=%fused_computation.26 | loop fusion | flops 8 | bytes 40 | tf_op jit(solution)/shard_map/eq | solution.py:520
  0.8 1.1 %copy.15 = bf16[4,8,8,8,128]{4,3,2,0,1:T(8,128)(2,1)S(1)} copy(bf16[4,8,8,8,128]{4,3,2,1,0:T(8,128)(2,1)} %param.10) | data formatting | bytes 1048576 | tf_op args[0]
  1.9 0.1 broadcast_select_fusion
  2.0 3.7 %collective-permute-start.1 = (bf16[4,64,128]{2,1,0:T(8,128)(2,1)S(1)}, bf16[4,64,128]{2,1,0:T(8,128)(2,1)S(1)}, u32[]{:S(2)}, u32[]{:S(2)}) collective-permute-start(bf16[4,64,128]{2,1,0:T(8,128)(2,1)S(1)} %get-tuple-element.25), channel_id=1, source_target_pairs={{1,2},{2,1},{3,4},{4,3},{5,6},{6,5},{7,8},{8,7},{9,10},{10,9},{11,... | collective-permute-start | bytes 196616 | tf_op jit(solution)/shard_map/ppermute | solution.py:501
  5.7 0.1 collective-permute-start
  5.8 0.0 copy-start.8
  5.8 0.6 %copy-done.8 = s32[1,8]{1,0:T(1,128)S(1)} copy-done((s32[1,8]{1,0:T(1,128)S(1)}, s32[1,8]{1,0:T(1,128)}, u32[]{:S(2)}) %copy-start.8) | copy-done | bytes 56
  6.4 0.0 copy-start.9
  6.4 0.6 %copy-done.9 = s32[1,27]{1,0:T(1,128)S(1)} copy-done((s32[1,27]{1,0:T(1,128)S(1)}, s32[1,27]{1,0:T(1,128)}, u32[]{:S(2)}) %copy-start.9) | copy-done | bytes 132
  7.1 0.1 fusion.7.code_ref
  7.2 0.0 copy-start.5
  7.2 0.0 copy-done.3
  7.2 0.7 %copy-done.5 = s32[4,27]{1,0:T(4,128)S(1)} copy-done((s32[4,27]{1,0:T(4,128)S(1)}, s32[4,27]{1,0:T(4,128)}, u32[]{:S(2)}) %copy-start.5) | copy-done | bytes 456
  7.9 0.0 copy-start.4
  7.9 1.0 %copy-done.4 = bf16[4,8,8,8,128]{4,3,2,1,0:T(8,128)(2,1)S(1)} copy-done((bf16[4,8,8,8,128]{4,3,2,1,0:T(8,128)(2,1)S(1)}, bf16[4,8,8,8,128]{4,3,2,1,0:T(8,128)(2,1)}, u32[]{:S(2)}) %copy-start.4) | copy-done | bytes 524312
  8.9 3.4 %inner.2 = (bf16[4,8,64,128]{3,2,1,0:T(8,128)(2,1)S(1)}, f32[4,2,64,128]{3,2,1,0:T(8,128)S(1)}) custom-call(s32[4,27]{1,0:T(4,128)S(1)} %copy-done.5, bf16[4,8,64,128]{3,2,1,0:T(8,128)(2,1)S(1)} %bitcast.42, bf16[3456,128]{1,0:T(8,128)(2,1)S(1)} %bitcast.40), custom_call_target="tpu_custom_call" | custom-call | flops 1811939328 | bytes 4194304 | tf_op jit(solution)/shard_map/inner/pallas_call | solution.py:124
  12.4 0.1 add_bitcast_fusion.info
  12.4 0.0 collective-permute-done.1.far_ref
  12.4 0.0 collective-permute-done.near_ref
  12.4 0.0 copy-start.6
  12.4 0.7 %copy-done.6 = s32[4]{0:T(128)S(1)} copy-done((s32[4]{0:T(128)S(1)}, s32[4]{0:T(128)}, u32[]{:S(2)}) %copy-start.6) | copy-done | bytes 40
  13.1 0.0 copy-start
  13.1 0.0 copy-start.1
  13.1 1.1 %outer_pool.1 = (bf16[4,8,64,128]{3,2,1,0:T(8,128)(2,1)S(1)}, bf16[272,128]{1,0:T(8,128)(2,1)S(1)}, bf16[144,128]{1,0:T(8,128)(2,1)S(1)}) custom-call(s32[4,27]{1,0:T(4,128)S(1)} %copy-done.5, s32[1,2]{1,0:T(1,128)S(1)} %add_bitcast_fusion.info, s32[1,4]{1,0:T(1,128)S(1)} %bitcast.43, bf16[4,64,128]{2,1,0:T(8,128)(2,1)S(1)} %collective-permute-done.near_ref, ...), custom_call_target="tpu_custom_call" | custom-call | tf_op jit(solution)/shard_map/outer_pool/pallas_call | solution.py:226
  14.2 0.5 %collective-permute-start.3 = (bf16[144,128]{1,0:T(8,128)(2,1)S(1)}, bf16[144,128]{1,0:T(8,128)(2,1)S(1)}, u32[]{:S(2)}, u32[]{:S(2)}) collective-permute-start(bf16[144,128]{1,0:T(8,128)(2,1)S(1)} %get-tuple-element.18), channel_id=1, source_target_pairs={{0,1},{1,0},{2,3},{3,2},{4,5},{5,4},{6,7},{7,6},{8,9},{9,8},{10,11... | collective-permute-start | bytes 110600 | tf_op jit(solution)/shard_map/ppermute | solution.py:501
  14.7 0.9 %collective-permute-done.3 = bf16[144,128]{1,0:T(8,128)(2,1)S(1)} collective-permute-done((bf16[144,128]{1,0:T(8,128)(2,1)S(1)}, bf16[144,128]{1,0:T(8,128)(2,1)S(1)}, u32[]{:S(2)}, u32[]{:S(2)}) %collective-permute-start.3) | collective-permute-done | bytes 36896 | tf_op jit(solution)/shard_map/ppermute | solution.py:501
  15.6 3.4 %collective-permute-start.4 = (bf16[288,128]{1,0:T(8,128)(2,1)S(1)}, bf16[288,128]{1,0:T(8,128)(2,1)S(1)}, u32[]{:S(2)}, u32[]{:S(2)}) collective-permute-start(bf16[288,128]{1,0:T(8,128)(2,1)S(1)} %pad_maximum_fusion.1), channel_id=1, source_target_pairs={{1,4},{3,6},{4,1},{5,8},{6,3},{7,10},{8,5},{9,12},{10,7},{11,14},{... | collective-permute-start | bytes 221192 | tf_op jit(solution)/shard_map/ppermute | solution.py:501
  19.0 2.4 %collective-permute-done.4 = bf16[288,128]{1,0:T(8,128)(2,1)S(1)} collective-permute-done((bf16[288,128]{1,0:T(8,128)(2,1)S(1)}, bf16[288,128]{1,0:T(8,128)(2,1)S(1)}, u32[]{:S(2)}, u32[]{:S(2)}) %collective-permute-start.4) | collective-permute-done | bytes 73760 | tf_op jit(solution)/shard_map/ppermute | solution.py:501
  21.4 0.3 collective-permute-start.5
  21.7 3.7 %collective-permute-done.5 = bf16[560,128]{1,0:T(8,128)(2,1)S(1)} collective-permute-done((bf16[560,128]{1,0:T(8,128)(2,1)S(1)}, bf16[560,128]{1,0:T(8,128)(2,1)S(1)}, u32[]{:S(2)}, u32[]{:S(2)}) %collective-permute-start.5) | collective-permute-done | bytes 143392 | tf_op jit(solution)/shard_map/ppermute | solution.py:501
  25.5 0.1 collective-permute-start.6
  25.6 0.5 %collective-permute-start.2 = (bf16[272,128]{1,0:T(8,128)(2,1)S(1)}, bf16[272,128]{1,0:T(8,128)(2,1)S(1)}, u32[]{:S(2)}, u32[]{:S(2)}) collective-permute-start(bf16[272,128]{1,0:T(8,128)(2,1)S(1)} %get-tuple-element.17.own_ref), channel_id=1, source_target_pairs={{0,1},{1,0},{2,3},{3,2},{4,5},{5,4},{6,7},{7,6},{8,9},{9,8},{10,11... | collective-permute-start | bytes 208904 | tf_op jit(solution)/shard_map/ppermute | solution.py:501
  26.1 1.1 %collective-permute-done.2.core_ref = bf16[272,128]{1,0:T(8,128)(2,1)S(1)} collective-permute-done((bf16[272,128]{1,0:T(8,128)(2,1)S(1)}, bf16[272,128]{1,0:T(8,128)(2,1)S(1)}, u32[]{:S(2)}, u32[]{:S(2)}) %collective-permute-start.2) | collective-permute-done | bytes 69664 | tf_op jit(solution)/shard_map/ppermute | solution.py:501
  27.1 0.0 collective-permute-done.6.bigc_ref
  27.1 0.0 copy-start.7
  27.1 0.0 copy-done
  27.1 0.0 copy-done.1
  27.1 0.7 %copy-done.7 = s32[1,2,4]{2,1,0:T(2,128)S(1)} copy-done((s32[1,2,4]{2,1,0:T(2,128)S(1)}, s32[1,2,4]{2,1,0:T(2,128)}, u32[]{:S(2)}) %copy-start.7) | copy-done | bytes 56
  27.8 0.0 copy-start.2
  27.8 6.7 %coarse.1 = (bf16[4,8,64,128]{3,2,1,0:T(8,128)(2,1)S(1)}, bf16[4,64,128]{2,1,0:T(8,128)(2,1)S(1)}, bf16[4,64,128]{2,1,0:T(8,128)(2,1)S(1)}) custom-call(s32[1,4]{1,0:T(1,128)S(1)} %bitcast.44, s32[1,2]{1,0:T(1,128)S(1)} %add_bitcast_fusion.info, s32[2,4]{1,0:T(2,128)S(1)} %bitcast.45, bf16[272,128]{1,0:T(8,128)(2,1)S(1)} %get-tuple-element.17.own_ref, ...), custom_call_target="tpu_custom_call" | custom-call | tf_op jit(solution)/shard_map/coarse/pallas_call | solution.py:448
  34.5 0.3 collective-permute-start.7
  34.8 5.1 %collective-permute-start.8 = (bf16[4,64,128]{2,1,0:T(8,128)(2,1)S(1)}, bf16[4,64,128]{2,1,0:T(8,128)(2,1)S(1)}, u32[]{:S(2)}, u32[]{:S(2)}) collective-permute-start(bf16[4,64,128]{2,1,0:T(8,128)(2,1)S(1)} %get-tuple-element.21), channel_id=1, source_target_pairs={{1,2},{2,1},{3,4},{4,3},{5,6},{6,5},{7,8},{8,7},{9,10},{10,9},{11,... | collective-permute-start | bytes 196616 | tf_op jit(solution)/shard_map/ppermute | solution.py:501
  39.9 0.0 copy-done.2
  39.9 3.5 %inner.3 = (bf16[4,8,64,128]{3,2,1,0:T(8,128)(2,1)S(1)}, f32[4,2,64,128]{3,2,1,0:T(8,128)S(1)}) custom-call(s32[4,27]{1,0:T(4,128)S(1)} %copy-done.5, bf16[4,8,64,128]{3,2,1,0:T(8,128)(2,1)S(1)} %get-tuple-element.22.x_ref, bf16[3456,128]{1,0:T(8,128)(2,1)S(1)} %bitcast.38), custom_call_target="tpu_custom_call" | custom-call | flops 1811939328 | bytes 4194304 | tf_op jit(solution)/shard_map/inner/pallas_call | solution.py:124
  43.4 0.0 collective-permute-done.7.near_ref
  43.4 0.0 collective-permute-done.8.far_ref
  43.4 1.9 %outer.1 = bf16[4,8,64,128]{3,2,1,0:T(8,128)(2,1)} custom-call(s32[4,27]{1,0:T(4,128)S(1)} %copy-done.5, s32[1,2]{1,0:T(1,128)S(1)} %add_bitcast_fusion.info, bf16[4,64,128]{2,1,0:T(8,128)(2,1)S(1)} %collective-permute-done.7.near_ref, bf16[4,64,128]{2,1,0:T(8,128)(2,1)S(1)} %collective-permute-done.8.far_ref, ...), custom_call_target="tpu_custom_call" | custom-call | tf_op jit(solution)/shard_map/outer/pallas_call | solution.py:190
  (7 shorter events, 0.1 us)
Async XLA Ops:
  0.0 7.2 %copy-start.3 = (bf16[27,128,128]{2,1,0:T(8,128)(2,1)S(1)}, bf16[27,128,128]{2,1,0:T(8,128)(2,1)}, u32[]{:S(2)}) copy-start(bf16[27,128,128]{2,1,0:T(8,128)(2,1)} %param.16) | copy-start | bytes 2654212
  2.0 10.5 %collective-permute-start.1 = (bf16[4,64,128]{2,1,0:T(8,128)(2,1)S(1)}, bf16[4,64,128]{2,1,0:T(8,128)(2,1)S(1)}, u32[]{:S(2)}, u32[]{:S(2)}) collective-permute-start(bf16[4,64,128]{2,1,0:T(8,128)(2,1)S(1)} %get-tuple-element.25), channel_id=1, source_target_pairs={{1,2},{2,1},{3,4},{4,3},{5,6},{6,5},{7,8},{8,7},{9,10},{10,9},{11,... | collective-permute-start | bytes 196616 | tf_op jit(solution)/shard_map/ppermute | solution.py:501
  5.7 6.8 %collective-permute-start = (bf16[4,64,128]{2,1,0:T(8,128)(2,1)S(1)}, bf16[4,64,128]{2,1,0:T(8,128)(2,1)S(1)}, u32[]{:S(2)}, u32[]{:S(2)}) collective-permute-start(bf16[4,64,128]{2,1,0:T(8,128)(2,1)S(1)} %get-tuple-element.26), channel_id=1, source_target_pairs={{0,1},{1,0},{2,3},{3,2},{4,5},{5,4},{6,7},{7,6},{8,9},{9,8},{10,11... | collective-permute-start | bytes 196616 | tf_op jit(solution)/shard_map/ppermute | solution.py:501
  5.8 0.7 %copy-start.8 = (s32[1,8]{1,0:T(1,128)S(1)}, s32[1,8]{1,0:T(1,128)}, u32[]{:S(2)}) copy-start(s32[1,8]{1,0:T(1,128)} %param.14) | copy-start | bytes 100
  6.4 0.7 %copy-start.9 = (s32[1,27]{1,0:T(1,128)S(1)}, s32[1,27]{1,0:T(1,128)}, u32[]{:S(2)}) copy-start(s32[1,27]{1,0:T(1,128)} %param.15) | copy-start | bytes 328
  7.2 0.7 %copy-start.5 = (s32[4,27]{1,0:T(4,128)S(1)}, s32[4,27]{1,0:T(4,128)}, u32[]{:S(2)}) copy-start(s32[4,27]{1,0:T(4,128)} %nbr.7) | copy-start | bytes 1300
  7.9 1.0 %copy-start.4 = (bf16[4,8,8,8,128]{4,3,2,1,0:T(8,128)(2,1)S(1)}, bf16[4,8,8,8,128]{4,3,2,1,0:T(8,128)(2,1)}, u32[]{:S(2)}) copy-start(bf16[4,8,8,8,128]{4,3,2,1,0:T(8,128)(2,1)} %param.10) | copy-start | bytes 1572868
  12.4 0.7 %copy-start.6 = (s32[4]{0:T(128)S(1)}, s32[4]{0:T(128)}, u32[]{:S(2)}) copy-start(s32[4]{0:T(128)} %param.13) | copy-start | bytes 52
  13.1 14.0 %copy-start = (bf16[27,128,128]{2,1,0:T(8,128)(2,1)S(1)}, bf16[27,128,128]{2,1,0:T(8,128)(2,1)}, u32[]{:S(2)}) copy-start(bf16[27,128,128]{2,1,0:T(8,128)(2,1)} %param.17) | copy-start | bytes 2654212
  13.1 14.0 %copy-start.1 = (bf16[27,128,128]{2,1,0:T(8,128)(2,1)S(1)}, bf16[27,128,128]{2,1,0:T(8,128)(2,1)}, u32[]{:S(2)}) copy-start(bf16[27,128,128]{2,1,0:T(8,128)(2,1)} %param.18) | copy-start | bytes 2654212
  14.2 1.4 %collective-permute-start.3 = (bf16[144,128]{1,0:T(8,128)(2,1)S(1)}, bf16[144,128]{1,0:T(8,128)(2,1)S(1)}, u32[]{:S(2)}, u32[]{:S(2)}) collective-permute-start(bf16[144,128]{1,0:T(8,128)(2,1)S(1)} %get-tuple-element.18), channel_id=1, source_target_pairs={{0,1},{1,0},{2,3},{3,2},{4,5},{5,4},{6,7},{7,6},{8,9},{9,8},{10,11... | collective-permute-start | bytes 110600 | tf_op jit(solution)/shard_map/ppermute | solution.py:501
  15.6 5.8 %collective-permute-start.4 = (bf16[288,128]{1,0:T(8,128)(2,1)S(1)}, bf16[288,128]{1,0:T(8,128)(2,1)S(1)}, u32[]{:S(2)}, u32[]{:S(2)}) collective-permute-start(bf16[288,128]{1,0:T(8,128)(2,1)S(1)} %pad_maximum_fusion.1), channel_id=1, source_target_pairs={{1,4},{3,6},{4,1},{5,8},{6,3},{7,10},{8,5},{9,12},{10,7},{11,14},{... | collective-permute-start | bytes 221192 | tf_op jit(solution)/shard_map/ppermute | solution.py:501
  21.4 4.0 %collective-permute-start.5 = (bf16[560,128]{1,0:T(8,128)(2,1)S(1)}, bf16[560,128]{1,0:T(8,128)(2,1)S(1)}, u32[]{:S(2)}, u32[]{:S(2)}) collective-permute-start(bf16[560,128]{1,0:T(8,128)(2,1)S(1)} %pad_maximum_fusion), channel_id=1, source_target_pairs={{0,2},{1,3},{2,0},{3,1},{4,6},{5,7},{6,4},{7,5},{8,10},{9,11},{10,... | collective-permute-start | bytes 430088 | tf_op jit(solution)/shard_map/ppermute | solution.py:501
  25.5 1.6 %collective-permute-start.6 = (bf16[848,128]{1,0:T(8,128)(2,1)S(1)}, bf16[848,128]{1,0:T(8,128)(2,1)S(1)}, u32[]{:S(2)}, u32[]{:S(2)}) collective-permute-start(bf16[848,128]{1,0:T(8,128)(2,1)S(1)} %constant_dynamic-update-slice_fusion.big_ref), channel_id=1, source_target_pairs={{0,1},{1,0},{2,3},{3,2},{4,5},{5,4},{6,7},{7,6},{8,9},{9,8},{10,11... | collective-permute-start | bytes 651272 | tf_op jit(solution)/shard_map/ppermute | solution.py:501
  25.6 1.6 %collective-permute-start.2 = (bf16[272,128]{1,0:T(8,128)(2,1)S(1)}, bf16[272,128]{1,0:T(8,128)(2,1)S(1)}, u32[]{:S(2)}, u32[]{:S(2)}) collective-permute-start(bf16[272,128]{1,0:T(8,128)(2,1)S(1)} %get-tuple-element.17.own_ref), channel_id=1, source_target_pairs={{0,1},{1,0},{2,3},{3,2},{4,5},{5,4},{6,7},{7,6},{8,9},{9,8},{10,11... | collective-permute-start | bytes 208904 | tf_op jit(solution)/shard_map/ppermute | solution.py:501
  27.1 0.7 %copy-start.7 = (s32[1,2,4]{2,1,0:T(2,128)S(1)}, s32[1,2,4]{2,1,0:T(2,128)}, u32[]{:S(2)}) copy-start(s32[1,2,4]{2,1,0:T(2,128)} %param.12) | copy-start | bytes 100
  27.8 12.1 %copy-start.2 = (bf16[27,128,128]{2,1,0:T(8,128)(2,1)S(1)}, bf16[27,128,128]{2,1,0:T(8,128)(2,1)}, u32[]{:S(2)}) copy-start(bf16[27,128,128]{2,1,0:T(8,128)(2,1)} %param.19) | copy-start | bytes 2654212
  34.5 8.9 %collective-permute-start.7 = (bf16[4,64,128]{2,1,0:T(8,128)(2,1)S(1)}, bf16[4,64,128]{2,1,0:T(8,128)(2,1)S(1)}, u32[]{:S(2)}, u32[]{:S(2)}) collective-permute-start(bf16[4,64,128]{2,1,0:T(8,128)(2,1)S(1)} %get-tuple-element.20), channel_id=1, source_target_pairs={{0,1},{1,0},{2,3},{3,2},{4,5},{5,4},{6,7},{7,6},{8,9},{9,8},{10,11... | collective-permute-start | bytes 196616 | tf_op jit(solution)/shard_map/ppermute | solution.py:501
  34.8 8.6 %collective-permute-start.8 = (bf16[4,64,128]{2,1,0:T(8,128)(2,1)S(1)}, bf16[4,64,128]{2,1,0:T(8,128)(2,1)S(1)}, u32[]{:S(2)}, u32[]{:S(2)}) collective-permute-start(bf16[4,64,128]{2,1,0:T(8,128)(2,1)S(1)} %get-tuple-element.21), channel_id=1, source_target_pairs={{1,2},{2,1},{3,4},{4,3},{5,6},{6,5},{7,8},{8,7},{9,10},{10,9},{11,... | collective-permute-start | bytes 196616 | tf_op jit(solution)/shard_map/ppermute | solution.py:501

commit v2 on v1

--- a/solution.py
+++ b/solution.py
@@ -6,6 +6,7 @@
 from jax.experimental import pallas as pl
 from jax.experimental.pallas import tpu as pltpu
 from jax.sharding import PartitionSpec as P
+
 
 LANES = 4
 GROUP = 1
@@ -16,6 +17,7 @@
 F32 = jnp.float32
 VMEM = pl.BlockSpec(memory_space=pltpu.VMEM)
 SMEM = pl.BlockSpec(memory_space=pltpu.SMEM)
+HBM = pl.BlockSpec(memory_space=pltpu.HBM)
 PARAMS = pltpu.CompilerParams(vmem_limit_bytes=16 << 20)
 
 
@@ -79,26 +81,105 @@
     return jnp.concatenate(sides, axis=2).reshape(planes, 2 * pairs * edge, width)
 
 
-def inner_kernel(nbr, x_ref, w_ref, out_ref, part_ref, cols):
-    slots, edge, rows, width = x_ref.shape
+def first_kernel(
+    info, x_hbm, nbr_hbm, send_hbm, parent_hbm, child_hbm, around_hbm,
+    near_ref, far_ref, meta_ref, codes_ref,
+    head_v, last_v, nbr_v, send_v, parent_v, child_v, around_v, numbers, sems,
+):
+    slots, edge, _, _ = x_hbm.shape
+    coarse_slots = child_v.shape[0]
+    pairs = [(x_hbm.at[:, 0], head_v), (x_hbm.at[:, edge - 1], last_v)]
+    pairs += [(nbr_hbm, nbr_v), (send_hbm, send_v), (parent_hbm, parent_v)]
+    pairs += [(child_hbm, child_v), (around_hbm, around_v)]
+    copies = [pltpu.make_async_copy(*pair, sems.at[i]) for i, pair in enumerate(pairs)]
+    for copy in copies:
+        copy.start()
+    for copy in copies:
+        copy.wait()
+    position = info[0, 0]
+    meta_ref[...] = jnp.full(meta_ref.shape, position, jnp.int32)
+    meta_ref[0:slots, 0:27] = nbr_v[...]
+    meta_ref[slots : slots + 2, 0:slots] = send_v[...]
+    meta_ref[slots + 2 : slots + 3, 0:slots] = parent_v[...]
+    numbers[...] = jnp.zeros_like(numbers)
+    child = child_v[...]
+    numbers[0:coarse_slots, 0:8] = jnp.where(child >= 0, (child & (LANES * slots - 1)) + 1, 0)
+    around = around_v[...]
+    first = ((position >> 2) - 1) * LANES * coarse_slots
+    numbers[coarse_slots : 2 * coarse_slots, 0:27] = jnp.where(around >= 0, around - first + 1, 0)
+    codes_ref[...] = numbers[...].astype(F32).astype(BF16)
+    is_odd = (position & 1) == 1
+    send = send_v[...]
+    slot_of = lax.broadcasted_iota(jnp.int32, send.shape, 1)
+    listed = jnp.where(send == slot_of, 1.0, 0.0)
+    for b in range(slots):
+        last = last_v[b].astype(F32) * listed[0:1, b : b + 1]
+        head = head_v[b].astype(F32) * listed[1:2, b : b + 1]
+        near_ref[b] = jnp.where(is_odd, head, last).astype(BF16)
+        far_ref[b] = jnp.where(is_odd, last, head).astype(BF16)
+
+
+def stay(value):
+    return pltpu.with_memory_space_constraint(value, pltpu.HBM)
+
+
+def first(info, x, nbr, send, parent, child, around):
+    slots, _, rows, width = x.shape
+    coarse_slots = child.shape[0]
+    assert 2 * coarse_slots <= TILE and (LANES * slots) & (LANES * slots - 1) == 0
+    face = jax.ShapeDtypeStruct((slots, rows, width), BF16)
+    return pl.pallas_call(
+        first_kernel,
+        out_shape=(
+            face,
+            face,
+            jax.ShapeDtypeStruct((slots + 4, width), jnp.int32),
+            jax.ShapeDtypeStruct((TILE, width), BF16),
+        ),
+        in_specs=[SMEM] + [HBM] * 6,
+        out_specs=(VMEM,) * 4,
+        scratch_shapes=[pltpu.VMEM((slots, rows, width), BF16)] * 2
+        + [pltpu.VMEM(v.shape, jnp.int32) for v in (nbr, send, parent, child, around)]
+        + [pltpu.VMEM((TILE, width), jnp.int32), pltpu.SemaphoreType.DMA((7,))],
+        compiler_params=PARAMS,
+        cost_estimate=pl.CostEstimate(flops=0, bytes_accessed=2097152, transcendentals=0),
+        name="first",
+    )(info, *[stay(v) for v in (x, nbr, send, parent, child, around)])
+
+
+def loading_kernel(nbr, x_hbm, w_hbm, out_ref, part_ref, cols, x_ref, w_ref, sems):
+    copies = [
+        pltpu.make_async_copy(source, target, sems.at[i])
+        for i, (source, target) in enumerate(((x_hbm, x_ref), (w_hbm, w_ref)))
+    ]
+    for copy in copies:
+        copy.start()
+    copies[0].wait()
+    inner_kernel(nbr, x_ref, w_ref, out_ref, part_ref, cols, copies[1])
+
+
+def inner_kernel(nbr, x_ref, w_ref, out_ref, part_ref, cols, waiting=None):
+    slots, edge, _, width = x_ref.shape
     pairs = edge // 2
     empty = jnp.zeros((slots, 4, 3, pairs * edge, width), BF16)
     cols[:, :, :, 0] = empty
     cols[:, :, :, edge + 1] = empty
+    for b in range(slots):
+        def fetch(dy, dz):
+            slot = nbr[b, tap(0, dy, dz)]
+            held = jnp.maximum(slot, 0)
+            value = y_rows(lambda r, n: x_ref[held, :, r : r + n, :].astype(F32), dy, edge)
+            return jnp.where(slot >= 0, value, 0.0)
+
+        for k, full in enumerate(columns(fetch, edge)):
+            for j in range(4):
+                cols[b, j, k, 1 : edge + 1] = pair_rows(full, j, pairs)
+    if waiting is not None:
+        waiting.wait()
     weights = pair_weights(w_ref, range(3), width)
     for group in range(0, slots, GROUP):
         bricks = []
         for b in range(group, group + GROUP):
-
-            def fetch(dy, dz):
-                slot = nbr[b, tap(0, dy, dz)]
-                held = jnp.maximum(slot, 0)
-                value = y_rows(lambda r, n: x_ref[held, :, r : r + n, :].astype(F32), dy, edge)
-                return jnp.where(slot >= 0, value, 0.0)
-
-            for k, full in enumerate(columns(fetch, edge)):
-                for j in range(4):
-                    cols[b, j, k, 1 : edge + 1] = pair_rows(full, j, pairs)
             taps = []
             for dx in range(3):
                 for j in range(4):
@@ -119,19 +200,21 @@
             part_ref[b, 1] = total[edge - 1]
 
 
-def inner(x, nbr, weights):
+def inner(x, nbr, weights, load=False):
     slots, edge, rows, width = x.shape
     return pl.pallas_call(
-        inner_kernel,
+        loading_kernel if load else inner_kernel,
         out_shape=(
             jax.ShapeDtypeStruct(x.shape, BF16),
             jax.ShapeDtypeStruct((slots, 2, rows, width), F32),
         ),
-        in_specs=[SMEM, VMEM, VMEM],
+        in_specs=[SMEM] + [HBM if load else VMEM] * 2,
         out_specs=(VMEM, VMEM),
         scratch_shapes=[
             pltpu.VMEM((slots, 4, 3, edge + 2, rows // 2, width), BF16),
-        ],
+        ]
+        + load
+        * [pltpu.VMEM(x.shape, BF16), pltpu.VMEM(weights.shape, BF16), pltpu.SemaphoreType.DMA((2,))],
         compiler_params=PARAMS,
         cost_estimate=pl.CostEstimate(
             flops=2 * slots * edge * rows * 27 * width * width,
@@ -139,14 +222,14 @@
             transcendentals=0,
         ),
         name="inner",
-    )(nbr, x, weights)
-
-
-def outer_planes(nbr, info, near_ref, far_ref, part_ref, w_ref, out_ref):
+    )(nbr, *([stay(x), stay(weights)] if load else [x, weights]))
+
+
+def outer_planes(nbr, near_ref, far_ref, part_ref, w_ref, out_ref):
     slots, _, rows, width = part_ref.shape
     edge = out_ref.shape[1]
     pairs = edge // 2
-    is_odd = info[0, 0] == 1
+    is_odd = (nbr[slots + 3, 0] & 1) == 1
     for side, dx in enumerate((-1, 1)):
         use_near = is_odd if side == 0 else jnp.logical_not(is_odd)
         bricks = []
@@ -181,29 +264,30 @@
             out_ref[b, plane] = jnp.maximum(total, 0.0).astype(BF16)
 
 
-def outer_kernel(nbr, info, near_ref, far_ref, part_ref, w_ref, main_ref, out_ref):
+def outer_kernel(nbr, near_ref, far_ref, part_ref, w_ref, main_ref, out_ref):
     out_ref[:, 1 : out_ref.shape[1] - 1] = main_ref[:, 1 : out_ref.shape[1] - 1]
-    outer_planes(nbr, info, near_ref, far_ref, part_ref, w_ref, out_ref)
-
-
-def outer(main, part, near, far, nbr, info, weights):
+    outer_planes(nbr, near_ref, far_ref, part_ref, w_ref, out_ref)
+
+
+def outer(main, part, near, far, nbr, weights):
     return pl.pallas_call(
         outer_kernel,
         out_shape=jax.ShapeDtypeStruct(main.shape, BF16),
-        in_specs=[SMEM, SMEM, VMEM, VMEM, VMEM, VMEM, VMEM],
+        in_specs=[SMEM, VMEM, VMEM, VMEM, VMEM, VMEM],
         out_specs=VMEM,
         compiler_params=PARAMS,
+        cost_estimate=pl.CostEstimate(flops=536870912, bytes_accessed=4194304, transcendentals=0),
         name="outer",
-    )(nbr, info, near, far, part, weights, main)
+    )(nbr, near, far, part, weights, main)
 
 
 def outer_pool_kernel(
-    nbr, info, parent, near_ref, far_ref, part_ref, w_ref, main_ref, code_ref, out_ref, pool_ref, rim_ref, sums
+    nbr, near_ref, far_ref, part_ref, w_ref, main_ref, code_ref, out_ref, pool_ref, rim_ref, sums
 ):
-    slots, edge, rows, width = out_ref.shape
+    slots, edge, _, width = out_ref.shape
     half = edge // 2
     out_ref[:, 1 : edge - 1] = main_ref[:, 1 : edge - 1]
-    outer_planes(nbr, info, near_ref, far_ref, part_ref, w_ref, out_ref)
+    outer_planes(nbr, near_ref, far_ref, part_ref, w_ref, out_ref)
     cells = half**3
     pool_ref[slots * cells :] = code_ref[...]
     rim_ref[slots * cells // 2 :] = code_ref[...]
@@ -215,13 +299,13 @@
         high = sums[b, pl.ds(1, cells, stride=2), :]
         pooled = (low + high) * 0.125
         pool_ref[b * cells : (b + 1) * cells, :] = pooled.astype(BF16)
-        outer_x = (jnp.maximum(parent[0, b], 0) >> 2) & 1
+        outer_x = (jnp.maximum(nbr[slots + 2, b], 0) >> 2) & 1
         rim = jnp.where(outer_x == 0, pooled[: cells // 2], pooled[cells // 2 :])
         rim_ref[b * cells // 2 : (b + 1) * cells // 2, :] = rim.astype(BF16)
 
 
-def outer_pool(main, part, near, far, nbr, info, parent, weights, codes):
-    slots, edge, rows, width = main.shape
+def outer_pool(main, part, near, far, nbr, weights, codes):
+    slots, edge, _, width = main.shape
     cells = (edge // 2) ** 3
     return pl.pallas_call(
         outer_pool_kernel,
@@ -230,12 +314,13 @@
             jax.ShapeDtypeStruct((slots * cells + TILE, width), BF16),
             jax.ShapeDtypeStruct((slots * cells // 2 + TILE, width), BF16),
         ),
-        in_specs=[SMEM, SMEM, SMEM, VMEM, VMEM, VMEM, VMEM, VMEM, VMEM],
+        in_specs=[SMEM, VMEM, VMEM, VMEM, VMEM, VMEM, VMEM],
         out_specs=(VMEM, VMEM, VMEM),
         scratch_shapes=[pltpu.VMEM((slots, 2 * cells, width), F32)],
         compiler_params=PARAMS,
+        cost_estimate=pl.CostEstimate(flops=536870912, bytes_accessed=4194304, transcendentals=0),
         name="outer_pool",
-    )(nbr, info, parent, near, far, part, weights, main, codes)
+    )(nbr, near, far, part, weights, main, codes)
 
 
 def source_row(rel, device, lane_y, lane_c):
@@ -295,27 +380,25 @@
 
 
 def coarse_kernel(
-    coarse_slots, parent, info, send, own_ref, core_ref, big_ref, bigc_ref, enc_ref, w1_ref, w2_ref,
+    coarse_slots, meta, own_ref, core_ref, y_ref, yc_ref, big_ref, bigc_ref, enc_ref, w1_ref, w2_ref,
     out_ref, near_ref, far_ref, held, codes, even, odd, even2, odd2, spread, table, row_s, there_s, sem,
 ):
     slots, edge, rows, width = enc_ref.shape
     half = edge // 2
     plane = half * half
     cells = half * plane
-    position = info[0, 1]
+    position = meta[slots + 3, 0]
     lane_y = (position >> 1) & 1
     lane_c = position & 1
     whole_rows = slots * cells
     rim_rows = whole_rows // 2
-    rim_at = [0, rim_rows + TILE, 2 * rim_rows + whole_rows + 3 * TILE]
-    rim_at.append(rim_at[2] + rim_rows + TILE)
-    whole_at = 2 * (rim_rows + TILE)
-    places = [(own_ref, 0, whole_rows), (core_ref, 0, whole_rows)]
-    places += [(ref, whole_at, whole_rows) for ref in (big_ref, bigc_ref)]
+    rim_at = [i * (rim_rows + TILE) for i in range(4)]
+    places = [(ref, 0, whole_rows) for ref in (own_ref, core_ref, y_ref, yc_ref)]
     places += [(ref, at, rim_rows) for ref in (big_ref, bigc_ref) for at in rim_at]
+    lines = 2 * coarse_slots
     for i, (ref, at, count) in enumerate(places):
-        line = ref[at + count : at + count + TILE].astype(F32)[:1]
-        codes[i : i + 1] = line.astype(jnp.int32)
+        line = ref[at + count : at + count + TILE].astype(F32)[:lines]
+        codes[i * lines : (i + 1) * lines] = line.astype(jnp.int32)
     copy = pltpu.make_async_copy(codes, table, sem)
     copy.start()
     first = 0
@@ -333,7 +416,7 @@
     regions = []
     masks = []
     for b in range(slots):
-        own = parent[0, b]
+        own = meta[slots + 2, b]
         known = own >= 0
         own = jnp.maximum(own, 0)
         octant = own & 7
@@ -348,15 +431,15 @@
             for scale, s, c in zip((9, 3, 1), sign, crossed):
                 if c:
                     number = number + scale * s
-            found = table[home, 8 * coarse_slots + home_slot * 27 + number] - 1
+            found = table[home * lines + coarse_slots + home_slot, number] - 1
             there = known & (found >= 0)
             there_s[b, cross] = jnp.where(there, 1, 0)
             found = jnp.maximum(found, 0)
             rel = found // (LANES * coarse_slots) - 1
             lane = found // coarse_slots % LANES
-            start = found % coarse_slots * 8
+            start = found % coarse_slots
             row = source_row(rel, lane, lane_y, lane_c)
-            row_s[b, cross] = jnp.where(there, (rel + 1) * 65536 + row * 1024 + start, -1)
+            row_s[b, cross] = jnp.where(there, (rel + 1) * 65536 + row * lines + start, -1)
 
         def base_of(ex, ey, ez):
             cross = 0
@@ -369,7 +452,7 @@
             there = entry >= 0
             entry = jnp.maximum(entry, 0)
             rel = (entry >> 16) - 1
-            child = table[(entry >> 10) & 63, (entry & 1023) + (octant ^ flip)] - 1
+            child = table[entry & 65535, octant ^ flip] - 1
             valid = there & (child >= 0)
             child = jnp.maximum(child, 0)
             source = source_row(rel, child // slots, lane_y, lane_c)
@@ -425,7 +508,7 @@
     fines = valid_conv(mids, x_pair_weights(w2_ref, width), (even2, odd2), edge, width)
     is_odd = lane_c == 1
     for b in range(slots):
-        value = jnp.where(parent[0, b] >= 0, fines[b], 0.0).reshape(plane * edge, width)
+        value = jnp.where(meta[slots + 2, b] >= 0, fines[b], 0.0).reshape(plane * edge, width)
         spread[b, pl.ds(0, plane * edge, stride=2), :] = value
         spread[b, pl.ds(1, plane * edge, stride=2), :] = value
         up = spread[b].reshape(half, half, 2 * edge, width)[:, :, :edge]
@@ -433,13 +516,13 @@
         total = base + up[:, None, :, None]
         total = total.reshape(edge, rows, width).astype(BF16)
         out_ref[b] = total
-        last = jnp.where(send[0, b] == b, total[edge - 1], 0)
-        head = jnp.where(send[1, b] == b, total[0], 0)
+        last = jnp.where(meta[slots, b] == b, total[edge - 1], 0)
+        head = jnp.where(meta[slots + 1, b] == b, total[0], 0)
         near_ref[b] = jnp.where(is_odd, head, last)
         far_ref[b] = jnp.where(is_odd, last, head)
 
 
-def coarse(parent, info, send, blocks, enc, w1, w2, coarse_slots):
+def coarse(meta, blocks, enc, w1, w2, coarse_slots):
     slots, edge, rows, width = enc.shape
     half = edge // 2
     inside = edge - 2
@@ -448,34 +531,25 @@
     return pl.pallas_call(
         functools.partial(coarse_kernel, coarse_slots),
         out_shape=(jax.ShapeDtypeStruct(enc.shape, BF16), face, face),
-        in_specs=[SMEM] * 3 + [VMEM] * 7,
+        in_specs=[SMEM] + [VMEM] * 9,
         out_specs=(VMEM, VMEM, VMEM),
         scratch_shapes=[
             pltpu.VMEM((total, width), BF16),
-            pltpu.VMEM((TILE, width), jnp.int32),
+            pltpu.VMEM((3 * LANES * 2 * coarse_slots, width), jnp.int32),
             pltpu.VMEM((slots, 3, edge, edge * edge, width), BF16),
             pltpu.VMEM((slots, 3, edge, inside * edge, width), BF16),
             pltpu.VMEM((slots, 3, inside, inside * edge, width), BF16),
             pltpu.VMEM((slots, 3, inside, half * edge, width), BF16),
             pltpu.VMEM((slots, 2 * half * half * edge, width), F32),
-            pltpu.SMEM((TILE, width), jnp.int32),
+            pltpu.SMEM((3 * LANES * 2 * coarse_slots, width), jnp.int32),
             pltpu.SMEM((slots, 8), jnp.int32),
             pltpu.SMEM((slots, 8), jnp.int32),
             pltpu.SemaphoreType.DMA,
         ],
         compiler_params=PARAMS,
+        cost_estimate=pl.CostEstimate(flops=2147483648, bytes_accessed=8388608, transcendentals=0),
         name="coarse",
-    )(parent, info, send, *blocks, enc, w1, w2)
-
-
-def encode(coarse_child, coarse_nbr, position, slots, width):
-    coarse_slots = coarse_nbr.shape[0]
-    child = jnp.where(coarse_child >= 0, coarse_child % (LANES * slots) + 1, 0)
-    first = (position // LANES - 1) * LANES * coarse_slots
-    neighbour = jnp.where(coarse_nbr >= 0, coarse_nbr - first + 1, 0)
-    line = jnp.concatenate([child.reshape(1, -1), neighbour.reshape(1, -1)], axis=1)
-    line = jnp.pad(line, ((0, TILE - 1), (0, width - line.shape[1])))
-    return line.astype(BF16)
+    )(meta, *blocks, enc, w1, w2)
 
 
 def per_device(
@@ -494,7 +568,6 @@
     coarse_slots = coarse_nbr.shape[0]
     size = lax.axis_size("gx")
     position = lax.axis_index("gx")
-    is_odd = position % 2
 
     def swap(value, partner):
         pairs = [(i, partner(i)) for i in range(size) if 0 <= partner(i) < size]
@@ -514,31 +587,29 @@
 
     x = features.reshape(slots, edge, edge * edge, width)
     flat = [w.reshape(27 * width, width) for w in (enc_fine_w, enc_coarse_w, dec_coarse_w, dec_fine_w)]
-    info = jnp.stack([is_odd, position]).astype(jnp.int32).reshape(1, 2)
-    parent = fine_parent.reshape(1, slots)
-    send = fine_send[0]
-    listed = (send == jnp.arange(slots, dtype=jnp.int32)[None, :])[:, :, None, None]
-    last = jnp.where(listed[0], x[:, edge - 1], jnp.zeros((), BF16))
-    head = jnp.where(listed[1], x[:, 0], jnp.zeros((), BF16))
-    far = next_chip(jnp.where(is_odd == 1, last, head))
-    near = core(jnp.where(is_odd == 1, head, last))
-    codes = encode(coarse_child, coarse_nbr, position, slots, width)
-    main, part = inner(x, fine_nbr, flat[0])
-    enc, pooled, rim = outer_pool(main, part, near, far, fine_nbr, info, parent, flat[0], codes)
+    info = position.astype(jnp.int32).reshape(1, 1)
+    near, far, meta, codes = first(
+        info, x, fine_nbr, fine_send[0], fine_parent.reshape(1, slots), coarse_child, coarse_nbr
+    )
+    far = next_chip(far)
+    near = core(near)
+    main, part = inner(x, meta, flat[0], load=True)
+    enc, pooled, rim = outer_pool(main, part, near, far, meta, flat[0], codes)
 
     rim_c = core(rim)
+    rim_z = across_z(jnp.concatenate([rim, rim_c], axis=0))
+    pooled_y = across_y(pooled)
+    rim_zy = across_y(rim_z)
+    big = jnp.concatenate([rim_z, rim_zy], axis=0)
     pooled_c = core(pooled)
-    rim_z = across_z(jnp.concatenate([rim, rim_c], axis=0))
-    crossed = across_y(jnp.concatenate([pooled, rim_z], axis=0))
-    big = jnp.concatenate([rim_z, crossed], axis=0)
-    blocks = [pooled, pooled_c, big, core(big)]
-    dec_in, near_face, far_face = coarse(
-        parent, info, send, blocks, enc, flat[1], flat[2], coarse_slots
-    )
-    far = next_chip(far_face)
-    near = core(near_face)
-    main, part = inner(dec_in, fine_nbr, flat[3])
-    out = outer(main, part, near, far, fine_nbr, info, flat[3])
+    pooled_yc = core(pooled_y)
+    big_c = core(big)
+    blocks = [pooled, pooled_c, pooled_y, pooled_yc, big, big_c]
+    dec_in, near, far = coarse(meta, blocks, enc, flat[1], flat[2], coarse_slots)
+    far = next_chip(far)
+    near = core(near)
+    main, part = inner(dec_in, meta, flat[3])
+    out = outer(main, part, near, far, meta, flat[3])
     return out.reshape(features.shape)
 
 

time: 45.6 us -> 44.4 us (0.974)
  local copies, waits for them, and re-layouts: 5.46 us -> 0.04 us
  Pallas kernels: 16.6 us -> 19.4 us
  waiting for transfers between devices: 8.03 us -> 9.72 us
  other arithmetic: 1.04 us -> 0.01 us
  starting transfers between devices: 14 us -> 14.9 us
    unnamed x22 -> x9, local copies, waits for them, and re-layouts: 5.43 us -> 0.03 us
    pallas_call x2 -> x3, Pallas kernels: 6.95 us -> 9.62 us  [the longest x2 8.55 us: inner(): pl.pallas_call(loading_kernel if load else inner_kernel, out_shape=(jax.S...]
    ppermute x9 -> x11, waiting for transfers between devices: 8.03 us -> 9.72 us  [swap(): return lax.ppermute(value, 'gx', pairs)]
    ppermute x9 -> x11, starting transfers between devices: 14 us -> 14.9 us  [swap(): return lax.ppermute(value, 'gx', pairs)]
    eq x1 -> x0, other arithmetic: 0.76 us -> none  [per_device(): send == jnp.arange(slots, dtype=jnp.int32)[None, :]]
  transfers between devices with their start and end apart: 9 -> 11, of which waited for: 4 -> 5; matrix products, arithmetic and copies ran while one was open for 0% -> 0% of each run, Pallas kernels for 15% -> 19%
where the time goes in v2:
time: 44.4 us; the launch traced here: 44.2 us
  Pallas kernels  19.4 us (44%)
  starting transfers between devices  14.9 us (34%)
  waiting for transfers between devices  9.72 us (22%)
    ppermute x11, starting transfers between devices, swap(): return lax.ppermute(value, 'gx', pairs)  14.9 us
    ppermute x11, waiting for transfers between devices, swap(): return lax.ppermute(value, 'gx', pairs)  9.72 us
    pallas_call x2, Pallas kernels, inner(): pl.pallas_call(loading_kernel if load else inner_kernel, out_shape=(jax.S...  8.55 us
    pallas_call x1, Pallas kernels, coarse(): pl.pallas_call(functools.partial(coarse_kernel, coarse_slots), out_shape=...  6.73 us
    pallas_call x1, Pallas kernels, outer(): pl.pallas_call(outer_kernel, out_shape=jax.ShapeDtypeStruct(main.shape, B...  1.9 us
    pallas_call x1, Pallas kernels, outer_pool(): pl.pallas_call(outer_pool_kernel, out_shape=(jax.ShapeDtypeStruct(main.sh...  1.17 us
    pallas_call x1, Pallas kernels, first(): pl.pallas_call(first_kernel, out_shape=(face, face, jax.ShapeDtypeStruct(...  1.07 us
  transfers between devices with their start and end apart: 11, of which 5 were waited for; matrix products, arithmetic and copies ran while one was open for 0% of the time, Pallas kernels for 19%

profile of v2, /device:TPU:5, one launch (start us, length us, event | category | flops | bytes accessed | tf_op | source)
XLA Modules:
  0.0 44.2 jit_solution(11610031033541281559)
XLA Ops:
  0.0 1.1 %first.1 = (bf16[4,64,128]{2,1,0:T(8,128)(2,1)S(1)}, bf16[4,64,128]{2,1,0:T(8,128)(2,1)S(1)}, s32[8,128]{1,0:T(8,128)S(1)}, bf16[16,128]{1,0:T(8,128)(2,1)S(1)}) custom-call(s32[1,1]{1,0:T(1,128)} %bitcast.info, bf16[4,8,64,128]{3,2,1,0:T(8,128)(2,1)} %bitcast.15, s32[4,27]{1,0:T(4,128)} %nbr_hbm.1, s32[2,4]{1,0:T(2,128)} %bitcast.17, s32[1,4]{1,0:T(1,128)} %bitcast.18, ...), custom_call_target="tpu_custom_call" | custom-call | bytes 2097152 | tf_op jit(solution)/shard_map/first/pallas_call | solution.py:131
  1.1 0.7 %collective-permute-start = (bf16[4,64,128]{2,1,0:T(8,128)(2,1)S(1)}, bf16[4,64,128]{2,1,0:T(8,128)(2,1)S(1)}, u32[]{:S(2)}, u32[]{:S(2)}) collective-permute-start(bf16[4,64,128]{2,1,0:T(8,128)(2,1)S(1)} %get-tuple-element.20), channel_id=1, source_target_pairs={{0,1},{1,0},{2,3},{3,2},{4,5},{5,4},{6,7},{7,6},{8,9},{9,8},{10,11... | collective-permute-start | bytes 196616 | tf_op jit(solution)/shard_map/ppermute | solution.py:574
  1.8 3.0 %collective-permute-start.1 = (bf16[4,64,128]{2,1,0:T(8,128)(2,1)S(1)}, bf16[4,64,128]{2,1,0:T(8,128)(2,1)S(1)}, u32[]{:S(2)}, u32[]{:S(2)}) collective-permute-start(bf16[4,64,128]{2,1,0:T(8,128)(2,1)S(1)} %get-tuple-element.21), channel_id=1, source_target_pairs={{1,2},{2,1},{3,4},{4,3},{5,6},{6,5},{7,8},{8,7},{9,10},{10,9},{11,... | collective-permute-start | bytes 196616 | tf_op jit(solution)/shard_map/ppermute | solution.py:574
  4.9 0.0 copy-start.1
  4.9 5.0 %inner.2 = (bf16[4,8,64,128]{3,2,1,0:T(8,128)(2,1)S(1)}, f32[4,2,64,128]{3,2,1,0:T(8,128)S(1)}) custom-call(s32[8,128]{1,0:T(8,128)S(1)} %get-tuple-element.19.nbr.meta, bf16[4,8,64,128]{3,2,1,0:T(8,128)(2,1)} %bitcast.16, bf16[3456,128]{1,0:T(8,128)(2,1)} %bitcast.11), custom_call_target="tpu_custom_call" | custom-call | flops 1811939328 | bytes 4194304 | tf_op jit(solution)/shard_map/inner/pallas_call | solution.py:205
  9.9 0.0 collective-permute-done.near_ref
  9.9 0.0 collective-permute-done.1.far_ref
  9.9 0.0 copy-done.1
  9.9 0.0 copy-start.2
  9.9 0.0 copy-start.3
  10.0 1.2 %outer_pool.1 = (bf16[4,8,64,128]{3,2,1,0:T(8,128)(2,1)S(1)}, bf16[272,128]{1,0:T(8,128)(2,1)S(1)}, bf16[144,128]{1,0:T(8,128)(2,1)S(1)}) custom-call(s32[8,128]{1,0:T(8,128)S(1)} %get-tuple-element.19.nbr.meta, bf16[4,64,128]{2,1,0:T(8,128)(2,1)S(1)} %collective-permute-done.near_ref, bf16[4,64,128]{2,1,0:T(8,128)(2,1)S(1)} %collective-permute-done.1.far_ref, ...), custom_call_target="tpu_custom_call" | custom-call | flops 536870912 | bytes 4194304 | tf_op jit(solution)/shard_map/outer_pool/pallas_call | solution.py:310
  11.1 0.1 collective-permute-start.5
  11.2 1.2 %collective-permute-done.5 = bf16[144,128]{1,0:T(8,128)(2,1)S(1)} collective-permute-done((bf16[144,128]{1,0:T(8,128)(2,1)S(1)}, bf16[144,128]{1,0:T(8,128)(2,1)S(1)}, u32[]{:S(2)}, u32[]{:S(2)}) %collective-permute-start.5) | collective-permute-done | bytes 36896 | tf_op jit(solution)/shard_map/ppermute | solution.py:574
  12.4 3.2 %collective-permute-start.6 = (bf16[288,128]{1,0:T(8,128)(2,1)S(1)}, bf16[288,128]{1,0:T(8,128)(2,1)S(1)}, u32[]{:S(2)}, u32[]{:S(2)}) collective-permute-start(bf16[288,128]{1,0:T(8,128)(2,1)S(1)} %pad_maximum_fusion), channel_id=1, source_target_pairs={{1,4},{3,6},{4,1},{5,8},{6,3},{7,10},{8,5},{9,12},{10,7},{11,14},{... | collective-permute-start | bytes 221192 | tf_op jit(solution)/shard_map/ppermute | solution.py:574
  15.7 2.4 %collective-permute-done.6 = bf16[288,128]{1,0:T(8,128)(2,1)S(1)} collective-permute-done((bf16[288,128]{1,0:T(8,128)(2,1)S(1)}, bf16[288,128]{1,0:T(8,128)(2,1)S(1)}, u32[]{:S(2)}, u32[]{:S(2)}) %collective-permute-start.6) | collective-permute-done | bytes 73760 | tf_op jit(solution)/shard_map/ppermute | solution.py:574
  18.1 0.2 collective-permute-start.7
  18.3 3.0 %collective-permute-done.7 = bf16[288,128]{1,0:T(8,128)(2,1)S(1)} collective-permute-done((bf16[288,128]{1,0:T(8,128)(2,1)S(1)}, bf16[288,128]{1,0:T(8,128)(2,1)S(1)}, u32[]{:S(2)}, u32[]{:S(2)}) %collective-permute-start.7) | collective-permute-done | bytes 73760 | tf_op jit(solution)/shard_map/ppermute | solution.py:574
  21.3 0.1 collective-permute-start.8
  21.4 0.3 collective-permute-start.3
  21.7 0.7 %collective-permute-start.2 = (bf16[272,128]{1,0:T(8,128)(2,1)S(1)}, bf16[272,128]{1,0:T(8,128)(2,1)S(1)}, u32[]{:S(2)}, u32[]{:S(2)}) collective-permute-start(bf16[272,128]{1,0:T(8,128)(2,1)S(1)} %get-tuple-element.25.own_ref), channel_id=1, source_target_pairs={{0,1},{1,0},{2,3},{3,2},{4,5},{5,4},{6,7},{7,6},{8,9},{9,8},{10,11... | collective-permute-start | bytes 208904 | tf_op jit(solution)/shard_map/ppermute | solution.py:574
  22.4 2.2 %collective-permute-done.3.y_ref = bf16[272,128]{1,0:T(8,128)(2,1)S(1)} collective-permute-done((bf16[272,128]{1,0:T(8,128)(2,1)S(1)}, bf16[272,128]{1,0:T(8,128)(2,1)S(1)}, u32[]{:S(2)}, u32[]{:S(2)}) %collective-permute-start.3) | collective-permute-done | bytes 69664 | tf_op jit(solution)/shard_map/ppermute | solution.py:574
  24.6 1.6 %collective-permute-start.4 = (bf16[272,128]{1,0:T(8,128)(2,1)S(1)}, bf16[272,128]{1,0:T(8,128)(2,1)S(1)}, u32[]{:S(2)}, u32[]{:S(2)}) collective-permute-start(bf16[272,128]{1,0:T(8,128)(2,1)S(1)} %collective-permute-done.3.y_ref), channel_id=1, source_target_pairs={{0,1},{1,0},{2,3},{3,2},{4,5},{5,4},{6,7},{7,6},{8,9},{9,8},{10,11... | collective-permute-start | bytes 208904 | tf_op jit(solution)/shard_map/ppermute | solution.py:574
  26.2 0.0 collective-permute-done.2.core_ref
  26.2 0.9 %collective-permute-done.4.yc_ref = bf16[272,128]{1,0:T(8,128)(2,1)S(1)} collective-permute-done((bf16[272,128]{1,0:T(8,128)(2,1)S(1)}, bf16[272,128]{1,0:T(8,128)(2,1)S(1)}, u32[]{:S(2)}, u32[]{:S(2)}) %collective-permute-start.4) | collective-permute-done | bytes 69664 | tf_op jit(solution)/shard_map/ppermute | solution.py:574
  27.1 0.0 collective-permute-done.8.bigc_ref
  27.1 0.0 copy-done.2
  27.1 0.0 copy-done.3
  27.1 0.0 copy-start
  27.1 6.7 %coarse.1 = (bf16[4,8,64,128]{3,2,1,0:T(8,128)(2,1)S(1)}, bf16[4,64,128]{2,1,0:T(8,128)(2,1)S(1)}, bf16[4,64,128]{2,1,0:T(8,128)(2,1)S(1)}) custom-call(s32[8,128]{1,0:T(8,128)S(1)} %get-tuple-element.19.nbr.meta, bf16[272,128]{1,0:T(8,128)(2,1)S(1)} %get-tuple-element.25.own_ref, bf16[272,128]{1,0:T(8,128)(2,1)S(1)} %collective-permute-done.2.core_ref, ...), custom_call_target="tpu_custom_call" | custom-call | flops 2147483648 | bytes 8388608 | tf_op jit(solution)/shard_map/coarse/pallas_call | solution.py:531
  33.8 0.4 collective-permute-start.9
  34.3 4.5 %collective-permute-start.10 = (bf16[4,64,128]{2,1,0:T(8,128)(2,1)S(1)}, bf16[4,64,128]{2,1,0:T(8,128)(2,1)S(1)}, u32[]{:S(2)}, u32[]{:S(2)}) collective-permute-start(bf16[4,64,128]{2,1,0:T(8,128)(2,1)S(1)} %get-tuple-element.29), channel_id=1, source_target_pairs={{1,2},{2,1},{3,4},{4,3},{5,6},{6,5},{7,8},{8,7},{9,10},{10,9},{11,... | collective-permute-start | bytes 196616 | tf_op jit(solution)/shard_map/ppermute | solution.py:574
  38.7 0.0 copy-done
  38.8 3.5 %inner.3 = (bf16[4,8,64,128]{3,2,1,0:T(8,128)(2,1)S(1)}, f32[4,2,64,128]{3,2,1,0:T(8,128)S(1)}) custom-call(s32[8,128]{1,0:T(8,128)S(1)} %get-tuple-element.19.nbr.meta, bf16[4,8,64,128]{3,2,1,0:T(8,128)(2,1)S(1)} %get-tuple-element.30.x_ref, bf16[3456,128]{1,0:T(8,128)(2,1)S(1)} %bitcast.9), custom_call_target="tpu_custom_call" | custom-call | flops 1811939328 | bytes 4194304 | tf_op jit(solution)/shard_map/inner/pallas_call | solution.py:205
  42.3 0.0 collective-permute-done.9.near_ref
  42.3 0.0 collective-permute-done.10.far_ref
  42.3 1.9 %outer.1 = bf16[4,8,64,128]{3,2,1,0:T(8,128)(2,1)} custom-call(s32[8,128]{1,0:T(8,128)S(1)} %get-tuple-element.19.nbr.meta, bf16[4,64,128]{2,1,0:T(8,128)(2,1)S(1)} %collective-permute-done.9.near_ref, bf16[4,64,128]{2,1,0:T(8,128)(2,1)S(1)} %collective-permute-done.10.far_ref, f32[4,2,64,128]{3,2,1,0:T(8,128)S(1)} %get-tuple-element.31.part_ref, ...), custom_call_target="tpu_custom_call" | custom-call | flops 536870912 | bytes 4194304 | tf_op jit(solution)/shard_map/outer/pallas_call | solution.py:273
  (3 shorter events, 0.0 us)
Async XLA Ops:
  1.1 8.8 %collective-permute-start = (bf16[4,64,128]{2,1,0:T(8,128)(2,1)S(1)}, bf16[4,64,128]{2,1,0:T(8,128)(2,1)S(1)}, u32[]{:S(2)}, u32[]{:S(2)}) collective-permute-start(bf16[4,64,128]{2,1,0:T(8,128)(2,1)S(1)} %get-tuple-element.20), channel_id=1, source_target_pairs={{0,1},{1,0},{2,3},{3,2},{4,5},{5,4},{6,7},{7,6},{8,9},{9,8},{10,11... | collective-permute-start | bytes 196616 | tf_op jit(solution)/shard_map/ppermute | solution.py:574
  1.8 8.1 %collective-permute-start.1 = (bf16[4,64,128]{2,1,0:T(8,128)(2,1)S(1)}, bf16[4,64,128]{2,1,0:T(8,128)(2,1)S(1)}, u32[]{:S(2)}, u32[]{:S(2)}) collective-permute-start(bf16[4,64,128]{2,1,0:T(8,128)(2,1)S(1)} %get-tuple-element.21), channel_id=1, source_target_pairs={{1,2},{2,1},{3,4},{4,3},{5,6},{6,5},{7,8},{8,7},{9,10},{10,9},{11,... | collective-permute-start | bytes 196616 | tf_op jit(solution)/shard_map/ppermute | solution.py:574
  4.9 5.1 %copy-start.1 = (bf16[27,128,128]{2,1,0:T(8,128)(2,1)S(1)}, bf16[27,128,128]{2,1,0:T(8,128)(2,1)}, u32[]{:S(2)}) copy-start(bf16[27,128,128]{2,1,0:T(8,128)(2,1)} %param.16) | copy-start | bytes 2654212
  9.9 17.2 %copy-start.2 = (bf16[27,128,128]{2,1,0:T(8,128)(2,1)S(1)}, bf16[27,128,128]{2,1,0:T(8,128)(2,1)}, u32[]{:S(2)}) copy-start(bf16[27,128,128]{2,1,0:T(8,128)(2,1)} %param.17) | copy-start | bytes 2654212
  9.9 17.2 %copy-start.3 = (bf16[27,128,128]{2,1,0:T(8,128)(2,1)S(1)}, bf16[27,128,128]{2,1,0:T(8,128)(2,1)}, u32[]{:S(2)}) copy-start(bf16[27,128,128]{2,1,0:T(8,128)(2,1)} %param.18) | copy-start | bytes 2654212
  11.1 1.3 %collective-permute-start.5 = (bf16[144,128]{1,0:T(8,128)(2,1)S(1)}, bf16[144,128]{1,0:T(8,128)(2,1)S(1)}, u32[]{:S(2)}, u32[]{:S(2)}) collective-permute-start(bf16[144,128]{1,0:T(8,128)(2,1)S(1)} %get-tuple-element.26), channel_id=1, source_target_pairs={{0,1},{1,0},{2,3},{3,2},{4,5},{5,4},{6,7},{7,6},{8,9},{9,8},{10,11... | collective-permute-start | bytes 110600 | tf_op jit(solution)/shard_map/ppermute | solution.py:574
  12.4 5.7 %collective-permute-start.6 = (bf16[288,128]{1,0:T(8,128)(2,1)S(1)}, bf16[288,128]{1,0:T(8,128)(2,1)S(1)}, u32[]{:S(2)}, u32[]{:S(2)}) collective-permute-start(bf16[288,128]{1,0:T(8,128)(2,1)S(1)} %pad_maximum_fusion), channel_id=1, source_target_pairs={{1,4},{3,6},{4,1},{5,8},{6,3},{7,10},{8,5},{9,12},{10,7},{11,14},{... | collective-permute-start | bytes 221192 | tf_op jit(solution)/shard_map/ppermute | solution.py:574
  18.1 3.2 %collective-permute-start.7 = (bf16[288,128]{1,0:T(8,128)(2,1)S(1)}, bf16[288,128]{1,0:T(8,128)(2,1)S(1)}, u32[]{:S(2)}, u32[]{:S(2)}) collective-permute-start(bf16[288,128]{1,0:T(8,128)(2,1)S(1)} %collective-permute-done.6), channel_id=1, source_target_pairs={{0,2},{1,3},{2,0},{3,1},{4,6},{5,7},{6,4},{7,5},{8,10},{9,11},{10,... | collective-permute-start | bytes 221192 | tf_op jit(solution)/shard_map/ppermute | solution.py:574
  21.3 5.8 %collective-permute-start.8 = (bf16[576,128]{1,0:T(8,128)(2,1)S(1)}, bf16[576,128]{1,0:T(8,128)(2,1)S(1)}, u32[]{:S(2)}, u32[]{:S(2)}) collective-permute-start(bf16[576,128]{1,0:T(8,128)(2,1)S(1)} %constant_dynamic-update-slice_fusion.big_ref), channel_id=1, source_target_pairs={{0,1},{1,0},{2,3},{3,2},{4,5},{5,4},{6,7},{7,6},{8,9},{9,8},{10,11... | collective-permute-start | bytes 442376 | tf_op jit(solution)/shard_map/ppermute | solution.py:574
  21.4 3.2 %collective-permute-start.3 = (bf16[272,128]{1,0:T(8,128)(2,1)S(1)}, bf16[272,128]{1,0:T(8,128)(2,1)S(1)}, u32[]{:S(2)}, u32[]{:S(2)}) collective-permute-start(bf16[272,128]{1,0:T(8,128)(2,1)S(1)} %get-tuple-element.25.own_ref), channel_id=1, source_target_pairs={{0,2},{1,3},{2,0},{3,1},{4,6},{5,7},{6,4},{7,5},{8,10},{9,11},{10,... | collective-permute-start | bytes 208904 | tf_op jit(solution)/shard_map/ppermute | solution.py:574
  21.7 4.5 %collective-permute-start.2 = (bf16[272,128]{1,0:T(8,128)(2,1)S(1)}, bf16[272,128]{1,0:T(8,128)(2,1)S(1)}, u32[]{:S(2)}, u32[]{:S(2)}) collective-permute-start(bf16[272,128]{1,0:T(8,128)(2,1)S(1)} %get-tuple-element.25.own_ref), channel_id=1, source_target_pairs={{0,1},{1,0},{2,3},{3,2},{4,5},{5,4},{6,7},{7,6},{8,9},{9,8},{10,11... | collective-permute-start | bytes 208904 | tf_op jit(solution)/shard_map/ppermute | solution.py:574
  24.6 2.5 %collective-permute-start.4 = (bf16[272,128]{1,0:T(8,128)(2,1)S(1)}, bf16[272,128]{1,0:T(8,128)(2,1)S(1)}, u32[]{:S(2)}, u32[]{:S(2)}) collective-permute-start(bf16[272,128]{1,0:T(8,128)(2,1)S(1)} %collective-permute-done.3.y_ref), channel_id=1, source_target_pairs={{0,1},{1,0},{2,3},{3,2},{4,5},{5,4},{6,7},{7,6},{8,9},{9,8},{10,11... | collective-permute-start | bytes 208904 | tf_op jit(solution)/shard_map/ppermute | solution.py:574
  27.1 11.6 %copy-start = (bf16[27,128,128]{2,1,0:T(8,128)(2,1)S(1)}, bf16[27,128,128]{2,1,0:T(8,128)(2,1)}, u32[]{:S(2)}) copy-start(bf16[27,128,128]{2,1,0:T(8,128)(2,1)} %param.19) | copy-start | bytes 2654212
  33.8 8.5 %collective-permute-start.9 = (bf16[4,64,128]{2,1,0:T(8,128)(2,1)S(1)}, bf16[4,64,128]{2,1,0:T(8,128)(2,1)S(1)}, u32[]{:S(2)}, u32[]{:S(2)}) collective-permute-start(bf16[4,64,128]{2,1,0:T(8,128)(2,1)S(1)} %get-tuple-element.28), channel_id=1, source_target_pairs={{0,1},{1,0},{2,3},{3,2},{4,5},{5,4},{6,7},{7,6},{8,9},{9,8},{10,11... | collective-permute-start | bytes 196616 | tf_op jit(solution)/shard_map/ppermute | solution.py:574
  34.3 8.0 %collective-permute-start.10 = (bf16[4,64,128]{2,1,0:T(8,128)(2,1)S(1)}, bf16[4,64,128]{2,1,0:T(8,128)(2,1)S(1)}, u32[]{:S(2)}, u32[]{:S(2)}) collective-permute-start(bf16[4,64,128]{2,1,0:T(8,128)(2,1)S(1)} %get-tuple-element.29), channel_id=1, source_target_pairs={{1,2},{2,1},{3,4},{4,3},{5,6},{6,5},{7,8},{8,7},{9,10},{10,9},{11,... | collective-permute-start | bytes 196616 | tf_op jit(solution)/shard_map/ppermute | solution.py:574

commit v3 on v2

--- a/solution.py
+++ b/solution.py
@@ -10,7 +10,7 @@
 
 LANES = 4
 GROUP = 1
-CONV_GROUP = 4
+CONV_GROUP = 2
 TILE = 16
 OFFSETS = (-1, 0, 1)
 BF16 = jnp.bfloat16
@@ -82,8 +82,8 @@
 
 
 def first_kernel(
-    info, x_hbm, nbr_hbm, send_hbm, parent_hbm, child_hbm, around_hbm,
-    near_ref, far_ref, meta_ref, codes_ref,
+    info, x_hbm, w_hbm, nbr_hbm, send_hbm, parent_hbm, child_hbm, around_hbm,
+    near_ref, far_ref, meta_ref, codes_ref, x_ref, w_ref,
     head_v, last_v, nbr_v, send_v, parent_v, child_v, around_v, numbers, sems,
 ):
     slots, edge, _, _ = x_hbm.shape
@@ -91,10 +91,11 @@
     pairs = [(x_hbm.at[:, 0], head_v), (x_hbm.at[:, edge - 1], last_v)]
     pairs += [(nbr_hbm, nbr_v), (send_hbm, send_v), (parent_hbm, parent_v)]
     pairs += [(child_hbm, child_v), (around_hbm, around_v)]
+    pairs += [(x_hbm, x_ref), (w_hbm, w_ref)]
     copies = [pltpu.make_async_copy(*pair, sems.at[i]) for i, pair in enumerate(pairs)]
     for copy in copies:
         copy.start()
-    for copy in copies:
+    for copy in copies[:-2]:
         copy.wait()
     position = info[0, 0]
     meta_ref[...] = jnp.full(meta_ref.shape, position, jnp.int32)
@@ -117,13 +118,15 @@
         head = head_v[b].astype(F32) * listed[1:2, b : b + 1]
         near_ref[b] = jnp.where(is_odd, head, last).astype(BF16)
         far_ref[b] = jnp.where(is_odd, last, head).astype(BF16)
+    for copy in copies[-2:]:
+        copy.wait()
 
 
 def stay(value):
     return pltpu.with_memory_space_constraint(value, pltpu.HBM)
 
 
-def first(info, x, nbr, send, parent, child, around):
+def first(info, x, weights, nbr, send, parent, child, around):
     slots, _, rows, width = x.shape
     coarse_slots = child.shape[0]
     assert 2 * coarse_slots <= TILE and (LANES * slots) & (LANES * slots - 1) == 0
@@ -135,51 +138,40 @@
             face,
             jax.ShapeDtypeStruct((slots + 4, width), jnp.int32),
             jax.ShapeDtypeStruct((TILE, width), BF16),
+            jax.ShapeDtypeStruct(x.shape, BF16),
+            jax.ShapeDtypeStruct(weights.shape, BF16),
         ),
-        in_specs=[SMEM] + [HBM] * 6,
-        out_specs=(VMEM,) * 4,
+        in_specs=[SMEM] + [HBM] * 7,
+        out_specs=(VMEM,) * 6,
         scratch_shapes=[pltpu.VMEM((slots, rows, width), BF16)] * 2
         + [pltpu.VMEM(v.shape, jnp.int32) for v in (nbr, send, parent, child, around)]
-        + [pltpu.VMEM((TILE, width), jnp.int32), pltpu.SemaphoreType.DMA((7,))],
+        + [pltpu.VMEM((TILE, width), jnp.int32), pltpu.SemaphoreType.DMA((9,))],
         compiler_params=PARAMS,
         cost_estimate=pl.CostEstimate(flops=0, bytes_accessed=2097152, transcendentals=0),
         name="first",
-    )(info, *[stay(v) for v in (x, nbr, send, parent, child, around)])
-
-
-def loading_kernel(nbr, x_hbm, w_hbm, out_ref, part_ref, cols, x_ref, w_ref, sems):
-    copies = [
-        pltpu.make_async_copy(source, target, sems.at[i])
-        for i, (source, target) in enumerate(((x_hbm, x_ref), (w_hbm, w_ref)))
-    ]
-    for copy in copies:
-        copy.start()
-    copies[0].wait()
-    inner_kernel(nbr, x_ref, w_ref, out_ref, part_ref, cols, copies[1])
-
-
-def inner_kernel(nbr, x_ref, w_ref, out_ref, part_ref, cols, waiting=None):
+    )(info, *[stay(v) for v in (x, weights, nbr, send, parent, child, around)])
+
+
+def inner_kernel(nbr, x_ref, w_ref, out_ref, part_ref, cols):
     slots, edge, _, width = x_ref.shape
     pairs = edge // 2
     empty = jnp.zeros((slots, 4, 3, pairs * edge, width), BF16)
     cols[:, :, :, 0] = empty
     cols[:, :, :, edge + 1] = empty
-    for b in range(slots):
-        def fetch(dy, dz):
-            slot = nbr[b, tap(0, dy, dz)]
-            held = jnp.maximum(slot, 0)
-            value = y_rows(lambda r, n: x_ref[held, :, r : r + n, :].astype(F32), dy, edge)
-            return jnp.where(slot >= 0, value, 0.0)
-
-        for k, full in enumerate(columns(fetch, edge)):
-            for j in range(4):
-                cols[b, j, k, 1 : edge + 1] = pair_rows(full, j, pairs)
-    if waiting is not None:
-        waiting.wait()
     weights = pair_weights(w_ref, range(3), width)
     for group in range(0, slots, GROUP):
         bricks = []
         for b in range(group, group + GROUP):
+
+            def fetch(dy, dz):
+                slot = nbr[b, tap(0, dy, dz)]
+                held = jnp.maximum(slot, 0)
+                value = y_rows(lambda r, n: x_ref[held, :, r : r + n, :].astype(F32), dy, edge)
+                return jnp.where(slot >= 0, value, 0.0)
+
+            for k, full in enumerate(columns(fetch, edge)):
+                for j in range(4):
+                    cols[b, j, k, 1 : edge + 1] = pair_rows(full, j, pairs)
             taps = []
             for dx in range(3):
                 for j in range(4):
@@ -200,21 +192,19 @@
             part_ref[b, 1] = total[edge - 1]
 
 
-def inner(x, nbr, weights, load=False):
+def inner(x, nbr, weights):
     slots, edge, rows, width = x.shape
     return pl.pallas_call(
-        loading_kernel if load else inner_kernel,
+        inner_kernel,
         out_shape=(
             jax.ShapeDtypeStruct(x.shape, BF16),
             jax.ShapeDtypeStruct((slots, 2, rows, width), F32),
         ),
-        in_specs=[SMEM] + [HBM if load else VMEM] * 2,
+        in_specs=[SMEM, VMEM, VMEM],
         out_specs=(VMEM, VMEM),
         scratch_shapes=[
             pltpu.VMEM((slots, 4, 3, edge + 2, rows // 2, width), BF16),
-        ]
-        + load
-        * [pltpu.VMEM(x.shape, BF16), pltpu.VMEM(weights.shape, BF16), pltpu.SemaphoreType.DMA((2,))],
+        ],
         compiler_params=PARAMS,
         cost_estimate=pl.CostEstimate(
             flops=2 * slots * edge * rows * 27 * width * width,
@@ -222,12 +212,11 @@
             transcendentals=0,
         ),
         name="inner",
-    )(nbr, *([stay(x), stay(weights)] if load else [x, weights]))
-
-
-def outer_planes(nbr, near_ref, far_ref, part_ref, w_ref, out_ref):
+    )(nbr, x, weights)
+
+
+def outer_planes(nbr, near_ref, far_ref, part_ref, w_ref, out_ref, edge):
     slots, _, rows, width = part_ref.shape
-    edge = out_ref.shape[1]
     pairs = edge // 2
     is_odd = (nbr[slots + 3, 0] & 1) == 1
     for side, dx in enumerate((-1, 1)):
@@ -264,9 +253,19 @@
             out_ref[b, plane] = jnp.maximum(total, 0.0).astype(BF16)
 
 
-def outer_kernel(nbr, near_ref, far_ref, part_ref, w_ref, main_ref, out_ref):
-    out_ref[:, 1 : out_ref.shape[1] - 1] = main_ref[:, 1 : out_ref.shape[1] - 1]
-    outer_planes(nbr, near_ref, far_ref, part_ref, w_ref, out_ref)
+def outer_kernel(nbr, near_ref, far_ref, part_ref, w_ref, main_ref, out_hbm, planes, sems):
+    edge = main_ref.shape[1]
+    inside = pltpu.make_async_copy(main_ref.at[:, 1 : edge - 1], out_hbm.at[:, 1 : edge - 1], sems.at[0])
+    inside.start()
+    outer_planes(nbr, near_ref, far_ref, part_ref, w_ref, planes, edge)
+    copies = [
+        pltpu.make_async_copy(planes.at[:, i], out_hbm.at[:, x], sems.at[i + 1])
+        for i, x in enumerate((0, edge - 1))
+    ]
+    for copy in copies:
+        copy.start()
+    for copy in copies + [inside]:
+        copy.wait()
 
 
 def outer(main, part, near, far, nbr, weights):
@@ -274,7 +273,8 @@
         outer_kernel,
         out_shape=jax.ShapeDtypeStruct(main.shape, BF16),
         in_specs=[SMEM, VMEM, VMEM, VMEM, VMEM, VMEM],
-        out_specs=VMEM,
+        out_specs=HBM,
+        scratch_shapes=[pltpu.VMEM(part.shape, BF16), pltpu.SemaphoreType.DMA((3,))],
         compiler_params=PARAMS,
         cost_estimate=pl.CostEstimate(flops=536870912, bytes_accessed=4194304, transcendentals=0),
         name="outer",
@@ -287,7 +287,7 @@
     slots, edge, _, width = out_ref.shape
     half = edge // 2
     out_ref[:, 1 : edge - 1] = main_ref[:, 1 : edge - 1]
-    outer_planes(nbr, near_ref, far_ref, part_ref, w_ref, out_ref)
+    outer_planes(nbr, near_ref, far_ref, part_ref, w_ref, out_ref, edge)
     cells = half**3
     pool_ref[slots * cells :] = code_ref[...]
     rim_ref[slots * cells // 2 :] = code_ref[...]
@@ -321,15 +321,6 @@
         cost_estimate=pl.CostEstimate(flops=536870912, bytes_accessed=4194304, transcendentals=0),
         name="outer_pool",
     )(nbr, near, far, part, weights, main, codes)
-
-
-def source_row(rel, device, lane_y, lane_c):
-    c = device & 1
-    flip_y = ((device >> 1) & 1) ^ lane_y
-    same = flip_y * 2 + (c ^ lane_c)
-    below = 4 + 4 * lane_c + flip_y * 2 + (1 - c)
-    above = 8 - 4 * lane_c + flip_y * 2 + c
-    return jnp.where(rel == 0, same, jnp.where(rel < 0, below, above))
 
 
 def x_pair_weights(w_ref, width):
@@ -381,33 +372,52 @@
 
 def coarse_kernel(
     coarse_slots, meta, own_ref, core_ref, y_ref, yc_ref, big_ref, bigc_ref, enc_ref, w1_ref, w2_ref,
-    out_ref, near_ref, far_ref, held, codes, even, odd, even2, odd2, spread, table, row_s, there_s, sem,
+    out_ref, near_ref, far_ref, held, codes, even, odd, even2, odd2, spread, table, code_s, part_s, sem,
 ):
     slots, edge, rows, width = enc_ref.shape
     half = edge // 2
     plane = half * half
     cells = half * plane
     position = meta[slots + 3, 0]
-    lane_y = (position >> 1) & 1
+    lane = position & (LANES - 1)
+    group_bits = (LANES * coarse_slots).bit_length() - 1
     lane_c = position & 1
     whole_rows = slots * cells
     rim_rows = whole_rows // 2
+    section = (LANES * slots + 1) * cells
     rim_at = [i * (rim_rows + TILE) for i in range(4)]
     places = [(ref, 0, whole_rows) for ref in (own_ref, core_ref, y_ref, yc_ref)]
     places += [(ref, at, rim_rows) for ref in (big_ref, bigc_ref) for at in rim_at]
-    lines = 2 * coarse_slots
-    for i, (ref, at, count) in enumerate(places):
-        line = ref[at + count : at + count + TILE].astype(F32)[:lines]
-        codes[i * lines : (i + 1) * lines] = line.astype(jnp.int32)
+    origins = [LANES + (lane ^ i) for i in range(LANES)]
+    near_rel = jnp.where(lane_c == 1, 2 * LANES, 0)
+    far_rel = 2 * LANES - near_rel
+    origins += [near_rel + (lane ^ 1 ^ i) for i in range(LANES)]
+    origins += [far_rel + (lane ^ i) for i in range(LANES)]
+    lines = 3 * LANES * coarse_slots + 1
+    codes[...] = jnp.zeros_like(codes)
+    for origin, (ref, at, count) in zip(origins, places):
+        line = ref[at + count : at + count + TILE].astype(F32).astype(jnp.int32)
+        row = 1 + origin * coarse_slots
+        codes[pl.ds(row, coarse_slots)] = line[:coarse_slots]
+        codes[pl.ds(lines + row, coarse_slots)] = line[coarse_slots : 2 * coarse_slots]
     copy = pltpu.make_async_copy(codes, table, sem)
     copy.start()
-    first = 0
-    for ref, at, count in places:
-        held[first : first + count] = ref[at : at + count]
-        first += count
-    zero_row = first
-    held[zero_row:] = jnp.zeros((cells, width), BF16)
-    full_rows = LANES * whole_rows
+    for i in range(4):
+        held[i * section : i * section + cells] = jnp.zeros((cells, width), BF16)
+    for i, (origin, (ref, at, count)) in enumerate(zip(origins, places)):
+        if i < LANES:
+            start = section + cells + origin * whole_rows
+            start = pl.multiple_of(start + section - LANES * whole_rows, TILE)
+            held[pl.ds(start, count)] = ref[at : at + count]
+        else:
+            group_start = jnp.where(origin >= LANES, 3 * section - 2 * LANES * whole_rows, section)
+            start = group_start + cells + origin * whole_rows
+            value = ref[at : at + count].reshape(slots, 1, cells // 2, width)
+            start = pl.multiple_of(start, TILE)
+            held[pl.ds(start, whole_rows)] = jnp.concatenate([value, value], axis=1).reshape(
+                whole_rows, width
+            )
+    group_first = (position >> 2) * LANES * coarse_slots
     copy.wait()
 
     row_of = lax.broadcasted_iota(jnp.int32, (1, edge, width), 1)
@@ -416,51 +426,27 @@
     regions = []
     masks = []
     for b in range(slots):
-        own = meta[slots + 2, b]
-        known = own >= 0
-        own = jnp.maximum(own, 0)
+        own = jnp.where(meta[slots + 2, b] >= 0, meta[slots + 2, b], group_first * 8)
         octant = own & 7
-        brick = own >> 3
         bits = ((octant >> 2) & 1, (octant >> 1) & 1, octant & 1)
-        home = source_row(0, brick // coarse_slots, lane_y, lane_c)
-        home_slot = brick % coarse_slots
-        sign = tuple(2 * bit - 1 for bit in bits)
-        for cross in range(8):
-            crossed = (cross >> 2, (cross >> 1) & 1, cross & 1)
-            number = 13
-            for scale, s, c in zip((9, 3, 1), sign, crossed):
-                if c:
-                    number = number + scale * s
-            found = table[home * lines + coarse_slots + home_slot, number] - 1
-            there = known & (found >= 0)
-            there_s[b, cross] = jnp.where(there, 1, 0)
-            found = jnp.maximum(found, 0)
-            rel = found // (LANES * coarse_slots) - 1
-            lane = found // coarse_slots % LANES
-            start = found % coarse_slots
-            row = source_row(rel, lane, lane_y, lane_c)
-            row_s[b, cross] = jnp.where(there, (rel + 1) * 65536 + row * lines + start, -1)
+        home = lines + 1 + LANES * coarse_slots + (own >> 3) - group_first
+        steps = [scale * (2 * bit - 1) for scale, bit in zip((9, 3, 1), bits)]
+        numbers = [13, 13 + steps[2]]
+        numbers += [number + steps[1] for number in numbers]
+        numbers += [number + steps[0] for number in numbers]
+        for cross, number in enumerate(numbers):
+            found = table[home, number]
+            code_s[b, cross] = found
+            part_s[b, cross] = ((found + LANES * coarse_slots - 1) >> group_bits) * section
+        turns = [octant ^ flip for flip in range(8)]
+        across = [{0: 0, 1: scale * bit, -1: scale * (1 - bit)} for scale, bit in zip((4, 2, 1), bits)]
 
         def base_of(ex, ey, ez):
-            cross = 0
-            flip = 0
-            for scale, bit, e in zip((4, 2, 1), bits, (ex, ey, ez)):
-                if e:
-                    cross = cross + scale * (bit if e > 0 else 1 - bit)
-                    flip += scale
-            entry = row_s[b, cross]
-            there = entry >= 0
-            entry = jnp.maximum(entry, 0)
-            rel = (entry >> 16) - 1
-            child = table[entry & 65535, octant ^ flip] - 1
-            valid = there & (child >= 0)
-            child = jnp.maximum(child, 0)
-            source = source_row(rel, child // slots, lane_y, lane_c)
-            slot = child % slots
-            whole = (source * slots + slot) * cells + (2 * plane if ex < 0 else 0)
-            rim = full_rows + ((source - LANES) * slots + slot) * (cells // 2)
-            base = jnp.where(rel == 0, whole, rim)
-            return pl.multiple_of(jnp.where(valid, base, zero_row), TILE)
+            flip = 4 * abs(ex) + 2 * abs(ey) + abs(ez)
+            cross = across[0][ex] + across[1][ey] + across[2][ez]
+            child = table[code_s[b, cross], turns[flip]]
+            base = part_s[b, cross] + child * cells
+            return pl.multiple_of(base + (2 * plane if ex < 0 else 0), TILE)
 
         x_parts = []
         for ex in OFFSETS:
@@ -488,11 +474,9 @@
         kinds = []
         for ex in OFFSETS:
             for ey in OFFSETS:
-                cross = 0
-                for scale, bit, e in zip((4, 2), bits, (ex, ey)):
-                    if e:
-                        cross = cross + scale * (bit if e > 0 else 1 - bit)
-                kinds.append(jnp.where(row_of == at_edge, there_s[b, cross + 1], there_s[b, cross]) == 1)
+                cross = across[0][ex] + across[1][ey]
+                there = jnp.where(row_of == at_edge, code_s[b, cross + 1], code_s[b, cross])
+                kinds.append(there > 0)
         masks.append(kinds)
 
     mids = []
@@ -526,7 +510,9 @@
     slots, edge, rows, width = enc.shape
     half = edge // 2
     inside = edge - 2
-    total = 2 * LANES * slots * half**3 + half**3
+    total = 4 * (LANES * slots + 1) * half**3
+    assert LANES * coarse_slots & (LANES * coarse_slots - 1) == 0
+    lines = 2 * (3 * LANES * coarse_slots + 1)
     face = jax.ShapeDtypeStruct((slots, rows, width), BF16)
     return pl.pallas_call(
         functools.partial(coarse_kernel, coarse_slots),
@@ -535,13 +521,13 @@
         out_specs=(VMEM, VMEM, VMEM),
         scratch_shapes=[
             pltpu.VMEM((total, width), BF16),
-            pltpu.VMEM((3 * LANES * 2 * coarse_slots, width), jnp.int32),
+            pltpu.VMEM((lines, width), jnp.int32),
             pltpu.VMEM((slots, 3, edge, edge * edge, width), BF16),
             pltpu.VMEM((slots, 3, edge, inside * edge, width), BF16),
             pltpu.VMEM((slots, 3, inside, inside * edge, width), BF16),
             pltpu.VMEM((slots, 3, inside, half * edge, width), BF16),
             pltpu.VMEM((slots, 2 * half * half * edge, width), F32),
-            pltpu.SMEM((3 * LANES * 2 * coarse_slots, width), jnp.int32),
+            pltpu.SMEM((lines, width), jnp.int32),
             pltpu.SMEM((slots, 8), jnp.int32),
             pltpu.SMEM((slots, 8), jnp.int32),
             pltpu.SemaphoreType.DMA,
@@ -588,13 +574,13 @@
     x = features.reshape(slots, edge, edge * edge, width)
     flat = [w.reshape(27 * width, width) for w in (enc_fine_w, enc_coarse_w, dec_coarse_w, dec_fine_w)]
     info = position.astype(jnp.int32).reshape(1, 1)
-    near, far, meta, codes = first(
-        info, x, fine_nbr, fine_send[0], fine_parent.reshape(1, slots), coarse_child, coarse_nbr
+    near, far, meta, codes, x, first_w = first(
+        info, x, flat[0], fine_nbr, fine_send[0], fine_parent.reshape(1, slots), coarse_child, coarse_nbr
     )
     far = next_chip(far)
     near = core(near)
-    main, part = inner(x, meta, flat[0], load=True)
-    enc, pooled, rim = outer_pool(main, part, near, far, meta, flat[0], codes)
+    main, part = inner(x, meta, first_w)
+    enc, pooled, rim = outer_pool(main, part, near, far, meta, first_w, codes)
 
     rim_c = core(rim)
     rim_z = across_z(jnp.concatenate([rim, rim_c], axis=0))

time: 44.4 us -> 40.9 us (0.921)
  Pallas kernels: 19.4 us -> 15.9 us
    pallas_call x1, Pallas kernels: 6.73 us -> 4.5 us  [coarse(): pl.pallas_call(functools.partial(coarse_kernel, coarse_slots), out_shape=...]
    pallas_call x2, Pallas kernels: 8.55 us -> 6.97 us  [inner(): pl.pallas_call(inner_kernel, out_shape=(jax.ShapeDtypeStruct(x.shape, BF1...]
    pallas_call x1, Pallas kernels: 1.07 us -> 1.56 us  [first(): pl.pallas_call(first_kernel, out_shape=(face, face, jax.ShapeDtypeStruct(...]
  transfers between devices with their start and end apart: 11 -> 11, of which waited for: 5 -> 5; matrix products, arithmetic and copies ran while one was open for 0% -> 0% of each run, Pallas kernels for 19% -> 17%
where the time goes in v3:
time: 40.9 us; the launch traced here: 40.7 us
  Pallas kernels  15.9 us (39%)
  starting transfers between devices  14.9 us (36%)
  waiting for transfers between devices  9.72 us (24%)
    ppermute x11, starting transfers between devices, swap(): return lax.ppermute(value, 'gx', pairs)  14.9 us
    ppermute x11, waiting for transfers between devices, swap(): return lax.ppermute(value, 'gx', pairs)  9.72 us
    pallas_call x2, Pallas kernels, inner(): pl.pallas_call(inner_kernel, out_shape=(jax.ShapeDtypeStruct(x.shape, BF1...  6.97 us
    pallas_call x1, Pallas kernels, coarse(): pl.pallas_call(functools.partial(coarse_kernel, coarse_slots), out_shape=...  4.5 us
    pallas_call x1, Pallas kernels, outer(): pl.pallas_call(outer_kernel, out_shape=jax.ShapeDtypeStruct(main.shape, B...  1.79 us
    pallas_call x1, Pallas kernels, first(): pl.pallas_call(first_kernel, out_shape=(face, face, jax.ShapeDtypeStruct(...  1.56 us
    pallas_call x1, Pallas kernels, outer_pool(): pl.pallas_call(outer_pool_kernel, out_shape=(jax.ShapeDtypeStruct(main.sh...  1.12 us
  transfers between devices with their start and end apart: 11, of which 5 were waited for; matrix products, arithmetic and copies ran while one was open for 0% of the time, Pallas kernels for 17%

profile of v3, /device:TPU:5, one launch (start us, length us, event | category | flops | bytes accessed | tf_op | source)
XLA Modules:
  0.0 40.7 jit_solution(5385435231391989774)
XLA Ops:
  0.0 1.6 %first.1 = (bf16[4,64,128]{2,1,0:T(8,128)(2,1)S(1)}, bf16[4,64,128]{2,1,0:T(8,128)(2,1)S(1)}, s32[8,128]{1,0:T(8,128)S(1)}, bf16[16,128]{1,0:T(8,128)(2,1)S(1)},...) custom-call(s32[1,1]{1,0:T(1,128)} %bitcast.info, bf16[4,8,64,128]{3,2,1,0:T(8,128)(2,1)} %bitcast.14, ...), custom_call_target="tpu_custom_call" | custom-call | bytes 2097152 | tf_op jit(solution)/shard_map/first/pallas_call | solution.py:134
  1.6 0.7 %collective-permute-start = (bf16[4,64,128]{2,1,0:T(8,128)(2,1)S(1)}, bf16[4,64,128]{2,1,0:T(8,128)(2,1)S(1)}, u32[]{:S(2)}, u32[]{:S(2)}) collective-permute-start(bf16[4,64,128]{2,1,0:T(8,128)(2,1)S(1)} %get-tuple-element.22), channel_id=1, source_target_pairs={{0,1},{1,0},{2,3},{3,2},{4,5},{5,4},{6,7},{7,6},{8,9},{9,8},{10,11... | collective-permute-start | bytes 196616 | tf_op jit(solution)/shard_map/ppermute | solution.py:560
  2.3 3.0 %collective-permute-start.1 = (bf16[4,64,128]{2,1,0:T(8,128)(2,1)S(1)}, bf16[4,64,128]{2,1,0:T(8,128)(2,1)S(1)}, u32[]{:S(2)}, u32[]{:S(2)}) collective-permute-start(bf16[4,64,128]{2,1,0:T(8,128)(2,1)S(1)} %get-tuple-element.23), channel_id=1, source_target_pairs={{1,2},{2,1},{3,4},{4,3},{5,6},{6,5},{7,8},{8,7},{9,10},{10,9},{11,... | collective-permute-start | bytes 196616 | tf_op jit(solution)/shard_map/ppermute | solution.py:560
  5.4 3.4 %inner.2 = (bf16[4,8,64,128]{3,2,1,0:T(8,128)(2,1)S(1)}, f32[4,2,64,128]{3,2,1,0:T(8,128)S(1)}) custom-call(s32[8,128]{1,0:T(8,128)S(1)} %get-tuple-element.21.nbr.meta, bf16[4,8,64,128]{3,2,1,0:T(8,128)(2,1)S(1)} %get-tuple-element.24.x_ref, bf16[3456,128]{1,0:T(8,128)(2,1)S(1)} %get-tuple-element.25.w_ref), custom_call_target="tpu_custom_call" | custom-call | flops 1811939328 | bytes 4194304 | tf_op jit(solution)/shard_map/inner/pallas_call | solution.py:197
  8.8 0.0 collective-permute-done.near_ref
  8.8 0.0 collective-permute-done.1.far_ref
  8.8 0.0 copy-start.1
  8.8 0.0 copy-start.2
  8.8 1.1 %outer_pool.1 = (bf16[4,8,64,128]{3,2,1,0:T(8,128)(2,1)S(1)}, bf16[272,128]{1,0:T(8,128)(2,1)S(1)}, bf16[144,128]{1,0:T(8,128)(2,1)S(1)}) custom-call(s32[8,128]{1,0:T(8,128)S(1)} %get-tuple-element.21.nbr.meta, bf16[4,64,128]{2,1,0:T(8,128)(2,1)S(1)} %collective-permute-done.near_ref, bf16[4,64,128]{2,1,0:T(8,128)(2,1)S(1)} %collective-permute-done.1.far_ref, ...), custom_call_target="tpu_custom_call" | custom-call | flops 536870912 | bytes 4194304 | tf_op jit(solution)/shard_map/outer_pool/pallas_call | solution.py:310
  10.0 0.1 collective-permute-start.5
  10.0 1.2 %collective-permute-done.5 = bf16[144,128]{1,0:T(8,128)(2,1)S(1)} collective-permute-done((bf16[144,128]{1,0:T(8,128)(2,1)S(1)}, bf16[144,128]{1,0:T(8,128)(2,1)S(1)}, u32[]{:S(2)}, u32[]{:S(2)}) %collective-permute-start.5) | collective-permute-done | bytes 36896 | tf_op jit(solution)/shard_map/ppermute | solution.py:560
  11.3 3.2 %collective-permute-start.6 = (bf16[288,128]{1,0:T(8,128)(2,1)S(1)}, bf16[288,128]{1,0:T(8,128)(2,1)S(1)}, u32[]{:S(2)}, u32[]{:S(2)}) collective-permute-start(bf16[288,128]{1,0:T(8,128)(2,1)S(1)} %pad_maximum_fusion), channel_id=1, source_target_pairs={{1,4},{3,6},{4,1},{5,8},{6,3},{7,10},{8,5},{9,12},{10,7},{11,14},{... | collective-permute-start | bytes 221192 | tf_op jit(solution)/shard_map/ppermute | solution.py:560
  14.5 2.4 %collective-permute-done.6 = bf16[288,128]{1,0:T(8,128)(2,1)S(1)} collective-permute-done((bf16[288,128]{1,0:T(8,128)(2,1)S(1)}, bf16[288,128]{1,0:T(8,128)(2,1)S(1)}, u32[]{:S(2)}, u32[]{:S(2)}) %collective-permute-start.6) | collective-permute-done | bytes 73760 | tf_op jit(solution)/shard_map/ppermute | solution.py:560
  16.9 0.2 collective-permute-start.7
  17.1 3.0 %collective-permute-done.7 = bf16[288,128]{1,0:T(8,128)(2,1)S(1)} collective-permute-done((bf16[288,128]{1,0:T(8,128)(2,1)S(1)}, bf16[288,128]{1,0:T(8,128)(2,1)S(1)}, u32[]{:S(2)}, u32[]{:S(2)}) %collective-permute-start.7) | collective-permute-done | bytes 73760 | tf_op jit(solution)/shard_map/ppermute | solution.py:560
  20.1 0.1 collective-permute-start.8
  20.2 0.3 collective-permute-start.3
  20.5 0.7 %collective-permute-start.2 = (bf16[272,128]{1,0:T(8,128)(2,1)S(1)}, bf16[272,128]{1,0:T(8,128)(2,1)S(1)}, u32[]{:S(2)}, u32[]{:S(2)}) collective-permute-start(bf16[272,128]{1,0:T(8,128)(2,1)S(1)} %get-tuple-element.29.own_ref), channel_id=1, source_target_pairs={{0,1},{1,0},{2,3},{3,2},{4,5},{5,4},{6,7},{7,6},{8,9},{9,8},{10,11... | collective-permute-start | bytes 208904 | tf_op jit(solution)/shard_map/ppermute | solution.py:560
  21.2 2.2 %collective-permute-done.3.y_ref = bf16[272,128]{1,0:T(8,128)(2,1)S(1)} collective-permute-done((bf16[272,128]{1,0:T(8,128)(2,1)S(1)}, bf16[272,128]{1,0:T(8,128)(2,1)S(1)}, u32[]{:S(2)}, u32[]{:S(2)}) %collective-permute-start.3) | collective-permute-done | bytes 69664 | tf_op jit(solution)/shard_map/ppermute | solution.py:560
  23.4 1.6 %collective-permute-start.4 = (bf16[272,128]{1,0:T(8,128)(2,1)S(1)}, bf16[272,128]{1,0:T(8,128)(2,1)S(1)}, u32[]{:S(2)}, u32[]{:S(2)}) collective-permute-start(bf16[272,128]{1,0:T(8,128)(2,1)S(1)} %collective-permute-done.3.y_ref), channel_id=1, source_target_pairs={{0,1},{1,0},{2,3},{3,2},{4,5},{5,4},{6,7},{7,6},{8,9},{9,8},{10,11... | collective-permute-start | bytes 208904 | tf_op jit(solution)/shard_map/ppermute | solution.py:560
  25.0 0.0 collective-permute-done.2.core_ref
  25.0 0.9 %collective-permute-done.4.yc_ref = bf16[272,128]{1,0:T(8,128)(2,1)S(1)} collective-permute-done((bf16[272,128]{1,0:T(8,128)(2,1)S(1)}, bf16[272,128]{1,0:T(8,128)(2,1)S(1)}, u32[]{:S(2)}, u32[]{:S(2)}) %collective-permute-start.4) | collective-permute-done | bytes 69664 | tf_op jit(solution)/shard_map/ppermute | solution.py:560
  25.9 0.0 collective-permute-done.8.bigc_ref
  25.9 0.0 copy-done.1
  25.9 0.0 copy-done.2
  25.9 0.0 copy-start
  25.9 4.5 %coarse.1 = (bf16[4,8,64,128]{3,2,1,0:T(8,128)(2,1)S(1)}, bf16[4,64,128]{2,1,0:T(8,128)(2,1)S(1)}, bf16[4,64,128]{2,1,0:T(8,128)(2,1)S(1)}) custom-call(s32[8,128]{1,0:T(8,128)S(1)} %get-tuple-element.21.nbr.meta, bf16[272,128]{1,0:T(8,128)(2,1)S(1)} %get-tuple-element.29.own_ref, bf16[272,128]{1,0:T(8,128)(2,1)S(1)} %collective-permute-done.2.core_ref, ...), custom_call_target="tpu_custom_call" | custom-call | flops 2147483648 | bytes 8388608 | tf_op jit(solution)/shard_map/coarse/pallas_call | solution.py:517
  30.4 0.4 %collective-permute-start.9 = (bf16[4,64,128]{2,1,0:T(8,128)(2,1)S(1)}, bf16[4,64,128]{2,1,0:T(8,128)(2,1)S(1)}, u32[]{:S(2)}, u32[]{:S(2)}) collective-permute-start(bf16[4,64,128]{2,1,0:T(8,128)(2,1)S(1)} %get-tuple-element.32), channel_id=1, source_target_pairs={{0,1},{1,0},{2,3},{3,2},{4,5},{5,4},{6,7},{7,6},{8,9},{9,8},{10,11... | collective-permute-start | bytes 196616 | tf_op jit(solution)/shard_map/ppermute | solution.py:560
  30.9 4.5 %collective-permute-start.10 = (bf16[4,64,128]{2,1,0:T(8,128)(2,1)S(1)}, bf16[4,64,128]{2,1,0:T(8,128)(2,1)S(1)}, u32[]{:S(2)}, u32[]{:S(2)}) collective-permute-start(bf16[4,64,128]{2,1,0:T(8,128)(2,1)S(1)} %get-tuple-element.33), channel_id=1, source_target_pairs={{1,2},{2,1},{3,4},{4,3},{5,6},{6,5},{7,8},{8,7},{9,10},{10,9},{11,... | collective-permute-start | bytes 196616 | tf_op jit(solution)/shard_map/ppermute | solution.py:560
  35.4 0.0 copy-done
  35.4 3.5 %inner.3 = (bf16[4,8,64,128]{3,2,1,0:T(8,128)(2,1)S(1)}, f32[4,2,64,128]{3,2,1,0:T(8,128)S(1)}) custom-call(s32[8,128]{1,0:T(8,128)S(1)} %get-tuple-element.21.nbr.meta, bf16[4,8,64,128]{3,2,1,0:T(8,128)(2,1)S(1)} %get-tuple-element.34.x_ref, bf16[3456,128]{1,0:T(8,128)(2,1)S(1)} %bitcast.9), custom_call_target="tpu_custom_call" | custom-call | flops 1811939328 | bytes 4194304 | tf_op jit(solution)/shard_map/inner/pallas_call | solution.py:197
  38.9 0.0 collective-permute-done.9.near_ref
  38.9 0.0 collective-permute-done.10.far_ref
  38.9 1.8 %outer.1 = bf16[4,8,64,128]{3,2,1,0:T(8,128)(2,1)} custom-call(s32[8,128]{1,0:T(8,128)S(1)} %get-tuple-element.21.nbr.meta, bf16[4,64,128]{2,1,0:T(8,128)(2,1)S(1)} %collective-permute-done.9.near_ref, bf16[4,64,128]{2,1,0:T(8,128)(2,1)S(1)} %collective-permute-done.10.far_ref, f32[4,2,64,128]{3,2,1,0:T(8,128)S(1)} %get-tuple-element.35.part_ref, ...), custom_call_target="tpu_custom_call" | custom-call | flops 536870912 | bytes 4194304 | tf_op jit(solution)/shard_map/outer/pallas_call | solution.py:272
  (3 shorter events, 0.0 us)
Async XLA Ops:
  1.6 7.2 %collective-permute-start = (bf16[4,64,128]{2,1,0:T(8,128)(2,1)S(1)}, bf16[4,64,128]{2,1,0:T(8,128)(2,1)S(1)}, u32[]{:S(2)}, u32[]{:S(2)}) collective-permute-start(bf16[4,64,128]{2,1,0:T(8,128)(2,1)S(1)} %get-tuple-element.22), channel_id=1, source_target_pairs={{0,1},{1,0},{2,3},{3,2},{4,5},{5,4},{6,7},{7,6},{8,9},{9,8},{10,11... | collective-permute-start | bytes 196616 | tf_op jit(solution)/shard_map/ppermute | solution.py:560
  2.3 6.5 %collective-permute-start.1 = (bf16[4,64,128]{2,1,0:T(8,128)(2,1)S(1)}, bf16[4,64,128]{2,1,0:T(8,128)(2,1)S(1)}, u32[]{:S(2)}, u32[]{:S(2)}) collective-permute-start(bf16[4,64,128]{2,1,0:T(8,128)(2,1)S(1)} %get-tuple-element.23), channel_id=1, source_target_pairs={{1,2},{2,1},{3,4},{4,3},{5,6},{6,5},{7,8},{8,7},{9,10},{10,9},{11,... | collective-permute-start | bytes 196616 | tf_op jit(solution)/shard_map/ppermute | solution.py:560
  8.8 17.1 %copy-start.1 = (bf16[27,128,128]{2,1,0:T(8,128)(2,1)S(1)}, bf16[27,128,128]{2,1,0:T(8,128)(2,1)}, u32[]{:S(2)}) copy-start(bf16[27,128,128]{2,1,0:T(8,128)(2,1)} %param.17) | copy-start | bytes 2654212
  8.8 17.1 %copy-start.2 = (bf16[27,128,128]{2,1,0:T(8,128)(2,1)S(1)}, bf16[27,128,128]{2,1,0:T(8,128)(2,1)}, u32[]{:S(2)}) copy-start(bf16[27,128,128]{2,1,0:T(8,128)(2,1)} %param.18) | copy-start | bytes 2654212
  10.0 1.3 %collective-permute-start.5 = (bf16[144,128]{1,0:T(8,128)(2,1)S(1)}, bf16[144,128]{1,0:T(8,128)(2,1)S(1)}, u32[]{:S(2)}, u32[]{:S(2)}) collective-permute-start(bf16[144,128]{1,0:T(8,128)(2,1)S(1)} %get-tuple-element.30), channel_id=1, source_target_pairs={{0,1},{1,0},{2,3},{3,2},{4,5},{5,4},{6,7},{7,6},{8,9},{9,8},{10,11... | collective-permute-start | bytes 110600 | tf_op jit(solution)/shard_map/ppermute | solution.py:560
  11.3 5.7 %collective-permute-start.6 = (bf16[288,128]{1,0:T(8,128)(2,1)S(1)}, bf16[288,128]{1,0:T(8,128)(2,1)S(1)}, u32[]{:S(2)}, u32[]{:S(2)}) collective-permute-start(bf16[288,128]{1,0:T(8,128)(2,1)S(1)} %pad_maximum_fusion), channel_id=1, source_target_pairs={{1,4},{3,6},{4,1},{5,8},{6,3},{7,10},{8,5},{9,12},{10,7},{11,14},{... | collective-permute-start | bytes 221192 | tf_op jit(solution)/shard_map/ppermute | solution.py:560
  16.9 3.2 %collective-permute-start.7 = (bf16[288,128]{1,0:T(8,128)(2,1)S(1)}, bf16[288,128]{1,0:T(8,128)(2,1)S(1)}, u32[]{:S(2)}, u32[]{:S(2)}) collective-permute-start(bf16[288,128]{1,0:T(8,128)(2,1)S(1)} %collective-permute-done.6), channel_id=1, source_target_pairs={{0,2},{1,3},{2,0},{3,1},{4,6},{5,7},{6,4},{7,5},{8,10},{9,11},{10,... | collective-permute-start | bytes 221192 | tf_op jit(solution)/shard_map/ppermute | solution.py:560
  20.1 5.8 %collective-permute-start.8 = (bf16[576,128]{1,0:T(8,128)(2,1)S(1)}, bf16[576,128]{1,0:T(8,128)(2,1)S(1)}, u32[]{:S(2)}, u32[]{:S(2)}) collective-permute-start(bf16[576,128]{1,0:T(8,128)(2,1)S(1)} %constant_dynamic-update-slice_fusion.big_ref), channel_id=1, source_target_pairs={{0,1},{1,0},{2,3},{3,2},{4,5},{5,4},{6,7},{7,6},{8,9},{9,8},{10,11... | collective-permute-start | bytes 442376 | tf_op jit(solution)/shard_map/ppermute | solution.py:560
  20.2 3.2 %collective-permute-start.3 = (bf16[272,128]{1,0:T(8,128)(2,1)S(1)}, bf16[272,128]{1,0:T(8,128)(2,1)S(1)}, u32[]{:S(2)}, u32[]{:S(2)}) collective-permute-start(bf16[272,128]{1,0:T(8,128)(2,1)S(1)} %get-tuple-element.29.own_ref), channel_id=1, source_target_pairs={{0,2},{1,3},{2,0},{3,1},{4,6},{5,7},{6,4},{7,5},{8,10},{9,11},{10,... | collective-permute-start | bytes 208904 | tf_op jit(solution)/shard_map/ppermute | solution.py:560
  20.5 4.5 %collective-permute-start.2 = (bf16[272,128]{1,0:T(8,128)(2,1)S(1)}, bf16[272,128]{1,0:T(8,128)(2,1)S(1)}, u32[]{:S(2)}, u32[]{:S(2)}) collective-permute-start(bf16[272,128]{1,0:T(8,128)(2,1)S(1)} %get-tuple-element.29.own_ref), channel_id=1, source_target_pairs={{0,1},{1,0},{2,3},{3,2},{4,5},{5,4},{6,7},{7,6},{8,9},{9,8},{10,11... | collective-permute-start | bytes 208904 | tf_op jit(solution)/shard_map/ppermute | solution.py:560
  23.4 2.5 %collective-permute-start.4 = (bf16[272,128]{1,0:T(8,128)(2,1)S(1)}, bf16[272,128]{1,0:T(8,128)(2,1)S(1)}, u32[]{:S(2)}, u32[]{:S(2)}) collective-permute-start(bf16[272,128]{1,0:T(8,128)(2,1)S(1)} %collective-permute-done.3.y_ref), channel_id=1, source_target_pairs={{0,1},{1,0},{2,3},{3,2},{4,5},{5,4},{6,7},{7,6},{8,9},{9,8},{10,11... | collective-permute-start | bytes 208904 | tf_op jit(solution)/shard_map/ppermute | solution.py:560
  25.9 9.4 %copy-start = (bf16[27,128,128]{2,1,0:T(8,128)(2,1)S(1)}, bf16[27,128,128]{2,1,0:T(8,128)(2,1)}, u32[]{:S(2)}) copy-start(bf16[27,128,128]{2,1,0:T(8,128)(2,1)} %param.19) | copy-start | bytes 2654212
  30.4 8.5 %collective-permute-start.9 = (bf16[4,64,128]{2,1,0:T(8,128)(2,1)S(1)}, bf16[4,64,128]{2,1,0:T(8,128)(2,1)S(1)}, u32[]{:S(2)}, u32[]{:S(2)}) collective-permute-start(bf16[4,64,128]{2,1,0:T(8,128)(2,1)S(1)} %get-tuple-element.32), channel_id=1, source_target_pairs={{0,1},{1,0},{2,3},{3,2},{4,5},{5,4},{6,7},{7,6},{8,9},{9,8},{10,11... | collective-permute-start | bytes 196616 | tf_op jit(solution)/shard_map/ppermute | solution.py:560
  30.9 8.0 %collective-permute-start.10 = (bf16[4,64,128]{2,1,0:T(8,128)(2,1)S(1)}, bf16[4,64,128]{2,1,0:T(8,128)(2,1)S(1)}, u32[]{:S(2)}, u32[]{:S(2)}) collective-permute-start(bf16[4,64,128]{2,1,0:T(8,128)(2,1)S(1)} %get-tuple-element.33), channel_id=1, source_target_pairs={{1,2},{2,1},{3,4},{4,3},{5,6},{6,5},{7,8},{8,7},{9,10},{10,9},{11,... | collective-permute-start | bytes 196616 | tf_op jit(solution)/shard_map/ppermute | solution.py:560

commit v4 on v3

--- a/solution.py
+++ b/solution.py
@@ -9,8 +9,9 @@
 
 
 LANES = 4
-GROUP = 1
-CONV_GROUP = 2
+GROUP = 2
+ENC_GROUP = 1
+DEC_GROUP = 4
 TILE = 16
 OFFSETS = (-1, 0, 1)
 BF16 = jnp.bfloat16
@@ -107,7 +108,9 @@
     numbers[0:coarse_slots, 0:8] = jnp.where(child >= 0, (child & (LANES * slots - 1)) + 1, 0)
     around = around_v[...]
     first = ((position >> 2) - 1) * LANES * coarse_slots
-    numbers[coarse_slots : 2 * coarse_slots, 0:27] = jnp.where(around >= 0, around - first + 1, 0)
+    place = around - first
+    inside = (around >= 0) & (place >= 0) & (place < 3 * LANES * coarse_slots)
+    numbers[coarse_slots : 2 * coarse_slots, 0:27] = jnp.where(inside, place + 1, 0)
     codes_ref[...] = numbers[...].astype(F32).astype(BF16)
     is_odd = (position & 1) == 1
     send = send_v[...]
@@ -215,25 +218,24 @@
     )(nbr, x, weights)
 
 
-def outer_planes(nbr, near_ref, far_ref, part_ref, w_ref, out_ref, edge):
+def outer_planes(nbr, near_ref, far_ref, part_ref, w_ref, out_ref, stack, edge):
     slots, _, rows, width = part_ref.shape
     pairs = edge // 2
-    is_odd = (nbr[slots + 3, 0] & 1) == 1
+    is_odd = nbr[slots + 3, 0] & 1
+    stack[:slots] = near_ref[...].astype(F32)
+    stack[slots : 2 * slots] = far_ref[...].astype(F32)
+    stack[2 * slots] = jnp.zeros((rows, width), F32)
     for side, dx in enumerate((-1, 1)):
-        use_near = is_odd if side == 0 else jnp.logical_not(is_odd)
+        offset = slots * (1 - is_odd if side == 0 else is_odd)
         bricks = []
         for b in range(slots):
 
             def fetch(dy, dz):
                 slot = nbr[b, tap(dx, dy, dz)]
-                held = jnp.maximum(slot, 0)
-
-                def load(r, n):
-                    near = near_ref[held, r : r + n, :].astype(F32)
-                    far = far_ref[held, r : r + n, :].astype(F32)
-                    return jnp.where(use_near, near, far)[None]
-
-                return jnp.where(slot >= 0, y_rows(load, dy, edge), 0.0)
+                held = jnp.where(slot >= 0, slot + offset, 2 * slots)
+                first, count = {-1: (edge - 1, 1), 0: (0, edge), 1: (0, 1)}[dy]
+                value = stack[held, first * edge : (first + count) * edge]
+                return value.reshape(1, count, edge, width)
 
             shifted = columns(fetch, edge)
             taps = []
@@ -253,11 +255,11 @@
             out_ref[b, plane] = jnp.maximum(total, 0.0).astype(BF16)
 
 
-def outer_kernel(nbr, near_ref, far_ref, part_ref, w_ref, main_ref, out_hbm, planes, sems):
+def outer_kernel(nbr, near_ref, far_ref, part_ref, w_ref, main_ref, out_hbm, planes, stack, sems):
     edge = main_ref.shape[1]
     inside = pltpu.make_async_copy(main_ref.at[:, 1 : edge - 1], out_hbm.at[:, 1 : edge - 1], sems.at[0])
     inside.start()
-    outer_planes(nbr, near_ref, far_ref, part_ref, w_ref, planes, edge)
+    outer_planes(nbr, near_ref, far_ref, part_ref, w_ref, planes, stack, edge)
     copies = [
         pltpu.make_async_copy(planes.at[:, i], out_hbm.at[:, x], sems.at[i + 1])
         for i, x in enumerate((0, edge - 1))
@@ -274,7 +276,11 @@
         out_shape=jax.ShapeDtypeStruct(main.shape, BF16),
         in_specs=[SMEM, VMEM, VMEM, VMEM, VMEM, VMEM],
         out_specs=HBM,
-        scratch_shapes=[pltpu.VMEM(part.shape, BF16), pltpu.SemaphoreType.DMA((3,))],
+        scratch_shapes=[
+            pltpu.VMEM(part.shape, BF16),
+            pltpu.VMEM((2 * main.shape[0] + 1,) + main.shape[2:], F32),
+            pltpu.SemaphoreType.DMA((3,)),
+        ],
         compiler_params=PARAMS,
         cost_estimate=pl.CostEstimate(flops=536870912, bytes_accessed=4194304, transcendentals=0),
         name="outer",
@@ -282,12 +288,12 @@
 
 
 def outer_pool_kernel(
-    nbr, near_ref, far_ref, part_ref, w_ref, main_ref, code_ref, out_ref, pool_ref, rim_ref, sums
+    nbr, near_ref, far_ref, part_ref, w_ref, main_ref, code_ref, out_ref, pool_ref, rim_ref, sums, stack
 ):
     slots, edge, _, width = out_ref.shape
     half = edge // 2
     out_ref[:, 1 : edge - 1] = main_ref[:, 1 : edge - 1]
-    outer_planes(nbr, near_ref, far_ref, part_ref, w_ref, out_ref, edge)
+    outer_planes(nbr, near_ref, far_ref, part_ref, w_ref, out_ref, stack, edge)
     cells = half**3
     pool_ref[slots * cells :] = code_ref[...]
     rim_ref[slots * cells // 2 :] = code_ref[...]
@@ -305,7 +311,7 @@
 
 
 def outer_pool(main, part, near, far, nbr, weights, codes):
-    slots, edge, _, width = main.shape
+    slots, edge, rows, width = main.shape
     cells = (edge // 2) ** 3
     return pl.pallas_call(
         outer_pool_kernel,
@@ -316,7 +322,10 @@
         ),
         in_specs=[SMEM, VMEM, VMEM, VMEM, VMEM, VMEM, VMEM],
         out_specs=(VMEM, VMEM, VMEM),
-        scratch_shapes=[pltpu.VMEM((slots, 2 * cells, width), F32)],
+        scratch_shapes=[
+            pltpu.VMEM((slots, 2 * cells, width), F32),
+            pltpu.VMEM((2 * slots + 1, rows, width), F32),
+        ],
         compiler_params=PARAMS,
         cost_estimate=pl.CostEstimate(flops=536870912, bytes_accessed=4194304, transcendentals=0),
         name="outer_pool",
@@ -333,7 +342,7 @@
     return jnp.concatenate(blocks, axis=0)
 
 
-def valid_conv(values, weights, cols, edge, width):
+def valid_conv(values, weights, cols, edge, width, group):
     size = values[0].shape[0]
     inside = size - 2
     pairs = inside // 2
@@ -359,8 +368,8 @@
         bricks.append(jnp.concatenate(taps, axis=1))
     rows = inside * edge
     outs = []
-    for first in range(0, len(values), CONV_GROUP):
-        picked = bricks[first : first + CONV_GROUP]
+    for first in range(0, len(values), group):
+        picked = bricks[first : first + group]
         total = jnp.dot(jnp.concatenate(picked, axis=0), weights, preferred_element_type=F32)
         total = jnp.maximum(total, 0.0).astype(BF16).astype(F32)
         for i in range(len(picked)):
@@ -371,8 +380,8 @@
 
 
 def coarse_kernel(
-    coarse_slots, meta, own_ref, core_ref, y_ref, yc_ref, big_ref, bigc_ref, enc_ref, w1_ref, w2_ref,
-    out_ref, near_ref, far_ref, held, codes, even, odd, even2, odd2, spread, table, code_s, part_s, sem,
+    coarse_slots, meta, own_ref, core_ref, y_ref, yc_ref, z_ref, zy_ref, zc_ref, zyc_ref, enc_ref, w1_ref, w2_ref,
+    out_ref, near_ref, far_ref, held, codes, even, odd, even2, odd2, spread, table, code_s, sem,
 ):
     slots, edge, rows, width = enc_ref.shape
     half = edge // 2
@@ -380,14 +389,13 @@
     cells = half * plane
     position = meta[slots + 3, 0]
     lane = position & (LANES - 1)
-    group_bits = (LANES * coarse_slots).bit_length() - 1
     lane_c = position & 1
     whole_rows = slots * cells
     rim_rows = whole_rows // 2
     section = (LANES * slots + 1) * cells
-    rim_at = [i * (rim_rows + TILE) for i in range(4)]
     places = [(ref, 0, whole_rows) for ref in (own_ref, core_ref, y_ref, yc_ref)]
-    places += [(ref, at, rim_rows) for ref in (big_ref, bigc_ref) for at in rim_at]
+    for ref in (z_ref, zy_ref, zc_ref, zyc_ref):
+        places += [(ref, at, rim_rows) for at in (0, rim_rows + TILE)]
     origins = [LANES + (lane ^ i) for i in range(LANES)]
     near_rel = jnp.where(lane_c == 1, 2 * LANES, 0)
     far_rel = 2 * LANES - near_rel
@@ -395,10 +403,11 @@
     origins += [far_rel + (lane ^ i) for i in range(LANES)]
     lines = 3 * LANES * coarse_slots + 1
     codes[...] = jnp.zeros_like(codes)
-    for origin, (ref, at, count) in zip(origins, places):
+    for i, (origin, (ref, at, count)) in enumerate(zip(origins, places)):
         line = ref[at + count : at + count + TILE].astype(F32).astype(jnp.int32)
         row = 1 + origin * coarse_slots
-        codes[pl.ds(row, coarse_slots)] = line[:coarse_slots]
+        start = 2 * section if i < LANES else jnp.where(origin >= LANES, 3 * section, section)
+        codes[pl.ds(row, coarse_slots)] = line[:coarse_slots] * cells + start
         codes[pl.ds(lines + row, coarse_slots)] = line[coarse_slots : 2 * coarse_slots]
     copy = pltpu.make_async_copy(codes, table, sem)
     copy.start()
@@ -429,23 +438,21 @@
         own = jnp.where(meta[slots + 2, b] >= 0, meta[slots + 2, b], group_first * 8)
         octant = own & 7
         bits = ((octant >> 2) & 1, (octant >> 1) & 1, octant & 1)
-        home = lines + 1 + LANES * coarse_slots + (own >> 3) - group_first
+        brick = jnp.clip((own >> 3) - group_first, 0, LANES * coarse_slots - 1)
+        home = lines + 1 + LANES * coarse_slots + brick
         steps = [scale * (2 * bit - 1) for scale, bit in zip((9, 3, 1), bits)]
         numbers = [13, 13 + steps[2]]
         numbers += [number + steps[1] for number in numbers]
         numbers += [number + steps[0] for number in numbers]
         for cross, number in enumerate(numbers):
-            found = table[home, number]
-            code_s[b, cross] = found
-            part_s[b, cross] = ((found + LANES * coarse_slots - 1) >> group_bits) * section
+            code_s[b, cross] = table[home, number]
         turns = [octant ^ flip for flip in range(8)]
         across = [{0: 0, 1: scale * bit, -1: scale * (1 - bit)} for scale, bit in zip((4, 2, 1), bits)]
 
         def base_of(ex, ey, ez):
             flip = 4 * abs(ex) + 2 * abs(ey) + abs(ez)
             cross = across[0][ex] + across[1][ey] + across[2][ez]
-            child = table[code_s[b, cross], turns[flip]]
-            base = part_s[b, cross] + child * cells
+            base = table[code_s[b, cross], turns[flip]]
             return pl.multiple_of(base + (2 * plane if ex < 0 else 0), TILE)
 
         x_parts = []
@@ -480,7 +487,7 @@
         masks.append(kinds)
 
     mids = []
-    for value, kinds in zip(valid_conv(regions, x_pair_weights(w1_ref, width), (even, odd), edge, width), masks):
+    for value, kinds in zip(valid_conv(regions, x_pair_weights(w1_ref, width), (even, odd), edge, width, ENC_GROUP), masks):
         spans = ((0, 1), (1, half + 1), (half + 1, half + 2))
         x_parts = []
         for i, (x0, x1) in enumerate(spans):
@@ -489,7 +496,7 @@
                 y_parts.append(jnp.where(kinds[3 * i + n][None], value[x0:x1, y0:y1], 0.0))
             x_parts.append(jnp.concatenate(y_parts, axis=1))
         mids.append(jnp.concatenate(x_parts, axis=0))
-    fines = valid_conv(mids, x_pair_weights(w2_ref, width), (even2, odd2), edge, width)
+    fines = valid_conv(mids, x_pair_weights(w2_ref, width), (even2, odd2), edge, width, DEC_GROUP)
     is_odd = lane_c == 1
     for b in range(slots):
         value = jnp.where(meta[slots + 2, b] >= 0, fines[b], 0.0).reshape(plane * edge, width)
@@ -511,13 +518,12 @@
     half = edge // 2
     inside = edge - 2
     total = 4 * (LANES * slots + 1) * half**3
-    assert LANES * coarse_slots & (LANES * coarse_slots - 1) == 0
     lines = 2 * (3 * LANES * coarse_slots + 1)
     face = jax.ShapeDtypeStruct((slots, rows, width), BF16)
     return pl.pallas_call(
         functools.partial(coarse_kernel, coarse_slots),
         out_shape=(jax.ShapeDtypeStruct(enc.shape, BF16), face, face),
-        in_specs=[SMEM] + [VMEM] * 9,
+        in_specs=[SMEM] + [VMEM] * 11,
         out_specs=(VMEM, VMEM, VMEM),
         scratch_shapes=[
             pltpu.VMEM((total, width), BF16),
@@ -528,7 +534,6 @@
             pltpu.VMEM((slots, 3, inside, half * edge, width), BF16),
             pltpu.VMEM((slots, 2 * half * half * edge, width), F32),
             pltpu.SMEM((lines, width), jnp.int32),
-            pltpu.SMEM((slots, 8), jnp.int32),
             pltpu.SMEM((slots, 8), jnp.int32),
             pltpu.SemaphoreType.DMA,
         ],
@@ -586,11 +591,11 @@
     rim_z = across_z(jnp.concatenate([rim, rim_c], axis=0))
     pooled_y = across_y(pooled)
     rim_zy = across_y(rim_z)
-    big = jnp.concatenate([rim_z, rim_zy], axis=0)
     pooled_c = core(pooled)
     pooled_yc = core(pooled_y)
-    big_c = core(big)
-    blocks = [pooled, pooled_c, pooled_y, pooled_yc, big, big_c]
+    rim_zc = core(rim_z)
+    rim_zyc = core(rim_zy)
+    blocks = [pooled, pooled_c, pooled_y, pooled_yc, rim_z, rim_zy, rim_zc, rim_zyc]
     dec_in, near, far = coarse(meta, blocks, enc, flat[1], flat[2], coarse_slots)
     far = next_chip(far)
     near = core(near)

time: 40.9 us -> 37.3 us (0.912)
  waiting for transfers between devices: 9.72 us -> 6.85 us
    ppermute x11 -> x12, waiting for transfers between devices: 9.72 us -> 6.85 us  [swap(): return lax.ppermute(value, 'gx', pairs)]
    ppermute x11 -> x12, starting transfers between devices: 14.9 us -> 14.6 us  [swap(): return lax.ppermute(value, 'gx', pairs)]
  transfers between devices with their start and end apart: 11 -> 12, of which waited for: 5 -> 6; matrix products, arithmetic and copies ran while one was open for 0% -> 0% of each run, Pallas kernels for 17% -> 19%
where the time goes in v4:
time: 37.3 us; the launch traced here: 37.1 us
  Pallas kernels  15.5 us (42%)
  starting transfers between devices  14.6 us (39%)
  waiting for transfers between devices  6.85 us (18%)
    ppermute x12, starting transfers between devices, swap(): return lax.ppermute(value, 'gx', pairs)  14.6 us
    pallas_call x2, Pallas kernels, inner(): pl.pallas_call(inner_kernel, out_shape=(jax.ShapeDtypeStruct(x.shape, BF1...  6.93 us
    ppermute x12, waiting for transfers between devices, swap(): return lax.ppermute(value, 'gx', pairs)  6.85 us
    pallas_call x1, Pallas kernels, coarse(): pl.pallas_call(functools.partial(coarse_kernel, coarse_slots), out_shape=...  4.29 us
    pallas_call x1, Pallas kernels, outer(): pl.pallas_call(outer_kernel, out_shape=jax.ShapeDtypeStruct(main.shape, B...  1.69 us
    pallas_call x1, Pallas kernels, first(): pl.pallas_call(first_kernel, out_shape=(face, face, jax.ShapeDtypeStruct(...  1.56 us
    pallas_call x1, Pallas kernels, outer_pool(): pl.pallas_call(outer_pool_kernel, out_shape=(jax.ShapeDtypeStruct(main.sh...  1.03 us
  transfers between devices with their start and end apart: 12, of which 6 were waited for; matrix products, arithmetic and copies ran while one was open for 0% of the time, Pallas kernels for 19%

profile of v4, /device:TPU:5, one launch (start us, length us, event | category | flops | bytes accessed | tf_op | source)
XLA Modules:
  0.0 37.1 jit_solution(2117266011765611703)
XLA Ops:
  0.0 1.6 %first.1 = (bf16[4,64,128]{2,1,0:T(8,128)(2,1)S(1)}, bf16[4,64,128]{2,1,0:T(8,128)(2,1)S(1)}, s32[8,128]{1,0:T(8,128)S(1)}, bf16[16,128]{1,0:T(8,128)(2,1)S(1)},...) custom-call(s32[1,1]{1,0:T(1,128)} %bitcast.info, bf16[4,8,64,128]{3,2,1,0:T(8,128)(2,1)} %bitcast.14, ...), custom_call_target="tpu_custom_call" | custom-call | bytes 2097152 | tf_op jit(solution)/shard_map/first/pallas_call | solution.py:137
  1.6 0.7 %collective-permute-start = (bf16[4,64,128]{2,1,0:T(8,128)(2,1)S(1)}, bf16[4,64,128]{2,1,0:T(8,128)(2,1)S(1)}, u32[]{:S(2)}, u32[]{:S(2)}) collective-permute-start(bf16[4,64,128]{2,1,0:T(8,128)(2,1)S(1)} %get-tuple-element.22), channel_id=1, source_target_pairs={{0,1},{1,0},{2,3},{3,2},{4,5},{5,4},{6,7},{7,6},{8,9},{9,8},{10,11... | collective-permute-start | bytes 196616 | tf_op jit(solution)/shard_map/ppermute | solution.py:565
  2.3 3.0 %collective-permute-start.1 = (bf16[4,64,128]{2,1,0:T(8,128)(2,1)S(1)}, bf16[4,64,128]{2,1,0:T(8,128)(2,1)S(1)}, u32[]{:S(2)}, u32[]{:S(2)}) collective-permute-start(bf16[4,64,128]{2,1,0:T(8,128)(2,1)S(1)} %get-tuple-element.23), channel_id=1, source_target_pairs={{1,2},{2,1},{3,4},{4,3},{5,6},{6,5},{7,8},{8,7},{9,10},{10,9},{11,... | collective-permute-start | bytes 196616 | tf_op jit(solution)/shard_map/ppermute | solution.py:565
  5.4 3.4 %inner.2 = (bf16[4,8,64,128]{3,2,1,0:T(8,128)(2,1)S(1)}, f32[4,2,64,128]{3,2,1,0:T(8,128)S(1)}) custom-call(s32[8,128]{1,0:T(8,128)S(1)} %get-tuple-element.21.nbr.meta, bf16[4,8,64,128]{3,2,1,0:T(8,128)(2,1)S(1)} %get-tuple-element.24.x_ref, bf16[3456,128]{1,0:T(8,128)(2,1)S(1)} %get-tuple-element.25.w_ref), custom_call_target="tpu_custom_call" | custom-call | flops 1811939328 | bytes 4194304 | tf_op jit(solution)/shard_map/inner/pallas_call | solution.py:200
  8.8 0.0 collective-permute-done.near_ref
  8.8 0.0 collective-permute-done.1.far_ref
  8.8 0.0 copy-start.1
  8.8 0.0 copy-start.2
  8.9 1.0 %outer_pool.1 = (bf16[4,8,64,128]{3,2,1,0:T(8,128)(2,1)S(1)}, bf16[272,128]{1,0:T(8,128)(2,1)S(1)}, bf16[144,128]{1,0:T(8,128)(2,1)S(1)}) custom-call(s32[8,128]{1,0:T(8,128)S(1)} %get-tuple-element.21.nbr.meta, bf16[4,64,128]{2,1,0:T(8,128)(2,1)S(1)} %collective-permute-done.near_ref, bf16[4,64,128]{2,1,0:T(8,128)(2,1)S(1)} %collective-permute-done.1.far_ref, ...), custom_call_target="tpu_custom_call" | custom-call | flops 536870912 | bytes 4194304 | tf_op jit(solution)/shard_map/outer_pool/pallas_call | solution.py:316
  9.9 0.1 collective-permute-start.5
  10.0 1.2 %collective-permute-done.5 = bf16[144,128]{1,0:T(8,128)(2,1)S(1)} collective-permute-done((bf16[144,128]{1,0:T(8,128)(2,1)S(1)}, bf16[144,128]{1,0:T(8,128)(2,1)S(1)}, u32[]{:S(2)}, u32[]{:S(2)}) %collective-permute-start.5) | collective-permute-done | bytes 36896 | tf_op jit(solution)/shard_map/ppermute | solution.py:565
  11.2 3.2 %collective-permute-start.6 = (bf16[288,128]{1,0:T(8,128)(2,1)S(1)}, bf16[288,128]{1,0:T(8,128)(2,1)S(1)}, u32[]{:S(2)}, u32[]{:S(2)}) collective-permute-start(bf16[288,128]{1,0:T(8,128)(2,1)S(1)} %pad_maximum_fusion), channel_id=1, source_target_pairs={{1,4},{3,6},{4,1},{5,8},{6,3},{7,10},{8,5},{9,12},{10,7},{11,14},{... | collective-permute-start | bytes 221192 | tf_op jit(solution)/shard_map/ppermute | solution.py:565
  14.4 2.4 %collective-permute-done.6.z_ref = bf16[288,128]{1,0:T(8,128)(2,1)S(1)} collective-permute-done((bf16[288,128]{1,0:T(8,128)(2,1)S(1)}, bf16[288,128]{1,0:T(8,128)(2,1)S(1)}, u32[]{:S(2)}, u32[]{:S(2)}) %collective-permute-start.6) | collective-permute-done | bytes 73760 | tf_op jit(solution)/shard_map/ppermute | solution.py:565
  16.8 0.5 %collective-permute-start.7 = (bf16[288,128]{1,0:T(8,128)(2,1)S(1)}, bf16[288,128]{1,0:T(8,128)(2,1)S(1)}, u32[]{:S(2)}, u32[]{:S(2)}) collective-permute-start(bf16[288,128]{1,0:T(8,128)(2,1)S(1)} %collective-permute-done.6.z_ref), channel_id=1, source_target_pairs={{0,2},{1,3},{2,0},{3,1},{4,6},{5,7},{6,4},{7,5},{8,10},{9,11},{10,... | collective-permute-start | bytes 221192 | tf_op jit(solution)/shard_map/ppermute | solution.py:565
  17.4 0.9 %collective-permute-start.3 = (bf16[272,128]{1,0:T(8,128)(2,1)S(1)}, bf16[272,128]{1,0:T(8,128)(2,1)S(1)}, u32[]{:S(2)}, u32[]{:S(2)}) collective-permute-start(bf16[272,128]{1,0:T(8,128)(2,1)S(1)} %get-tuple-element.29.own_ref), channel_id=1, source_target_pairs={{0,2},{1,3},{2,0},{3,1},{4,6},{5,7},{6,4},{7,5},{8,10},{9,11},{10,... | collective-permute-start | bytes 208904 | tf_op jit(solution)/shard_map/ppermute | solution.py:565
  18.3 0.0 collective-permute-start.8
  18.3 1.7 %collective-permute-done.7.zy_ref = bf16[288,128]{1,0:T(8,128)(2,1)S(1)} collective-permute-done((bf16[288,128]{1,0:T(8,128)(2,1)S(1)}, bf16[288,128]{1,0:T(8,128)(2,1)S(1)}, u32[]{:S(2)}, u32[]{:S(2)}) %collective-permute-start.7) | collective-permute-done | bytes 73760 | tf_op jit(solution)/shard_map/ppermute | solution.py:565
  20.0 0.0 collective-permute-start.9
  20.0 0.5 %collective-permute-start.2 = (bf16[272,128]{1,0:T(8,128)(2,1)S(1)}, bf16[272,128]{1,0:T(8,128)(2,1)S(1)}, u32[]{:S(2)}, u32[]{:S(2)}) collective-permute-start(bf16[272,128]{1,0:T(8,128)(2,1)S(1)} %get-tuple-element.29.own_ref), channel_id=1, source_target_pairs={{0,1},{1,0},{2,3},{3,2},{4,5},{5,4},{6,7},{7,6},{8,9},{9,8},{10,11... | collective-permute-start | bytes 208904 | tf_op jit(solution)/shard_map/ppermute | solution.py:565
  20.5 0.2 collective-permute-done.3.y_ref
  20.8 0.0 collective-permute-start.4
  20.8 0.7 %collective-permute-done.2.core_ref = bf16[272,128]{1,0:T(8,128)(2,1)S(1)} collective-permute-done((bf16[272,128]{1,0:T(8,128)(2,1)S(1)}, bf16[272,128]{1,0:T(8,128)(2,1)S(1)}, u32[]{:S(2)}, u32[]{:S(2)}) %collective-permute-start.2) | collective-permute-done | bytes 69664 | tf_op jit(solution)/shard_map/ppermute | solution.py:565
  21.5 0.6 %collective-permute-done.4.yc_ref = bf16[272,128]{1,0:T(8,128)(2,1)S(1)} collective-permute-done((bf16[272,128]{1,0:T(8,128)(2,1)S(1)}, bf16[272,128]{1,0:T(8,128)(2,1)S(1)}, u32[]{:S(2)}, u32[]{:S(2)}) %collective-permute-start.4) | collective-permute-done | bytes 69664 | tf_op jit(solution)/shard_map/ppermute | solution.py:565
  22.0 0.0 collective-permute-done.8.zc_ref
  22.0 0.0 collective-permute-done.9.zyc_ref
  22.1 0.0 copy-done.1
  22.1 0.0 copy-done.2
  22.1 0.0 copy-start
  22.1 4.3 %coarse.1 = (bf16[4,8,64,128]{3,2,1,0:T(8,128)(2,1)S(1)}, bf16[4,64,128]{2,1,0:T(8,128)(2,1)S(1)}, bf16[4,64,128]{2,1,0:T(8,128)(2,1)S(1)}) custom-call(s32[8,128]{1,0:T(8,128)S(1)} %get-tuple-element.21.nbr.meta, bf16[272,128]{1,0:T(8,128)(2,1)S(1)} %get-tuple-element.29.own_ref, bf16[272,128]{1,0:T(8,128)(2,1)S(1)} %collective-permute-done.2.core_ref, ...), custom_call_target="tpu_custom_call" | custom-call | flops 2147483648 | bytes 8388608 | tf_op jit(solution)/shard_map/coarse/pallas_call | solution.py:523
  26.4 0.2 collective-permute-start.10
  26.6 5.3 %collective-permute-start.11 = (bf16[4,64,128]{2,1,0:T(8,128)(2,1)S(1)}, bf16[4,64,128]{2,1,0:T(8,128)(2,1)S(1)}, u32[]{:S(2)}, u32[]{:S(2)}) collective-permute-start(bf16[4,64,128]{2,1,0:T(8,128)(2,1)S(1)} %get-tuple-element.33), channel_id=1, source_target_pairs={{1,2},{2,1},{3,4},{4,3},{5,6},{6,5},{7,8},{8,7},{9,10},{10,9},{11,... | collective-permute-start | bytes 196616 | tf_op jit(solution)/shard_map/ppermute | solution.py:565
  31.9 0.0 copy-done
  31.9 3.5 %inner.3 = (bf16[4,8,64,128]{3,2,1,0:T(8,128)(2,1)S(1)}, f32[4,2,64,128]{3,2,1,0:T(8,128)S(1)}) custom-call(s32[8,128]{1,0:T(8,128)S(1)} %get-tuple-element.21.nbr.meta, bf16[4,8,64,128]{3,2,1,0:T(8,128)(2,1)S(1)} %get-tuple-element.34.x_ref, bf16[3456,128]{1,0:T(8,128)(2,1)S(1)} %bitcast.9), custom_call_target="tpu_custom_call" | custom-call | flops 1811939328 | bytes 4194304 | tf_op jit(solution)/shard_map/inner/pallas_call | solution.py:200
  35.4 0.0 collective-permute-done.10.near_ref
  35.4 0.0 collective-permute-done.11.far_ref
  35.4 1.7 %outer.1 = bf16[4,8,64,128]{3,2,1,0:T(8,128)(2,1)} custom-call(s32[8,128]{1,0:T(8,128)S(1)} %get-tuple-element.21.nbr.meta, bf16[4,64,128]{2,1,0:T(8,128)(2,1)S(1)} %collective-permute-done.10.near_ref, bf16[4,64,128]{2,1,0:T(8,128)(2,1)S(1)} %collective-permute-done.11.far_ref, f32[4,2,64,128]{3,2,1,0:T(8,128)S(1)} %get-tuple-element.35.part_ref, ...), custom_call_target="tpu_custom_call" | custom-call | flops 536870912 | bytes 4194304 | tf_op jit(solution)/shard_map/outer/pallas_call | solution.py:274
  (1 shorter events, 0.0 us)
Async XLA Ops:
  1.6 7.2 %collective-permute-start = (bf16[4,64,128]{2,1,0:T(8,128)(2,1)S(1)}, bf16[4,64,128]{2,1,0:T(8,128)(2,1)S(1)}, u32[]{:S(2)}, u32[]{:S(2)}) collective-permute-start(bf16[4,64,128]{2,1,0:T(8,128)(2,1)S(1)} %get-tuple-element.22), channel_id=1, source_target_pairs={{0,1},{1,0},{2,3},{3,2},{4,5},{5,4},{6,7},{7,6},{8,9},{9,8},{10,11... | collective-permute-start | bytes 196616 | tf_op jit(solution)/shard_map/ppermute | solution.py:565
  2.3 6.5 %collective-permute-start.1 = (bf16[4,64,128]{2,1,0:T(8,128)(2,1)S(1)}, bf16[4,64,128]{2,1,0:T(8,128)(2,1)S(1)}, u32[]{:S(2)}, u32[]{:S(2)}) collective-permute-start(bf16[4,64,128]{2,1,0:T(8,128)(2,1)S(1)} %get-tuple-element.23), channel_id=1, source_target_pairs={{1,2},{2,1},{3,4},{4,3},{5,6},{6,5},{7,8},{8,7},{9,10},{10,9},{11,... | collective-permute-start | bytes 196616 | tf_op jit(solution)/shard_map/ppermute | solution.py:565
  8.8 13.2 %copy-start.1 = (bf16[27,128,128]{2,1,0:T(8,128)(2,1)S(1)}, bf16[27,128,128]{2,1,0:T(8,128)(2,1)}, u32[]{:S(2)}) copy-start(bf16[27,128,128]{2,1,0:T(8,128)(2,1)} %param.17) | copy-start | bytes 2654212
  8.8 13.2 %copy-start.2 = (bf16[27,128,128]{2,1,0:T(8,128)(2,1)S(1)}, bf16[27,128,128]{2,1,0:T(8,128)(2,1)}, u32[]{:S(2)}) copy-start(bf16[27,128,128]{2,1,0:T(8,128)(2,1)} %param.18) | copy-start | bytes 2654212
  9.9 1.3 %collective-permute-start.5 = (bf16[144,128]{1,0:T(8,128)(2,1)S(1)}, bf16[144,128]{1,0:T(8,128)(2,1)S(1)}, u32[]{:S(2)}, u32[]{:S(2)}) collective-permute-start(bf16[144,128]{1,0:T(8,128)(2,1)S(1)} %get-tuple-element.30), channel_id=1, source_target_pairs={{0,1},{1,0},{2,3},{3,2},{4,5},{5,4},{6,7},{7,6},{8,9},{9,8},{10,11... | collective-permute-start | bytes 110600 | tf_op jit(solution)/shard_map/ppermute | solution.py:565
  11.2 5.7 %collective-permute-start.6 = (bf16[288,128]{1,0:T(8,128)(2,1)S(1)}, bf16[288,128]{1,0:T(8,128)(2,1)S(1)}, u32[]{:S(2)}, u32[]{:S(2)}) collective-permute-start(bf16[288,128]{1,0:T(8,128)(2,1)S(1)} %pad_maximum_fusion), channel_id=1, source_target_pairs={{1,4},{3,6},{4,1},{5,8},{6,3},{7,10},{8,5},{9,12},{10,7},{11,14},{... | collective-permute-start | bytes 221192 | tf_op jit(solution)/shard_map/ppermute | solution.py:565
  16.8 3.2 %collective-permute-start.7 = (bf16[288,128]{1,0:T(8,128)(2,1)S(1)}, bf16[288,128]{1,0:T(8,128)(2,1)S(1)}, u32[]{:S(2)}, u32[]{:S(2)}) collective-permute-start(bf16[288,128]{1,0:T(8,128)(2,1)S(1)} %collective-permute-done.6.z_ref), channel_id=1, source_target_pairs={{0,2},{1,3},{2,0},{3,1},{4,6},{5,7},{6,4},{7,5},{8,10},{9,11},{10,... | collective-permute-start | bytes 221192 | tf_op jit(solution)/shard_map/ppermute | solution.py:565
  17.4 3.4 %collective-permute-start.3 = (bf16[272,128]{1,0:T(8,128)(2,1)S(1)}, bf16[272,128]{1,0:T(8,128)(2,1)S(1)}, u32[]{:S(2)}, u32[]{:S(2)}) collective-permute-start(bf16[272,128]{1,0:T(8,128)(2,1)S(1)} %get-tuple-element.29.own_ref), channel_id=1, source_target_pairs={{0,2},{1,3},{2,0},{3,1},{4,6},{5,7},{6,4},{7,5},{8,10},{9,11},{10,... | collective-permute-start | bytes 208904 | tf_op jit(solution)/shard_map/ppermute | solution.py:565
  18.3 3.7 %collective-permute-start.8 = (bf16[288,128]{1,0:T(8,128)(2,1)S(1)}, bf16[288,128]{1,0:T(8,128)(2,1)S(1)}, u32[]{:S(2)}, u32[]{:S(2)}) collective-permute-start(bf16[288,128]{1,0:T(8,128)(2,1)S(1)} %collective-permute-done.6.z_ref), channel_id=1, source_target_pairs={{0,1},{1,0},{2,3},{3,2},{4,5},{5,4},{6,7},{7,6},{8,9},{9,8},{10,11... | collective-permute-start | bytes 221192 | tf_op jit(solution)/shard_map/ppermute | solution.py:565
  20.0 2.0 %collective-permute-start.9 = (bf16[288,128]{1,0:T(8,128)(2,1)S(1)}, bf16[288,128]{1,0:T(8,128)(2,1)S(1)}, u32[]{:S(2)}, u32[]{:S(2)}) collective-permute-start(bf16[288,128]{1,0:T(8,128)(2,1)S(1)} %collective-permute-done.7.zy_ref), channel_id=1, source_target_pairs={{0,1},{1,0},{2,3},{3,2},{4,5},{5,4},{6,7},{7,6},{8,9},{9,8},{10,11... | collective-permute-start | bytes 221192 | tf_op jit(solution)/shard_map/ppermute | solution.py:565
  20.0 1.4 %collective-permute-start.2 = (bf16[272,128]{1,0:T(8,128)(2,1)S(1)}, bf16[272,128]{1,0:T(8,128)(2,1)S(1)}, u32[]{:S(2)}, u32[]{:S(2)}) collective-permute-start(bf16[272,128]{1,0:T(8,128)(2,1)S(1)} %get-tuple-element.29.own_ref), channel_id=1, source_target_pairs={{0,1},{1,0},{2,3},{3,2},{4,5},{5,4},{6,7},{7,6},{8,9},{9,8},{10,11... | collective-permute-start | bytes 208904 | tf_op jit(solution)/shard_map/ppermute | solution.py:565
  20.8 1.3 %collective-permute-start.4 = (bf16[272,128]{1,0:T(8,128)(2,1)S(1)}, bf16[272,128]{1,0:T(8,128)(2,1)S(1)}, u32[]{:S(2)}, u32[]{:S(2)}) collective-permute-start(bf16[272,128]{1,0:T(8,128)(2,1)S(1)} %collective-permute-done.3.y_ref), channel_id=1, source_target_pairs={{0,1},{1,0},{2,3},{3,2},{4,5},{5,4},{6,7},{7,6},{8,9},{9,8},{10,11... | collective-permute-start | bytes 208904 | tf_op jit(solution)/shard_map/ppermute | solution.py:565
  22.1 9.8 %copy-start = (bf16[27,128,128]{2,1,0:T(8,128)(2,1)S(1)}, bf16[27,128,128]{2,1,0:T(8,128)(2,1)}, u32[]{:S(2)}) copy-start(bf16[27,128,128]{2,1,0:T(8,128)(2,1)} %param.19) | copy-start | bytes 2654212
  26.4 9.0 %collective-permute-start.10 = (bf16[4,64,128]{2,1,0:T(8,128)(2,1)S(1)}, bf16[4,64,128]{2,1,0:T(8,128)(2,1)S(1)}, u32[]{:S(2)}, u32[]{:S(2)}) collective-permute-start(bf16[4,64,128]{2,1,0:T(8,128)(2,1)S(1)} %get-tuple-element.32), channel_id=1, source_target_pairs={{0,1},{1,0},{2,3},{3,2},{4,5},{5,4},{6,7},{7,6},{8,9},{9,8},{10,11... | collective-permute-start | bytes 196616 | tf_op jit(solution)/shard_map/ppermute | solution.py:565
  26.6 8.8 %collective-permute-start.11 = (bf16[4,64,128]{2,1,0:T(8,128)(2,1)S(1)}, bf16[4,64,128]{2,1,0:T(8,128)(2,1)S(1)}, u32[]{:S(2)}, u32[]{:S(2)}) collective-permute-start(bf16[4,64,128]{2,1,0:T(8,128)(2,1)S(1)} %get-tuple-element.33), channel_id=1, source_target_pairs={{1,2},{2,1},{3,4},{4,3},{5,6},{6,5},{7,8},{8,7},{9,10},{10,9},{11,... | collective-permute-start | bytes 196616 | tf_op jit(solution)/shard_map/ppermute | solution.py:565

commit v5 on v4

--- a/solution.py
+++ b/solution.py
@@ -83,11 +83,11 @@
 
 
 def first_kernel(
-    info, x_hbm, w_hbm, nbr_hbm, send_hbm, parent_hbm, child_hbm, around_hbm,
-    near_ref, far_ref, meta_ref, codes_ref, x_ref, w_ref,
+    x_hbm, w_hbm, nbr_hbm, send_hbm, parent_hbm, child_hbm, around_hbm,
+    near_ref, far_ref, meta_ref, codes_ref, x_ref, w_ref, ids_ref, low_ref,
     head_v, last_v, nbr_v, send_v, parent_v, child_v, around_v, numbers, sems,
 ):
-    slots, edge, _, _ = x_hbm.shape
+    slots, edge, _, width = x_hbm.shape
     coarse_slots = child_v.shape[0]
     pairs = [(x_hbm.at[:, 0], head_v), (x_hbm.at[:, edge - 1], last_v)]
     pairs += [(nbr_hbm, nbr_v), (send_hbm, send_v), (parent_hbm, parent_v)]
@@ -98,7 +98,7 @@
         copy.start()
     for copy in copies[:-2]:
         copy.wait()
-    position = info[0, 0]
+    position = lax.axis_index("gx")
     meta_ref[...] = jnp.full(meta_ref.shape, position, jnp.int32)
     meta_ref[0:slots, 0:27] = nbr_v[...]
     meta_ref[slots : slots + 2, 0:slots] = send_v[...]
@@ -121,6 +121,22 @@
         head = head_v[b].astype(F32) * listed[1:2, b : b + 1]
         near_ref[b] = jnp.where(is_odd, head, last).astype(BF16)
         far_ref[b] = jnp.where(is_odd, last, head).astype(BF16)
+    for b in range(slots):
+        parent = jnp.broadcast_to(parent_v[0:1, b : b + 1], (1, width))
+        low_ref[b : b + 1] = jnp.where((parent & 4) == 0, 1, 0)
+    z = lax.broadcasted_iota(jnp.int32, (edge, width), 0)
+    line = 0
+    for dx in (-1, 1):
+        for b in range(slots):
+            for dy in OFFSETS:
+                wide = [
+                    jnp.broadcast_to(nbr_v[b : b + 1, tap(dx, dy, dz) : tap(dx, dy, dz) + 1], (edge, width))
+                    for dz in OFFSETS
+                ]
+                ends = (jnp.where(z == 0, wide[0], wide[1]), wide[1], jnp.where(z == edge - 1, wide[2], wide[1]))
+                for value in ends:
+                    ids_ref[line : line + edge] = value
+                    line += edge
     for copy in copies[-2:]:
         copy.wait()
 
@@ -129,8 +145,8 @@
     return pltpu.with_memory_space_constraint(value, pltpu.HBM)
 
 
-def first(info, x, weights, nbr, send, parent, child, around):
-    slots, _, rows, width = x.shape
+def first(x, weights, nbr, send, parent, child, around):
+    slots, edge, rows, width = x.shape
     coarse_slots = child.shape[0]
     assert 2 * coarse_slots <= TILE and (LANES * slots) & (LANES * slots - 1) == 0
     face = jax.ShapeDtypeStruct((slots, rows, width), BF16)
@@ -143,16 +159,18 @@
             jax.ShapeDtypeStruct((TILE, width), BF16),
             jax.ShapeDtypeStruct(x.shape, BF16),
             jax.ShapeDtypeStruct(weights.shape, BF16),
+            jax.ShapeDtypeStruct((2 * slots * 9 * edge, width), jnp.int32),
+            jax.ShapeDtypeStruct((slots, width), jnp.int32),
         ),
-        in_specs=[SMEM] + [HBM] * 7,
-        out_specs=(VMEM,) * 6,
+        in_specs=[HBM] * 7,
+        out_specs=(VMEM,) * 8,
         scratch_shapes=[pltpu.VMEM((slots, rows, width), BF16)] * 2
         + [pltpu.VMEM(v.shape, jnp.int32) for v in (nbr, send, parent, child, around)]
         + [pltpu.VMEM((TILE, width), jnp.int32), pltpu.SemaphoreType.DMA((9,))],
         compiler_params=PARAMS,
         cost_estimate=pl.CostEstimate(flops=0, bytes_accessed=2097152, transcendentals=0),
         name="first",
-    )(info, *[stay(v) for v in (x, weights, nbr, send, parent, child, around)])
+    )(*[stay(v) for v in (x, weights, nbr, send, parent, child, around)])
 
 
 def inner_kernel(nbr, x_ref, w_ref, out_ref, part_ref, cols):
@@ -218,26 +236,32 @@
     )(nbr, x, weights)
 
 
-def outer_planes(nbr, near_ref, far_ref, part_ref, w_ref, out_ref, stack, edge):
+def outer_planes(ids_ref, near_ref, far_ref, part_ref, w_ref, out_ref, stack, edge):
     slots, _, rows, width = part_ref.shape
     pairs = edge // 2
-    is_odd = nbr[slots + 3, 0] & 1
-    stack[:slots] = near_ref[...].astype(F32)
-    stack[slots : 2 * slots] = far_ref[...].astype(F32)
-    stack[2 * slots] = jnp.zeros((rows, width), F32)
+    is_odd = lax.axis_index("gx") & 1
+    for first, ref in ((0, near_ref), (slots, far_ref)):
+        value = ref[...].astype(F32).reshape(slots * edge, edge, width)
+        for k, turn in enumerate((1, 0, edge - 1)):
+            moved = pltpu.roll(value, turn, 1) if turn else value
+            stack[k, first : first + slots] = moved.reshape(slots, rows, width)
     for side, dx in enumerate((-1, 1)):
         offset = slots * (1 - is_odd if side == 0 else is_odd)
         bricks = []
         for b in range(slots):
-
-            def fetch(dy, dz):
-                slot = nbr[b, tap(dx, dy, dz)]
-                held = jnp.where(slot >= 0, slot + offset, 2 * slots)
-                first, count = {-1: (edge - 1, 1), 0: (0, edge), 1: (0, 1)}[dy]
-                value = stack[held, first * edge : (first + count) * edge]
-                return value.reshape(1, count, edge, width)
-
-            shifted = columns(fetch, edge)
+            shifted = []
+            for k in range(3):
+                parts = []
+                for dy in OFFSETS:
+                    line = (((side * slots + b) * 3 + dy + 1) * 3 + k) * edge
+                    ids = ids_ref[line : line + edge][None]
+                    first, count = {-1: (edge - 1, 1), 0: (0, edge), 1: (0, 1)}[dy]
+                    value = jnp.zeros((count, edge, width), F32)
+                    for slot in range(slots):
+                        held = stack[k, offset + slot, first * edge : (first + count) * edge]
+                        value = jnp.where(ids == slot, held.reshape(count, edge, width), value)
+                    parts.append(value)
+                shifted.append(jnp.concatenate(parts, axis=0)[None])
             taps = []
             for j in range(4):
                 for k in range(3):
@@ -255,11 +279,11 @@
             out_ref[b, plane] = jnp.maximum(total, 0.0).astype(BF16)
 
 
-def outer_kernel(nbr, near_ref, far_ref, part_ref, w_ref, main_ref, out_hbm, planes, stack, sems):
+def outer_kernel(ids_ref, near_ref, far_ref, part_ref, w_ref, main_ref, out_hbm, planes, stack, sems):
     edge = main_ref.shape[1]
     inside = pltpu.make_async_copy(main_ref.at[:, 1 : edge - 1], out_hbm.at[:, 1 : edge - 1], sems.at[0])
     inside.start()
-    outer_planes(nbr, near_ref, far_ref, part_ref, w_ref, planes, stack, edge)
+    outer_planes(ids_ref, near_ref, far_ref, part_ref, w_ref, planes, stack, edge)
     copies = [
         pltpu.make_async_copy(planes.at[:, i], out_hbm.at[:, x], sems.at[i + 1])
         for i, x in enumerate((0, edge - 1))
@@ -270,30 +294,30 @@
         copy.wait()
 
 
-def outer(main, part, near, far, nbr, weights):
+def outer(main, part, near, far, ids, weights):
     return pl.pallas_call(
         outer_kernel,
         out_shape=jax.ShapeDtypeStruct(main.shape, BF16),
-        in_specs=[SMEM, VMEM, VMEM, VMEM, VMEM, VMEM],
+        in_specs=[VMEM] * 6,
         out_specs=HBM,
         scratch_shapes=[
             pltpu.VMEM(part.shape, BF16),
-            pltpu.VMEM((2 * main.shape[0] + 1,) + main.shape[2:], F32),
+            pltpu.VMEM((3, 2 * main.shape[0]) + main.shape[2:], F32),
             pltpu.SemaphoreType.DMA((3,)),
         ],
         compiler_params=PARAMS,
         cost_estimate=pl.CostEstimate(flops=536870912, bytes_accessed=4194304, transcendentals=0),
         name="outer",
-    )(nbr, near, far, part, weights, main)
+    )(ids, near, far, part, weights, main)
 
 
 def outer_pool_kernel(
-    nbr, near_ref, far_ref, part_ref, w_ref, main_ref, code_ref, out_ref, pool_ref, rim_ref, sums, stack
+    ids_ref, low_ref, near_ref, far_ref, part_ref, w_ref, main_ref, code_ref, out_ref, pool_ref, rim_ref, sums, stack
 ):
     slots, edge, _, width = out_ref.shape
     half = edge // 2
     out_ref[:, 1 : edge - 1] = main_ref[:, 1 : edge - 1]
-    outer_planes(nbr, near_ref, far_ref, part_ref, w_ref, out_ref, stack, edge)
+    outer_planes(ids_ref, near_ref, far_ref, part_ref, w_ref, out_ref, stack, edge)
     cells = half**3
     pool_ref[slots * cells :] = code_ref[...]
     rim_ref[slots * cells // 2 :] = code_ref[...]
@@ -305,12 +329,11 @@
         high = sums[b, pl.ds(1, cells, stride=2), :]
         pooled = (low + high) * 0.125
         pool_ref[b * cells : (b + 1) * cells, :] = pooled.astype(BF16)
-        outer_x = (jnp.maximum(nbr[slots + 2, b], 0) >> 2) & 1
-        rim = jnp.where(outer_x == 0, pooled[: cells // 2], pooled[cells // 2 :])
+        rim = jnp.where(low_ref[b : b + 1] == 1, pooled[: cells // 2], pooled[cells // 2 :])
         rim_ref[b * cells // 2 : (b + 1) * cells // 2, :] = rim.astype(BF16)
 
 
-def outer_pool(main, part, near, far, nbr, weights, codes):
+def outer_pool(main, part, near, far, ids, low, weights, codes):
     slots, edge, rows, width = main.shape
     cells = (edge // 2) ** 3
     return pl.pallas_call(
@@ -320,16 +343,16 @@
             jax.ShapeDtypeStruct((slots * cells + TILE, width), BF16),
             jax.ShapeDtypeStruct((slots * cells // 2 + TILE, width), BF16),
         ),
-        in_specs=[SMEM, VMEM, VMEM, VMEM, VMEM, VMEM, VMEM],
+        in_specs=[VMEM] * 8,
         out_specs=(VMEM, VMEM, VMEM),
         scratch_shapes=[
             pltpu.VMEM((slots, 2 * cells, width), F32),
-            pltpu.VMEM((2 * slots + 1, rows, width), F32),
+            pltpu.VMEM((3, 2 * slots, rows, width), F32),
         ],
         compiler_params=PARAMS,
         cost_estimate=pl.CostEstimate(flops=536870912, bytes_accessed=4194304, transcendentals=0),
         name="outer_pool",
-    )(nbr, near, far, part, weights, main, codes)
+    )(ids, low, near, far, part, weights, main, codes)
 
 
 def x_pair_weights(w_ref, width):
@@ -380,14 +403,14 @@
 
 
 def coarse_kernel(
-    coarse_slots, meta, own_ref, core_ref, y_ref, yc_ref, z_ref, zy_ref, zc_ref, zyc_ref, enc_ref, w1_ref, w2_ref,
+    coarse_slots, meta_ref, own_ref, core_ref, y_ref, yc_ref, z_ref, zy_ref, zc_ref, zyc_ref, enc_ref, w1_ref, w2_ref,
     out_ref, near_ref, far_ref, held, codes, even, odd, even2, odd2, spread, table, code_s, sem,
 ):
     slots, edge, rows, width = enc_ref.shape
     half = edge // 2
     plane = half * half
     cells = half * plane
-    position = meta[slots + 3, 0]
+    position = lax.axis_index("gx")
     lane = position & (LANES - 1)
     lane_c = position & 1
     whole_rows = slots * cells
@@ -403,6 +426,7 @@
     origins += [far_rel + (lane ^ i) for i in range(LANES)]
     lines = 3 * LANES * coarse_slots + 1
     codes[...] = jnp.zeros_like(codes)
+    codes[2 * lines : 2 * lines + slots + 4] = meta_ref[...]
     for i, (origin, (ref, at, count)) in enumerate(zip(origins, places)):
         line = ref[at + count : at + count + TILE].astype(F32).astype(jnp.int32)
         row = 1 + origin * coarse_slots
@@ -435,7 +459,7 @@
     regions = []
     masks = []
     for b in range(slots):
-        own = jnp.where(meta[slots + 2, b] >= 0, meta[slots + 2, b], group_first * 8)
+        own = jnp.where(table[2 * lines + slots + 2, b] >= 0, table[2 * lines + slots + 2, b], group_first * 8)
         octant = own & 7
         bits = ((octant >> 2) & 1, (octant >> 1) & 1, octant & 1)
         brick = jnp.clip((own >> 3) - group_first, 0, LANES * coarse_slots - 1)
@@ -499,7 +523,7 @@
     fines = valid_conv(mids, x_pair_weights(w2_ref, width), (even2, odd2), edge, width, DEC_GROUP)
     is_odd = lane_c == 1
     for b in range(slots):
-        value = jnp.where(meta[slots + 2, b] >= 0, fines[b], 0.0).reshape(plane * edge, width)
+        value = jnp.where(table[2 * lines + slots + 2, b] >= 0, fines[b], 0.0).reshape(plane * edge, width)
         spread[b, pl.ds(0, plane * edge, stride=2), :] = value
         spread[b, pl.ds(1, plane * edge, stride=2), :] = value
         up = spread[b].reshape(half, half, 2 * edge, width)[:, :, :edge]
@@ -507,8 +531,8 @@
         total = base + up[:, None, :, None]
         total = total.reshape(edge, rows, width).astype(BF16)
         out_ref[b] = total
-        last = jnp.where(meta[slots, b] == b, total[edge - 1], 0)
-        head = jnp.where(meta[slots + 1, b] == b, total[0], 0)
+        last = jnp.where(table[2 * lines + slots, b] == b, total[edge - 1], 0)
+        head = jnp.where(table[2 * lines + slots + 1, b] == b, total[0], 0)
         near_ref[b] = jnp.where(is_odd, head, last)
         far_ref[b] = jnp.where(is_odd, last, head)
 
@@ -518,12 +542,12 @@
     half = edge // 2
     inside = edge - 2
     total = 4 * (LANES * slots + 1) * half**3
-    lines = 2 * (3 * LANES * coarse_slots + 1)
+    lines = 2 * (3 * LANES * coarse_slots + 1) + slots + 4
     face = jax.ShapeDtypeStruct((slots, rows, width), BF16)
     return pl.pallas_call(
         functools.partial(coarse_kernel, coarse_slots),
         out_shape=(jax.ShapeDtypeStruct(enc.shape, BF16), face, face),
-        in_specs=[SMEM] + [VMEM] * 11,
+        in_specs=[VMEM] * 12,
         out_specs=(VMEM, VMEM, VMEM),
         scratch_shapes=[
             pltpu.VMEM((total, width), BF16),
@@ -558,7 +582,6 @@
     slots, edge, _, _, width = features.shape
     coarse_slots = coarse_nbr.shape[0]
     size = lax.axis_size("gx")
-    position = lax.axis_index("gx")
 
     def swap(value, partner):
         pairs = [(i, partner(i)) for i in range(size) if 0 <= partner(i) < size]
@@ -578,14 +601,13 @@
 
     x = features.reshape(slots, edge, edge * edge, width)
     flat = [w.reshape(27 * width, width) for w in (enc_fine_w, enc_coarse_w, dec_coarse_w, dec_fine_w)]
-    info = position.astype(jnp.int32).reshape(1, 1)
-    near, far, meta, codes, x, first_w = first(
-        info, x, flat[0], fine_nbr, fine_send[0], fine_parent.reshape(1, slots), coarse_child, coarse_nbr
+    near, far, meta, codes, x, first_w, ids, low = first(
+        x, flat[0], fine_nbr, fine_send[0], fine_parent.reshape(1, slots), coarse_child, coarse_nbr
     )
     far = next_chip(far)
     near = core(near)
     main, part = inner(x, meta, first_w)
-    enc, pooled, rim = outer_pool(main, part, near, far, meta, first_w, codes)
+    enc, pooled, rim = outer_pool(main, part, near, far, ids, low, first_w, codes)
 
     rim_c = core(rim)
     rim_z = across_z(jnp.concatenate([rim, rim_c], axis=0))
@@ -600,7 +622,7 @@
     far = next_chip(far)
     near = core(near)
     main, part = inner(dec_in, meta, flat[3])
-    out = outer(main, part, near, far, meta, flat[3])
+    out = outer(main, part, near, far, ids, flat[3])
     return out.reshape(features.shape)
 
 

time: 37.3 us -> 36 us (0.965)
  Pallas kernels: 15.5 us -> 14.2 us
    pallas_call x1, Pallas kernels: 4.29 us -> 3.76 us  [coarse(): pl.pallas_call(functools.partial(coarse_kernel, coarse_slots), out_shape=...]
    pallas_call x1, Pallas kernels: 1.69 us -> 1.25 us  [outer(): pl.pallas_call(outer_kernel, out_shape=jax.ShapeDtypeStruct(main.shape, B...]
    pallas_call x1, Pallas kernels: 1.03 us -> 0.61 us  [outer_pool(): pl.pallas_call(outer_pool_kernel, out_shape=(jax.ShapeDtypeStruct(main.sh...]
  transfers between devices with their start and end apart: 12 -> 12, of which waited for: 6 -> 6; matrix products, arithmetic and copies ran while one was open for 0% -> 0% of each run, Pallas kernels for 19% -> 20%
where the time goes in v5:
time: 36 us; the launch traced here: 35.8 us
  starting transfers between devices  14.6 us (41%)
  Pallas kernels  14.2 us (39%)
  waiting for transfers between devices  6.85 us (19%)
    ppermute x12, starting transfers between devices, swap(): return lax.ppermute(value, 'gx', pairs)  14.6 us
    pallas_call x2, Pallas kernels, inner(): pl.pallas_call(inner_kernel, out_shape=(jax.ShapeDtypeStruct(x.shape, BF1...  6.98 us
    ppermute x12, waiting for transfers between devices, swap(): return lax.ppermute(value, 'gx', pairs)  6.85 us
    pallas_call x1, Pallas kernels, coarse(): pl.pallas_call(functools.partial(coarse_kernel, coarse_slots), out_shape=...  3.76 us
    pallas_call x1, Pallas kernels, first(): pl.pallas_call(first_kernel, out_shape=(face, face, jax.ShapeDtypeStruct(...  1.56 us
    pallas_call x1, Pallas kernels, outer(): pl.pallas_call(outer_kernel, out_shape=jax.ShapeDtypeStruct(main.shape, B...  1.25 us
  transfers between devices with their start and end apart: 12, of which 6 were waited for; matrix products, arithmetic and copies ran while one was open for 0% of the time, Pallas kernels for 20%

profile of v5, /device:TPU:5, one launch (start us, length us, event | category | flops | bytes accessed | tf_op | source)
XLA Modules:
  0.0 35.8 jit_solution(8162247495985406474)
XLA Ops:
  0.0 1.6 %first.1 = (bf16[4,64,128]{2,1,0:T(8,128)(2,1)S(1)}, bf16[4,64,128]{2,1,0:T(8,128)(2,1)S(1)}, s32[8,128]{1,0:T(8,128)S(1)}, bf16[16,128]{1,0:T(8,128)(2,1)S(1)},...) custom-call(bf16[4,8,64,128]{3,2,1,0:T(8,128)(2,1)} %bitcast.13, ...), custom_call_target="tpu_custom_call" | custom-call | bytes 2097152 | tf_op jit(solution)/shard_map/first/pallas_call | solution.py:153
  1.6 0.7 %collective-permute-start = (bf16[4,64,128]{2,1,0:T(8,128)(2,1)S(1)}, bf16[4,64,128]{2,1,0:T(8,128)(2,1)S(1)}, u32[]{:S(2)}, u32[]{:S(2)}) collective-permute-start(bf16[4,64,128]{2,1,0:T(8,128)(2,1)S(1)} %get-tuple-element.26), channel_id=1, source_target_pairs={{0,1},{1,0},{2,3},{3,2},{4,5},{5,4},{6,7},{7,6},{8,9},{9,8},{10,11... | collective-permute-start | bytes 196616 | tf_op jit(solution)/shard_map/ppermute | solution.py:588
  2.3 3.0 %collective-permute-start.1 = (bf16[4,64,128]{2,1,0:T(8,128)(2,1)S(1)}, bf16[4,64,128]{2,1,0:T(8,128)(2,1)S(1)}, u32[]{:S(2)}, u32[]{:S(2)}) collective-permute-start(bf16[4,64,128]{2,1,0:T(8,128)(2,1)S(1)} %get-tuple-element.27), channel_id=1, source_target_pairs={{1,2},{2,1},{3,4},{4,3},{5,6},{6,5},{7,8},{8,7},{9,10},{10,9},{11,... | collective-permute-start | bytes 196616 | tf_op jit(solution)/shard_map/ppermute | solution.py:588
  5.4 3.5 %inner.2 = (bf16[4,8,64,128]{3,2,1,0:T(8,128)(2,1)S(1)}, f32[4,2,64,128]{3,2,1,0:T(8,128)S(1)}) custom-call(s32[8,128]{1,0:T(8,128)S(1)} %get-tuple-element.24.nbr.meta_ref, bf16[4,8,64,128]{3,2,1,0:T(8,128)(2,1)S(1)} %get-tuple-element.28.x_ref, bf16[3456,128]{1,0:T(8,128)(2,1)S(1)} %get-tuple-element.29.w_ref), custom_call_target="tpu_custom_call" | custom-call | flops 1811939328 | bytes 4194304 | tf_op jit(solution)/shard_map/inner/pallas_call | solution.py:218
  8.9 0.0 collective-permute-done.near_ref
  8.9 0.0 collective-permute-done.1.far_ref
  8.9 0.0 copy-start.1
  8.9 0.0 copy-start.2
  8.9 0.6 %outer_pool.1 = (bf16[4,8,64,128]{3,2,1,0:T(8,128)(2,1)S(1)}, bf16[272,128]{1,0:T(8,128)(2,1)S(1)}, bf16[144,128]{1,0:T(8,128)(2,1)S(1)}) custom-call(s32[576,128]{1,0:T(8,128)S(1)} %get-tuple-element.23.ids_ref, s32[4,128]{1,0:T(4,128)S(1)} %get-tuple-element.25.low_ref, bf16[4,64,128]{2,1,0:T(8,128)(2,1)S(1)} %collective-permute-done.near_ref, ...), custom_call_target="tpu_custom_call" | custom-call | flops 536870912 | bytes 4194304 | tf_op jit(solution)/shard_map/outer_pool/pallas_call | solution.py:339
  9.5 0.1 collective-permute-start.5
  9.6 1.2 %collective-permute-done.5 = bf16[144,128]{1,0:T(8,128)(2,1)S(1)} collective-permute-done((bf16[144,128]{1,0:T(8,128)(2,1)S(1)}, bf16[144,128]{1,0:T(8,128)(2,1)S(1)}, u32[]{:S(2)}, u32[]{:S(2)}) %collective-permute-start.5) | collective-permute-done | bytes 36896 | tf_op jit(solution)/shard_map/ppermute | solution.py:588
  10.8 3.2 %collective-permute-start.6 = (bf16[288,128]{1,0:T(8,128)(2,1)S(1)}, bf16[288,128]{1,0:T(8,128)(2,1)S(1)}, u32[]{:S(2)}, u32[]{:S(2)}) collective-permute-start(bf16[288,128]{1,0:T(8,128)(2,1)S(1)} %pad_maximum_fusion), channel_id=1, source_target_pairs={{1,4},{3,6},{4,1},{5,8},{6,3},{7,10},{8,5},{9,12},{10,7},{11,14},{... | collective-permute-start | bytes 221192 | tf_op jit(solution)/shard_map/ppermute | solution.py:588
  14.1 2.4 %collective-permute-done.6.z_ref = bf16[288,128]{1,0:T(8,128)(2,1)S(1)} collective-permute-done((bf16[288,128]{1,0:T(8,128)(2,1)S(1)}, bf16[288,128]{1,0:T(8,128)(2,1)S(1)}, u32[]{:S(2)}, u32[]{:S(2)}) %collective-permute-start.6) | collective-permute-done | bytes 73760 | tf_op jit(solution)/shard_map/ppermute | solution.py:588
  16.5 0.5 %collective-permute-start.7 = (bf16[288,128]{1,0:T(8,128)(2,1)S(1)}, bf16[288,128]{1,0:T(8,128)(2,1)S(1)}, u32[]{:S(2)}, u32[]{:S(2)}) collective-permute-start(bf16[288,128]{1,0:T(8,128)(2,1)S(1)} %collective-permute-done.6.z_ref), channel_id=1, source_target_pairs={{0,2},{1,3},{2,0},{3,1},{4,6},{5,7},{6,4},{7,5},{8,10},{9,11},{10,... | collective-permute-start | bytes 221192 | tf_op jit(solution)/shard_map/ppermute | solution.py:588
  17.0 0.9 %collective-permute-start.3 = (bf16[272,128]{1,0:T(8,128)(2,1)S(1)}, bf16[272,128]{1,0:T(8,128)(2,1)S(1)}, u32[]{:S(2)}, u32[]{:S(2)}) collective-permute-start(bf16[272,128]{1,0:T(8,128)(2,1)S(1)} %get-tuple-element.33.own_ref), channel_id=1, source_target_pairs={{0,2},{1,3},{2,0},{3,1},{4,6},{5,7},{6,4},{7,5},{8,10},{9,11},{10,... | collective-permute-start | bytes 208904 | tf_op jit(solution)/shard_map/ppermute | solution.py:588
  17.9 0.0 collective-permute-start.8
  17.9 1.7 %collective-permute-done.7.zy_ref = bf16[288,128]{1,0:T(8,128)(2,1)S(1)} collective-permute-done((bf16[288,128]{1,0:T(8,128)(2,1)S(1)}, bf16[288,128]{1,0:T(8,128)(2,1)S(1)}, u32[]{:S(2)}, u32[]{:S(2)}) %collective-permute-start.7) | collective-permute-done | bytes 73760 | tf_op jit(solution)/shard_map/ppermute | solution.py:588
  19.7 0.0 collective-permute-start.9
  19.7 0.5 %collective-permute-start.2 = (bf16[272,128]{1,0:T(8,128)(2,1)S(1)}, bf16[272,128]{1,0:T(8,128)(2,1)S(1)}, u32[]{:S(2)}, u32[]{:S(2)}) collective-permute-start(bf16[272,128]{1,0:T(8,128)(2,1)S(1)} %get-tuple-element.33.own_ref), channel_id=1, source_target_pairs={{0,1},{1,0},{2,3},{3,2},{4,5},{5,4},{6,7},{7,6},{8,9},{9,8},{10,11... | collective-permute-start | bytes 208904 | tf_op jit(solution)/shard_map/ppermute | solution.py:588
  20.2 0.2 collective-permute-done.3.y_ref
  20.4 0.0 collective-permute-start.4
  20.4 0.7 %collective-permute-done.2.core_ref = bf16[272,128]{1,0:T(8,128)(2,1)S(1)} collective-permute-done((bf16[272,128]{1,0:T(8,128)(2,1)S(1)}, bf16[272,128]{1,0:T(8,128)(2,1)S(1)}, u32[]{:S(2)}, u32[]{:S(2)}) %collective-permute-start.2) | collective-permute-done | bytes 69664 | tf_op jit(solution)/shard_map/ppermute | solution.py:588
  21.1 0.6 %collective-permute-done.4.yc_ref = bf16[272,128]{1,0:T(8,128)(2,1)S(1)} collective-permute-done((bf16[272,128]{1,0:T(8,128)(2,1)S(1)}, bf16[272,128]{1,0:T(8,128)(2,1)S(1)}, u32[]{:S(2)}, u32[]{:S(2)}) %collective-permute-start.4) | collective-permute-done | bytes 69664 | tf_op jit(solution)/shard_map/ppermute | solution.py:588
  21.7 0.0 collective-permute-done.8.zc_ref
  21.7 0.0 collective-permute-done.9.zyc_ref
  21.7 0.0 copy-done.1
  21.7 0.0 copy-done.2
  21.7 0.0 copy-start
  21.7 3.8 %coarse.1 = (bf16[4,8,64,128]{3,2,1,0:T(8,128)(2,1)S(1)}, bf16[4,64,128]{2,1,0:T(8,128)(2,1)S(1)}, bf16[4,64,128]{2,1,0:T(8,128)(2,1)S(1)}) custom-call(s32[8,128]{1,0:T(8,128)S(1)} %get-tuple-element.24.nbr.meta_ref, bf16[272,128]{1,0:T(8,128)(2,1)S(1)} %get-tuple-element.33.own_ref, bf16[272,128]{1,0:T(8,128)(2,1)S(1)} %collective-permute-done.2.core_ref, ...), custom_call_target="tpu_custom_call" | custom-call | flops 2147483648 | bytes 8388608 | tf_op jit(solution)/shard_map/coarse/pallas_call | solution.py:547
  25.5 0.2 collective-permute-start.10
  25.7 5.3 %collective-permute-start.11 = (bf16[4,64,128]{2,1,0:T(8,128)(2,1)S(1)}, bf16[4,64,128]{2,1,0:T(8,128)(2,1)S(1)}, u32[]{:S(2)}, u32[]{:S(2)}) collective-permute-start(bf16[4,64,128]{2,1,0:T(8,128)(2,1)S(1)} %get-tuple-element.37), channel_id=1, source_target_pairs={{1,2},{2,1},{3,4},{4,3},{5,6},{6,5},{7,8},{8,7},{9,10},{10,9},{11,... | collective-permute-start | bytes 196616 | tf_op jit(solution)/shard_map/ppermute | solution.py:588
  31.0 0.0 copy-done
  31.0 3.5 %inner.3 = (bf16[4,8,64,128]{3,2,1,0:T(8,128)(2,1)S(1)}, f32[4,2,64,128]{3,2,1,0:T(8,128)S(1)}) custom-call(s32[8,128]{1,0:T(8,128)S(1)} %get-tuple-element.24.nbr.meta_ref, bf16[4,8,64,128]{3,2,1,0:T(8,128)(2,1)S(1)} %get-tuple-element.38.x_ref, bf16[3456,128]{1,0:T(8,128)(2,1)S(1)} %bitcast.8), custom_call_target="tpu_custom_call" | custom-call | flops 1811939328 | bytes 4194304 | tf_op jit(solution)/shard_map/inner/pallas_call | solution.py:218
  34.5 0.0 collective-permute-done.10.near_ref
  34.5 0.0 collective-permute-done.11.far_ref
  34.5 1.2 %outer.1 = bf16[4,8,64,128]{3,2,1,0:T(8,128)(2,1)} custom-call(s32[576,128]{1,0:T(8,128)S(1)} %get-tuple-element.23.ids_ref, bf16[4,64,128]{2,1,0:T(8,128)(2,1)S(1)} %collective-permute-done.10.near_ref, bf16[4,64,128]{2,1,0:T(8,128)(2,1)S(1)} %collective-permute-done.11.far_ref, f32[4,2,64,128]{3,2,1,0:T(8,128)S(1)} %get-tuple-element.39.part_ref, ...), custom_call_target="tpu_custom_call" | custom-call | flops 536870912 | bytes 4194304 | tf_op jit(solution)/shard_map/outer/pallas_call | solution.py:298
  (1 shorter events, 0.0 us)
Async XLA Ops:
  1.6 7.3 %collective-permute-start = (bf16[4,64,128]{2,1,0:T(8,128)(2,1)S(1)}, bf16[4,64,128]{2,1,0:T(8,128)(2,1)S(1)}, u32[]{:S(2)}, u32[]{:S(2)}) collective-permute-start(bf16[4,64,128]{2,1,0:T(8,128)(2,1)S(1)} %get-tuple-element.26), channel_id=1, source_target_pairs={{0,1},{1,0},{2,3},{3,2},{4,5},{5,4},{6,7},{7,6},{8,9},{9,8},{10,11... | collective-permute-start | bytes 196616 | tf_op jit(solution)/shard_map/ppermute | solution.py:588
  2.3 6.6 %collective-permute-start.1 = (bf16[4,64,128]{2,1,0:T(8,128)(2,1)S(1)}, bf16[4,64,128]{2,1,0:T(8,128)(2,1)S(1)}, u32[]{:S(2)}, u32[]{:S(2)}) collective-permute-start(bf16[4,64,128]{2,1,0:T(8,128)(2,1)S(1)} %get-tuple-element.27), channel_id=1, source_target_pairs={{1,2},{2,1},{3,4},{4,3},{5,6},{6,5},{7,8},{8,7},{9,10},{10,9},{11,... | collective-permute-start | bytes 196616 | tf_op jit(solution)/shard_map/ppermute | solution.py:588
  8.9 12.8 %copy-start.1 = (bf16[27,128,128]{2,1,0:T(8,128)(2,1)S(1)}, bf16[27,128,128]{2,1,0:T(8,128)(2,1)}, u32[]{:S(2)}) copy-start(bf16[27,128,128]{2,1,0:T(8,128)(2,1)} %param.17) | copy-start | bytes 2654212
  8.9 12.8 %copy-start.2 = (bf16[27,128,128]{2,1,0:T(8,128)(2,1)S(1)}, bf16[27,128,128]{2,1,0:T(8,128)(2,1)}, u32[]{:S(2)}) copy-start(bf16[27,128,128]{2,1,0:T(8,128)(2,1)} %param.18) | copy-start | bytes 2654212
  9.5 1.3 %collective-permute-start.5 = (bf16[144,128]{1,0:T(8,128)(2,1)S(1)}, bf16[144,128]{1,0:T(8,128)(2,1)S(1)}, u32[]{:S(2)}, u32[]{:S(2)}) collective-permute-start(bf16[144,128]{1,0:T(8,128)(2,1)S(1)} %get-tuple-element.34), channel_id=1, source_target_pairs={{0,1},{1,0},{2,3},{3,2},{4,5},{5,4},{6,7},{7,6},{8,9},{9,8},{10,11... | collective-permute-start | bytes 110600 | tf_op jit(solution)/shard_map/ppermute | solution.py:588
  10.8 5.7 %collective-permute-start.6 = (bf16[288,128]{1,0:T(8,128)(2,1)S(1)}, bf16[288,128]{1,0:T(8,128)(2,1)S(1)}, u32[]{:S(2)}, u32[]{:S(2)}) collective-permute-start(bf16[288,128]{1,0:T(8,128)(2,1)S(1)} %pad_maximum_fusion), channel_id=1, source_target_pairs={{1,4},{3,6},{4,1},{5,8},{6,3},{7,10},{8,5},{9,12},{10,7},{11,14},{... | collective-permute-start | bytes 221192 | tf_op jit(solution)/shard_map/ppermute | solution.py:588
  16.5 3.2 %collective-permute-start.7 = (bf16[288,128]{1,0:T(8,128)(2,1)S(1)}, bf16[288,128]{1,0:T(8,128)(2,1)S(1)}, u32[]{:S(2)}, u32[]{:S(2)}) collective-permute-start(bf16[288,128]{1,0:T(8,128)(2,1)S(1)} %collective-permute-done.6.z_ref), channel_id=1, source_target_pairs={{0,2},{1,3},{2,0},{3,1},{4,6},{5,7},{6,4},{7,5},{8,10},{9,11},{10,... | collective-permute-start | bytes 221192 | tf_op jit(solution)/shard_map/ppermute | solution.py:588
  17.0 3.4 %collective-permute-start.3 = (bf16[272,128]{1,0:T(8,128)(2,1)S(1)}, bf16[272,128]{1,0:T(8,128)(2,1)S(1)}, u32[]{:S(2)}, u32[]{:S(2)}) collective-permute-start(bf16[272,128]{1,0:T(8,128)(2,1)S(1)} %get-tuple-element.33.own_ref), channel_id=1, source_target_pairs={{0,2},{1,3},{2,0},{3,1},{4,6},{5,7},{6,4},{7,5},{8,10},{9,11},{10,... | collective-permute-start | bytes 208904 | tf_op jit(solution)/shard_map/ppermute | solution.py:588
  17.9 3.7 %collective-permute-start.8 = (bf16[288,128]{1,0:T(8,128)(2,1)S(1)}, bf16[288,128]{1,0:T(8,128)(2,1)S(1)}, u32[]{:S(2)}, u32[]{:S(2)}) collective-permute-start(bf16[288,128]{1,0:T(8,128)(2,1)S(1)} %collective-permute-done.6.z_ref), channel_id=1, source_target_pairs={{0,1},{1,0},{2,3},{3,2},{4,5},{5,4},{6,7},{7,6},{8,9},{9,8},{10,11... | collective-permute-start | bytes 221192 | tf_op jit(solution)/shard_map/ppermute | solution.py:588
  19.7 2.0 %collective-permute-start.9 = (bf16[288,128]{1,0:T(8,128)(2,1)S(1)}, bf16[288,128]{1,0:T(8,128)(2,1)S(1)}, u32[]{:S(2)}, u32[]{:S(2)}) collective-permute-start(bf16[288,128]{1,0:T(8,128)(2,1)S(1)} %collective-permute-done.7.zy_ref), channel_id=1, source_target_pairs={{0,1},{1,0},{2,3},{3,2},{4,5},{5,4},{6,7},{7,6},{8,9},{9,8},{10,11... | collective-permute-start | bytes 221192 | tf_op jit(solution)/shard_map/ppermute | solution.py:588
  19.7 1.4 %collective-permute-start.2 = (bf16[272,128]{1,0:T(8,128)(2,1)S(1)}, bf16[272,128]{1,0:T(8,128)(2,1)S(1)}, u32[]{:S(2)}, u32[]{:S(2)}) collective-permute-start(bf16[272,128]{1,0:T(8,128)(2,1)S(1)} %get-tuple-element.33.own_ref), channel_id=1, source_target_pairs={{0,1},{1,0},{2,3},{3,2},{4,5},{5,4},{6,7},{7,6},{8,9},{9,8},{10,11... | collective-permute-start | bytes 208904 | tf_op jit(solution)/shard_map/ppermute | solution.py:588
  20.4 1.3 %collective-permute-start.4 = (bf16[272,128]{1,0:T(8,128)(2,1)S(1)}, bf16[272,128]{1,0:T(8,128)(2,1)S(1)}, u32[]{:S(2)}, u32[]{:S(2)}) collective-permute-start(bf16[272,128]{1,0:T(8,128)(2,1)S(1)} %collective-permute-done.3.y_ref), channel_id=1, source_target_pairs={{0,1},{1,0},{2,3},{3,2},{4,5},{5,4},{6,7},{7,6},{8,9},{9,8},{10,11... | collective-permute-start | bytes 208904 | tf_op jit(solution)/shard_map/ppermute | solution.py:588
  21.7 9.3 %copy-start = (bf16[27,128,128]{2,1,0:T(8,128)(2,1)S(1)}, bf16[27,128,128]{2,1,0:T(8,128)(2,1)}, u32[]{:S(2)}) copy-start(bf16[27,128,128]{2,1,0:T(8,128)(2,1)} %param.19) | copy-start | bytes 2654212
  25.5 9.0 %collective-permute-start.10 = (bf16[4,64,128]{2,1,0:T(8,128)(2,1)S(1)}, bf16[4,64,128]{2,1,0:T(8,128)(2,1)S(1)}, u32[]{:S(2)}, u32[]{:S(2)}) collective-permute-start(bf16[4,64,128]{2,1,0:T(8,128)(2,1)S(1)} %get-tuple-element.36), channel_id=1, source_target_pairs={{0,1},{1,0},{2,3},{3,2},{4,5},{5,4},{6,7},{7,6},{8,9},{9,8},{10,11... | collective-permute-start | bytes 196616 | tf_op jit(solution)/shard_map/ppermute | solution.py:588
  25.7 8.8 %collective-permute-start.11 = (bf16[4,64,128]{2,1,0:T(8,128)(2,1)S(1)}, bf16[4,64,128]{2,1,0:T(8,128)(2,1)S(1)}, u32[]{:S(2)}, u32[]{:S(2)}) collective-permute-start(bf16[4,64,128]{2,1,0:T(8,128)(2,1)S(1)} %get-tuple-element.37), channel_id=1, source_target_pairs={{1,2},{2,1},{3,4},{4,3},{5,6},{6,5},{7,8},{8,7},{9,10},{10,9},{11,... | collective-permute-start | bytes 196616 | tf_op jit(solution)/shard_map/ppermute | solution.py:588

commit v6 on v5

--- a/solution.py
+++ b/solution.py
@@ -17,42 +17,12 @@
 BF16 = jnp.bfloat16
 F32 = jnp.float32
 VMEM = pl.BlockSpec(memory_space=pltpu.VMEM)
-SMEM = pl.BlockSpec(memory_space=pltpu.SMEM)
 HBM = pl.BlockSpec(memory_space=pltpu.HBM)
 PARAMS = pltpu.CompilerParams(vmem_limit_bytes=16 << 20)
 
 
 def tap(dx, dy, dz):
     return 9 * (dx + 1) + 3 * (dy + 1) + dz + 1
-
-
-def z_shifts(center, below, above):
-    edge = center.shape[1]
-    z = lax.broadcasted_iota(jnp.int32, center.shape, 1)
-    down = jnp.where(z == 0, pltpu.roll(below, 1, 1), pltpu.roll(center, 1, 1))
-    up = jnp.where(z == edge - 1, pltpu.roll(above, edge - 1, 1), pltpu.roll(center, edge - 1, 1))
-    return down, center, up
-
-
-def columns(fetch, edge):
-    parts = []
-    for dy in OFFSETS:
-        triple = [fetch(dy, dz) for dz in (0, -1, 1)]
-        planes, rows, _, width = triple[0].shape
-        flat = [v.reshape(planes * rows, edge, width) for v in triple]
-        parts.append([s.reshape(planes, rows, edge, width) for s in z_shifts(*flat)])
-    return [jnp.concatenate([part[k] for part in parts], axis=1) for k in range(3)]
-
-
-def y_rows(load, dy, edge):
-    if dy == 0:
-        value = load(0, edge * edge)
-    elif dy < 0:
-        value = load(edge * edge - 2 * edge, 2 * edge)[:, edge:]
-    else:
-        value = load(0, 2 * edge)[:, :edge]
-    planes, rows, width = value.shape
-    return value.reshape(planes, rows // edge, edge, width)
 
 
 def pair_weights(w_ref, dxs, width):
@@ -126,7 +96,7 @@
         low_ref[b : b + 1] = jnp.where((parent & 4) == 0, 1, 0)
     z = lax.broadcasted_iota(jnp.int32, (edge, width), 0)
     line = 0
-    for dx in (-1, 1):
+    for dx in (-1, 1, 0):
         for b in range(slots):
             for dy in OFFSETS:
                 wide = [
@@ -159,7 +129,7 @@
             jax.ShapeDtypeStruct((TILE, width), BF16),
             jax.ShapeDtypeStruct(x.shape, BF16),
             jax.ShapeDtypeStruct(weights.shape, BF16),
-            jax.ShapeDtypeStruct((2 * slots * 9 * edge, width), jnp.int32),
+            jax.ShapeDtypeStruct((3 * slots * 9 * edge, width), jnp.int32),
             jax.ShapeDtypeStruct((slots, width), jnp.int32),
         ),
         in_specs=[HBM] * 7,
@@ -173,24 +143,36 @@
     )(*[stay(v) for v in (x, weights, nbr, send, parent, child, around)])
 
 
-def inner_kernel(nbr, x_ref, w_ref, out_ref, part_ref, cols):
+def inner_kernel(ids_ref, x_ref, w_ref, out_ref, part_ref, cols, stack):
     slots, edge, _, width = x_ref.shape
     pairs = edge // 2
     empty = jnp.zeros((slots, 4, 3, pairs * edge, width), BF16)
     cols[:, :, :, 0] = empty
     cols[:, :, :, edge + 1] = empty
+    for b in range(slots):
+        value = x_ref[b].astype(F32).reshape(edge * edge, edge, width)
+        for k, turn in enumerate((1, 0, edge - 1)):
+            moved = pltpu.roll(value, turn, 1) if turn else value
+            stack[k, b] = moved.reshape(edge, edge, edge, width)
     weights = pair_weights(w_ref, range(3), width)
     for group in range(0, slots, GROUP):
         bricks = []
         for b in range(group, group + GROUP):
-
-            def fetch(dy, dz):
-                slot = nbr[b, tap(0, dy, dz)]
-                held = jnp.maximum(slot, 0)
-                value = y_rows(lambda r, n: x_ref[held, :, r : r + n, :].astype(F32), dy, edge)
-                return jnp.where(slot >= 0, value, 0.0)
-
-            for k, full in enumerate(columns(fetch, edge)):
+            for k in range(3):
+                parts = []
+                for dy in OFFSETS:
+                    line = (((2 * slots + b) * 3 + dy + 1) * 3 + k) * edge
+                    ids = ids_ref[line : line + edge][None, None]
+                    first, count = {-1: (edge - 1, 1), 0: (0, edge), 1: (0, 1)}[dy]
+                    if dy == 0 and k == 1:
+                        value = jnp.where(ids == b, stack[k, b], 0.0)
+                    else:
+                        value = jnp.zeros((edge, count, edge, width), F32)
+                        for slot in range(slots):
+                            held = stack[k, slot, :, first : first + count]
+                            value = jnp.where(ids == slot, held, value)
+                    parts.append(value)
+                full = jnp.concatenate(parts, axis=1)
                 for j in range(4):
                     cols[b, j, k, 1 : edge + 1] = pair_rows(full, j, pairs)
             taps = []
@@ -213,7 +195,7 @@
             part_ref[b, 1] = total[edge - 1]
 
 
-def inner(x, nbr, weights):
+def inner(x, ids, weights):
     slots, edge, rows, width = x.shape
     return pl.pallas_call(
         inner_kernel,
@@ -221,10 +203,11 @@
             jax.ShapeDtypeStruct(x.shape, BF16),
             jax.ShapeDtypeStruct((slots, 2, rows, width), F32),
         ),
-        in_specs=[SMEM, VMEM, VMEM],
+        in_specs=[VMEM, VMEM, VMEM],
         out_specs=(VMEM, VMEM),
         scratch_shapes=[
             pltpu.VMEM((slots, 4, 3, edge + 2, rows // 2, width), BF16),
+            pltpu.VMEM((3, slots, edge, edge, edge, width), F32),
         ],
         compiler_params=PARAMS,
         cost_estimate=pl.CostEstimate(
@@ -233,7 +216,7 @@
             transcendentals=0,
         ),
         name="inner",
-    )(nbr, x, weights)
+    )(ids, x, weights)
 
 
 def outer_planes(ids_ref, near_ref, far_ref, part_ref, w_ref, out_ref, stack, edge):
@@ -606,7 +589,7 @@
     )
     far = next_chip(far)
     near = core(near)
-    main, part = inner(x, meta, first_w)
+    main, part = inner(x, ids, first_w)
     enc, pooled, rim = outer_pool(main, part, near, far, ids, low, first_w, codes)
 
     rim_c = core(rim)
@@ -621,7 +604,7 @@
     dec_in, near, far = coarse(meta, blocks, enc, flat[1], flat[2], coarse_slots)
     far = next_chip(far)
     near = core(near)
-    main, part = inner(dec_in, meta, flat[3])
+    main, part = inner(dec_in, ids, flat[3])
     out = outer(main, part, near, far, ids, flat[3])
     return out.reshape(features.shape)
 

time: 36 us -> 35.6 us (0.989); the launches traced: 35.8 us -> 35 us
  Pallas kernels: 14.2 us -> 13.2 us
  waiting for transfers between devices: 6.85 us -> 7.22 us
    pallas_call x2, Pallas kernels: 6.98 us -> 6.05 us  [inner(): pl.pallas_call(inner_kernel, out_shape=(jax.ShapeDtypeStruct(x.shape, BF1...]
    ppermute x12, waiting for transfers between devices: 6.85 us -> 7.22 us  [swap(): return lax.ppermute(value, 'gx', pairs)]
  transfers between devices with their start and end apart: 12 -> 12, of which waited for: 6 -> 7; matrix products, arithmetic and copies ran while one was open for 0% -> 0% of each run, Pallas kernels for 20% -> 17%
where the time goes in v6:
time: 35.6 us; the launch traced here: 35 us
  starting transfers between devices  14.4 us (40%)
  Pallas kernels  13.2 us (37%)
  waiting for transfers between devices  7.22 us (20%)
    ppermute x12, starting transfers between devices, swap(): return lax.ppermute(value, 'gx', pairs)  14.4 us
    ppermute x12, waiting for transfers between devices, swap(): return lax.ppermute(value, 'gx', pairs)  7.22 us
    pallas_call x2, Pallas kernels, inner(): pl.pallas_call(inner_kernel, out_shape=(jax.ShapeDtypeStruct(x.shape, BF1...  6.05 us
    pallas_call x1, Pallas kernels, coarse(): pl.pallas_call(functools.partial(coarse_kernel, coarse_slots), out_shape=...  3.76 us
    pallas_call x1, Pallas kernels, first(): pl.pallas_call(first_kernel, out_shape=(face, face, jax.ShapeDtypeStruct(...  1.56 us
    pallas_call x1, Pallas kernels, outer(): pl.pallas_call(outer_kernel, out_shape=jax.ShapeDtypeStruct(main.shape, B...  1.26 us
  transfers between devices with their start and end apart: 12, of which 7 were waited for; matrix products, arithmetic and copies ran while one was open for 0% of the time, Pallas kernels for 17%

profile of v6, /device:TPU:5, one launch (start us, length us, event | category | flops | bytes accessed | tf_op | source)
XLA Modules:
  0.0 35.0 jit_solution(5520279325336062436)
XLA Ops:
  0.0 1.6 %first.1 = (bf16[4,64,128]{2,1,0:T(8,128)(2,1)S(1)}, bf16[4,64,128]{2,1,0:T(8,128)(2,1)S(1)}, s32[8,128]{1,0:T(8,128)S(1)}, bf16[16,128]{1,0:T(8,128)(2,1)S(1)},...) custom-call(bf16[4,8,64,128]{3,2,1,0:T(8,128)(2,1)} %bitcast.13, ...), custom_call_target="tpu_custom_call" | custom-call | bytes 2097152 | tf_op jit(solution)/shard_map/first/pallas_call | solution.py:123
  1.6 0.7 %collective-permute-start = (bf16[4,64,128]{2,1,0:T(8,128)(2,1)S(1)}, bf16[4,64,128]{2,1,0:T(8,128)(2,1)S(1)}, u32[]{:S(2)}, u32[]{:S(2)}) collective-permute-start(bf16[4,64,128]{2,1,0:T(8,128)(2,1)S(1)} %get-tuple-element.26), channel_id=1, source_target_pairs={{0,1},{1,0},{2,3},{3,2},{4,5},{5,4},{6,7},{7,6},{8,9},{9,8},{10,11... | collective-permute-start | bytes 196616 | tf_op jit(solution)/shard_map/ppermute | solution.py:571
  2.3 3.0 %collective-permute-start.1 = (bf16[4,64,128]{2,1,0:T(8,128)(2,1)S(1)}, bf16[4,64,128]{2,1,0:T(8,128)(2,1)S(1)}, u32[]{:S(2)}, u32[]{:S(2)}) collective-permute-start(bf16[4,64,128]{2,1,0:T(8,128)(2,1)S(1)} %get-tuple-element.27), channel_id=1, source_target_pairs={{1,2},{2,1},{3,4},{4,3},{5,6},{6,5},{7,8},{8,7},{9,10},{10,9},{11,... | collective-permute-start | bytes 196616 | tf_op jit(solution)/shard_map/ppermute | solution.py:571
  5.4 3.0 %inner.2 = (bf16[4,8,64,128]{3,2,1,0:T(8,128)(2,1)S(1)}, f32[4,2,64,128]{3,2,1,0:T(8,128)S(1)}) custom-call(s32[864,128]{1,0:T(8,128)S(1)} %get-tuple-element.23.ids_ref, bf16[4,8,64,128]{3,2,1,0:T(8,128)(2,1)S(1)} %get-tuple-element.28.x_ref, bf16[3456,128]{1,0:T(8,128)(2,1)S(1)} %get-tuple-element.29.w_ref), custom_call_target="tpu_custom_call" | custom-call | flops 1811939328 | bytes 4194304 | tf_op jit(solution)/shard_map/inner/pallas_call | solution.py:200
  8.4 0.0 collective-permute-done.near_ref
  8.4 0.4 %collective-permute-done.1.far_ref = bf16[4,64,128]{2,1,0:T(8,128)(2,1)S(1)} collective-permute-done((bf16[4,64,128]{2,1,0:T(8,128)(2,1)S(1)}, bf16[4,64,128]{2,1,0:T(8,128)(2,1)S(1)}, u32[]{:S(2)}, u32[]{:S(2)}) %collective-permute-start.1) | collective-permute-done | bytes 65568 | tf_op jit(solution)/shard_map/ppermute | solution.py:571
  8.8 0.0 copy-start.1
  8.8 0.0 copy-start.2
  8.8 0.6 %outer_pool.1 = (bf16[4,8,64,128]{3,2,1,0:T(8,128)(2,1)S(1)}, bf16[272,128]{1,0:T(8,128)(2,1)S(1)}, bf16[144,128]{1,0:T(8,128)(2,1)S(1)}) custom-call(s32[864,128]{1,0:T(8,128)S(1)} %get-tuple-element.23.ids_ref, s32[4,128]{1,0:T(4,128)S(1)} %get-tuple-element.25.low_ref, bf16[4,64,128]{2,1,0:T(8,128)(2,1)S(1)} %collective-permute-done.near_ref, ...), custom_call_target="tpu_custom_call" | custom-call | flops 536870912 | bytes 4194304 | tf_op jit(solution)/shard_map/outer_pool/pallas_call | solution.py:322
  9.4 0.1 collective-permute-start.5
  9.5 1.2 %collective-permute-done.5 = bf16[144,128]{1,0:T(8,128)(2,1)S(1)} collective-permute-done((bf16[144,128]{1,0:T(8,128)(2,1)S(1)}, bf16[144,128]{1,0:T(8,128)(2,1)S(1)}, u32[]{:S(2)}, u32[]{:S(2)}) %collective-permute-start.5) | collective-permute-done | bytes 36896 | tf_op jit(solution)/shard_map/ppermute | solution.py:571
  10.7 3.2 %collective-permute-start.6 = (bf16[288,128]{1,0:T(8,128)(2,1)S(1)}, bf16[288,128]{1,0:T(8,128)(2,1)S(1)}, u32[]{:S(2)}, u32[]{:S(2)}) collective-permute-start(bf16[288,128]{1,0:T(8,128)(2,1)S(1)} %pad_maximum_fusion), channel_id=1, source_target_pairs={{1,4},{3,6},{4,1},{5,8},{6,3},{7,10},{8,5},{9,12},{10,7},{11,14},{... | collective-permute-start | bytes 221192 | tf_op jit(solution)/shard_map/ppermute | solution.py:571
  13.9 2.4 %collective-permute-done.6.z_ref = bf16[288,128]{1,0:T(8,128)(2,1)S(1)} collective-permute-done((bf16[288,128]{1,0:T(8,128)(2,1)S(1)}, bf16[288,128]{1,0:T(8,128)(2,1)S(1)}, u32[]{:S(2)}, u32[]{:S(2)}) %collective-permute-start.6) | collective-permute-done | bytes 73760 | tf_op jit(solution)/shard_map/ppermute | solution.py:571
  16.3 0.2 collective-permute-start.7
  16.5 1.3 %collective-permute-start.3 = (bf16[272,128]{1,0:T(8,128)(2,1)S(1)}, bf16[272,128]{1,0:T(8,128)(2,1)S(1)}, u32[]{:S(2)}, u32[]{:S(2)}) collective-permute-start(bf16[272,128]{1,0:T(8,128)(2,1)S(1)} %get-tuple-element.33.own_ref), channel_id=1, source_target_pairs={{0,2},{1,3},{2,0},{3,1},{4,6},{5,7},{6,4},{7,5},{8,10},{9,11},{10,... | collective-permute-start | bytes 208904 | tf_op jit(solution)/shard_map/ppermute | solution.py:571
  17.8 0.0 collective-permute-start.8
  17.8 1.7 %collective-permute-done.7.zy_ref = bf16[288,128]{1,0:T(8,128)(2,1)S(1)} collective-permute-done((bf16[288,128]{1,0:T(8,128)(2,1)S(1)}, bf16[288,128]{1,0:T(8,128)(2,1)S(1)}, u32[]{:S(2)}, u32[]{:S(2)}) %collective-permute-start.7) | collective-permute-done | bytes 73760 | tf_op jit(solution)/shard_map/ppermute | solution.py:571
  19.6 0.0 collective-permute-start.9
  19.6 0.5 %collective-permute-start.2 = (bf16[272,128]{1,0:T(8,128)(2,1)S(1)}, bf16[272,128]{1,0:T(8,128)(2,1)S(1)}, u32[]{:S(2)}, u32[]{:S(2)}) collective-permute-start(bf16[272,128]{1,0:T(8,128)(2,1)S(1)} %get-tuple-element.33.own_ref), channel_id=1, source_target_pairs={{0,1},{1,0},{2,3},{3,2},{4,5},{5,4},{6,7},{7,6},{8,9},{9,8},{10,11... | collective-permute-start | bytes 208904 | tf_op jit(solution)/shard_map/ppermute | solution.py:571
  20.1 0.2 collective-permute-done.3.y_ref
  20.3 0.0 collective-permute-start.4
  20.3 0.7 %collective-permute-done.2.core_ref = bf16[272,128]{1,0:T(8,128)(2,1)S(1)} collective-permute-done((bf16[272,128]{1,0:T(8,128)(2,1)S(1)}, bf16[272,128]{1,0:T(8,128)(2,1)S(1)}, u32[]{:S(2)}, u32[]{:S(2)}) %collective-permute-start.2) | collective-permute-done | bytes 69664 | tf_op jit(solution)/shard_map/ppermute | solution.py:571
  21.0 0.6 %collective-permute-done.4.yc_ref = bf16[272,128]{1,0:T(8,128)(2,1)S(1)} collective-permute-done((bf16[272,128]{1,0:T(8,128)(2,1)S(1)}, bf16[272,128]{1,0:T(8,128)(2,1)S(1)}, u32[]{:S(2)}, u32[]{:S(2)}) %collective-permute-start.4) | collective-permute-done | bytes 69664 | tf_op jit(solution)/shard_map/ppermute | solution.py:571
  21.6 0.0 collective-permute-done.8.zc_ref
  21.6 0.0 collective-permute-done.9.zyc_ref
  21.6 0.0 copy-done.1
  21.6 0.0 copy-done.2
  21.6 0.0 copy-start
  21.6 3.8 %coarse.1 = (bf16[4,8,64,128]{3,2,1,0:T(8,128)(2,1)S(1)}, bf16[4,64,128]{2,1,0:T(8,128)(2,1)S(1)}, bf16[4,64,128]{2,1,0:T(8,128)(2,1)S(1)}) custom-call(s32[8,128]{1,0:T(8,128)S(1)} %get-tuple-element.24.meta_ref, bf16[272,128]{1,0:T(8,128)(2,1)S(1)} %get-tuple-element.33.own_ref, bf16[272,128]{1,0:T(8,128)(2,1)S(1)} %collective-permute-done.2.core_ref, ...), custom_call_target="tpu_custom_call" | custom-call | flops 2147483648 | bytes 8388608 | tf_op jit(solution)/shard_map/coarse/pallas_call | solution.py:530
  25.4 0.2 collective-permute-start.10
  25.6 5.1 %collective-permute-start.11 = (bf16[4,64,128]{2,1,0:T(8,128)(2,1)S(1)}, bf16[4,64,128]{2,1,0:T(8,128)(2,1)S(1)}, u32[]{:S(2)}, u32[]{:S(2)}) collective-permute-start(bf16[4,64,128]{2,1,0:T(8,128)(2,1)S(1)} %get-tuple-element.37), channel_id=1, source_target_pairs={{1,2},{2,1},{3,4},{4,3},{5,6},{6,5},{7,8},{8,7},{9,10},{10,9},{11,... | collective-permute-start | bytes 196616 | tf_op jit(solution)/shard_map/ppermute | solution.py:571
  30.7 0.0 copy-done
  30.7 3.0 %inner.3 = (bf16[4,8,64,128]{3,2,1,0:T(8,128)(2,1)S(1)}, f32[4,2,64,128]{3,2,1,0:T(8,128)S(1)}) custom-call(s32[864,128]{1,0:T(8,128)S(1)} %get-tuple-element.23.ids_ref, bf16[4,8,64,128]{3,2,1,0:T(8,128)(2,1)S(1)} %get-tuple-element.38.x_ref, bf16[3456,128]{1,0:T(8,128)(2,1)S(1)} %bitcast.8), custom_call_target="tpu_custom_call" | custom-call | flops 1811939328 | bytes 4194304 | tf_op jit(solution)/shard_map/inner/pallas_call | solution.py:200
  33.7 0.0 collective-permute-done.10.near_ref
  33.7 0.0 collective-permute-done.11.far_ref
  33.7 1.3 %outer.1 = bf16[4,8,64,128]{3,2,1,0:T(8,128)(2,1)} custom-call(s32[864,128]{1,0:T(8,128)S(1)} %get-tuple-element.23.ids_ref, bf16[4,64,128]{2,1,0:T(8,128)(2,1)S(1)} %collective-permute-done.10.near_ref, bf16[4,64,128]{2,1,0:T(8,128)(2,1)S(1)} %collective-permute-done.11.far_ref, f32[4,2,64,128]{3,2,1,0:T(8,128)S(1)} %get-tuple-element.39.part_ref, ...), custom_call_target="tpu_custom_call" | custom-call | flops 536870912 | bytes 4194304 | tf_op jit(solution)/shard_map/outer/pallas_call | solution.py:281
  (1 shorter events, 0.0 us)
Async XLA Ops:
  1.6 6.8 %collective-permute-start = (bf16[4,64,128]{2,1,0:T(8,128)(2,1)S(1)}, bf16[4,64,128]{2,1,0:T(8,128)(2,1)S(1)}, u32[]{:S(2)}, u32[]{:S(2)}) collective-permute-start(bf16[4,64,128]{2,1,0:T(8,128)(2,1)S(1)} %get-tuple-element.26), channel_id=1, source_target_pairs={{0,1},{1,0},{2,3},{3,2},{4,5},{5,4},{6,7},{7,6},{8,9},{9,8},{10,11... | collective-permute-start | bytes 196616 | tf_op jit(solution)/shard_map/ppermute | solution.py:571
  2.3 6.5 %collective-permute-start.1 = (bf16[4,64,128]{2,1,0:T(8,128)(2,1)S(1)}, bf16[4,64,128]{2,1,0:T(8,128)(2,1)S(1)}, u32[]{:S(2)}, u32[]{:S(2)}) collective-permute-start(bf16[4,64,128]{2,1,0:T(8,128)(2,1)S(1)} %get-tuple-element.27), channel_id=1, source_target_pairs={{1,2},{2,1},{3,4},{4,3},{5,6},{6,5},{7,8},{8,7},{9,10},{10,9},{11,... | collective-permute-start | bytes 196616 | tf_op jit(solution)/shard_map/ppermute | solution.py:571
  8.8 12.8 %copy-start.1 = (bf16[27,128,128]{2,1,0:T(8,128)(2,1)S(1)}, bf16[27,128,128]{2,1,0:T(8,128)(2,1)}, u32[]{:S(2)}) copy-start(bf16[27,128,128]{2,1,0:T(8,128)(2,1)} %param.17) | copy-start | bytes 2654212
  8.8 12.8 %copy-start.2 = (bf16[27,128,128]{2,1,0:T(8,128)(2,1)S(1)}, bf16[27,128,128]{2,1,0:T(8,128)(2,1)}, u32[]{:S(2)}) copy-start(bf16[27,128,128]{2,1,0:T(8,128)(2,1)} %param.18) | copy-start | bytes 2654212
  9.4 1.3 %collective-permute-start.5 = (bf16[144,128]{1,0:T(8,128)(2,1)S(1)}, bf16[144,128]{1,0:T(8,128)(2,1)S(1)}, u32[]{:S(2)}, u32[]{:S(2)}) collective-permute-start(bf16[144,128]{1,0:T(8,128)(2,1)S(1)} %get-tuple-element.34), channel_id=1, source_target_pairs={{0,1},{1,0},{2,3},{3,2},{4,5},{5,4},{6,7},{7,6},{8,9},{9,8},{10,11... | collective-permute-start | bytes 110600 | tf_op jit(solution)/shard_map/ppermute | solution.py:571
  10.7 5.7 %collective-permute-start.6 = (bf16[288,128]{1,0:T(8,128)(2,1)S(1)}, bf16[288,128]{1,0:T(8,128)(2,1)S(1)}, u32[]{:S(2)}, u32[]{:S(2)}) collective-permute-start(bf16[288,128]{1,0:T(8,128)(2,1)S(1)} %pad_maximum_fusion), channel_id=1, source_target_pairs={{1,4},{3,6},{4,1},{5,8},{6,3},{7,10},{8,5},{9,12},{10,7},{11,14},{... | collective-permute-start | bytes 221192 | tf_op jit(solution)/shard_map/ppermute | solution.py:571
  16.3 3.2 %collective-permute-start.7 = (bf16[288,128]{1,0:T(8,128)(2,1)S(1)}, bf16[288,128]{1,0:T(8,128)(2,1)S(1)}, u32[]{:S(2)}, u32[]{:S(2)}) collective-permute-start(bf16[288,128]{1,0:T(8,128)(2,1)S(1)} %collective-permute-done.6.z_ref), channel_id=1, source_target_pairs={{0,2},{1,3},{2,0},{3,1},{4,6},{5,7},{6,4},{7,5},{8,10},{9,11},{10,... | collective-permute-start | bytes 221192 | tf_op jit(solution)/shard_map/ppermute | solution.py:571
  16.5 3.8 %collective-permute-start.3 = (bf16[272,128]{1,0:T(8,128)(2,1)S(1)}, bf16[272,128]{1,0:T(8,128)(2,1)S(1)}, u32[]{:S(2)}, u32[]{:S(2)}) collective-permute-start(bf16[272,128]{1,0:T(8,128)(2,1)S(1)} %get-tuple-element.33.own_ref), channel_id=1, source_target_pairs={{0,2},{1,3},{2,0},{3,1},{4,6},{5,7},{6,4},{7,5},{8,10},{9,11},{10,... | collective-permute-start | bytes 208904 | tf_op jit(solution)/shard_map/ppermute | solution.py:571
  17.8 3.7 %collective-permute-start.8 = (bf16[288,128]{1,0:T(8,128)(2,1)S(1)}, bf16[288,128]{1,0:T(8,128)(2,1)S(1)}, u32[]{:S(2)}, u32[]{:S(2)}) collective-permute-start(bf16[288,128]{1,0:T(8,128)(2,1)S(1)} %collective-permute-done.6.z_ref), channel_id=1, source_target_pairs={{0,1},{1,0},{2,3},{3,2},{4,5},{5,4},{6,7},{7,6},{8,9},{9,8},{10,11... | collective-permute-start | bytes 221192 | tf_op jit(solution)/shard_map/ppermute | solution.py:571
  19.6 2.0 %collective-permute-start.9 = (bf16[288,128]{1,0:T(8,128)(2,1)S(1)}, bf16[288,128]{1,0:T(8,128)(2,1)S(1)}, u32[]{:S(2)}, u32[]{:S(2)}) collective-permute-start(bf16[288,128]{1,0:T(8,128)(2,1)S(1)} %collective-permute-done.7.zy_ref), channel_id=1, source_target_pairs={{0,1},{1,0},{2,3},{3,2},{4,5},{5,4},{6,7},{7,6},{8,9},{9,8},{10,11... | collective-permute-start | bytes 221192 | tf_op jit(solution)/shard_map/ppermute | solution.py:571
  19.6 1.4 %collective-permute-start.2 = (bf16[272,128]{1,0:T(8,128)(2,1)S(1)}, bf16[272,128]{1,0:T(8,128)(2,1)S(1)}, u32[]{:S(2)}, u32[]{:S(2)}) collective-permute-start(bf16[272,128]{1,0:T(8,128)(2,1)S(1)} %get-tuple-element.33.own_ref), channel_id=1, source_target_pairs={{0,1},{1,0},{2,3},{3,2},{4,5},{5,4},{6,7},{7,6},{8,9},{9,8},{10,11... | collective-permute-start | bytes 208904 | tf_op jit(solution)/shard_map/ppermute | solution.py:571
  20.3 1.3 %collective-permute-start.4 = (bf16[272,128]{1,0:T(8,128)(2,1)S(1)}, bf16[272,128]{1,0:T(8,128)(2,1)S(1)}, u32[]{:S(2)}, u32[]{:S(2)}) collective-permute-start(bf16[272,128]{1,0:T(8,128)(2,1)S(1)} %collective-permute-done.3.y_ref), channel_id=1, source_target_pairs={{0,1},{1,0},{2,3},{3,2},{4,5},{5,4},{6,7},{7,6},{8,9},{9,8},{10,11... | collective-permute-start | bytes 208904 | tf_op jit(solution)/shard_map/ppermute | solution.py:571
  21.6 9.1 %copy-start = (bf16[27,128,128]{2,1,0:T(8,128)(2,1)S(1)}, bf16[27,128,128]{2,1,0:T(8,128)(2,1)}, u32[]{:S(2)}) copy-start(bf16[27,128,128]{2,1,0:T(8,128)(2,1)} %param.19) | copy-start | bytes 2654212
  25.4 8.3 %collective-permute-start.10 = (bf16[4,64,128]{2,1,0:T(8,128)(2,1)S(1)}, bf16[4,64,128]{2,1,0:T(8,128)(2,1)S(1)}, u32[]{:S(2)}, u32[]{:S(2)}) collective-permute-start(bf16[4,64,128]{2,1,0:T(8,128)(2,1)S(1)} %get-tuple-element.36), channel_id=1, source_target_pairs={{0,1},{1,0},{2,3},{3,2},{4,5},{5,4},{6,7},{7,6},{8,9},{9,8},{10,11... | collective-permute-start | bytes 196616 | tf_op jit(solution)/shard_map/ppermute | solution.py:571
  25.6 8.1 %collective-permute-start.11 = (bf16[4,64,128]{2,1,0:T(8,128)(2,1)S(1)}, bf16[4,64,128]{2,1,0:T(8,128)(2,1)S(1)}, u32[]{:S(2)}, u32[]{:S(2)}) collective-permute-start(bf16[4,64,128]{2,1,0:T(8,128)(2,1)S(1)} %get-tuple-element.37), channel_id=1, source_target_pairs={{1,2},{2,1},{3,4},{4,3},{5,6},{6,5},{7,8},{8,7},{9,10},{10,9},{11,... | collective-permute-start | bytes 196616 | tf_op jit(solution)/shard_map/ppermute | solution.py:571

commit v7 on v6

--- a/solution.py
+++ b/solution.py
@@ -9,7 +9,7 @@
 
 
 LANES = 4
-GROUP = 2
+GROUP = 4
 ENC_GROUP = 1
 DEC_GROUP = 4
 TILE = 16
@@ -219,7 +219,7 @@
     )(ids, x, weights)
 
 
-def outer_planes(ids_ref, near_ref, far_ref, part_ref, w_ref, out_ref, stack, edge):
+def outer_planes(ids_ref, near_ref, far_ref, part_ref, w_ref, out_ref, stack, edge, copies=None):
     slots, _, rows, width = part_ref.shape
     pairs = edge // 2
     is_odd = lax.axis_index("gx") & 1
@@ -260,19 +260,19 @@
         for b in range(slots):
             total = part_ref[b, side] + extra[b]
             out_ref[b, plane] = jnp.maximum(total, 0.0).astype(BF16)
+        if copies is not None:
+            copies[side].start()
 
 
 def outer_kernel(ids_ref, near_ref, far_ref, part_ref, w_ref, main_ref, out_hbm, planes, stack, sems):
     edge = main_ref.shape[1]
     inside = pltpu.make_async_copy(main_ref.at[:, 1 : edge - 1], out_hbm.at[:, 1 : edge - 1], sems.at[0])
     inside.start()
-    outer_planes(ids_ref, near_ref, far_ref, part_ref, w_ref, planes, stack, edge)
     copies = [
         pltpu.make_async_copy(planes.at[:, i], out_hbm.at[:, x], sems.at[i + 1])
         for i, x in enumerate((0, edge - 1))
     ]
-    for copy in copies:
-        copy.start()
+    outer_planes(ids_ref, near_ref, far_ref, part_ref, w_ref, planes, stack, edge, copies)
     for copy in copies + [inside]:
         copy.wait()
 
@@ -409,13 +409,16 @@
     origins += [far_rel + (lane ^ i) for i in range(LANES)]
     lines = 3 * LANES * coarse_slots + 1
     codes[...] = jnp.zeros_like(codes)
-    codes[2 * lines : 2 * lines + slots + 4] = meta_ref[...]
+    after = lines + LANES * coarse_slots
+    codes[after : after + 3] = meta_ref[slots : slots + 3]
     for i, (origin, (ref, at, count)) in enumerate(zip(origins, places)):
         line = ref[at + count : at + count + TILE].astype(F32).astype(jnp.int32)
         row = 1 + origin * coarse_slots
         start = 2 * section if i < LANES else jnp.where(origin >= LANES, 3 * section, section)
         codes[pl.ds(row, coarse_slots)] = line[:coarse_slots] * cells + start
-        codes[pl.ds(lines + row, coarse_slots)] = line[coarse_slots : 2 * coarse_slots]
+        if i < LANES:
+            row = lines + (origin - LANES) * coarse_slots
+            codes[pl.ds(row, coarse_slots)] = line[coarse_slots : 2 * coarse_slots]
     copy = pltpu.make_async_copy(codes, table, sem)
     copy.start()
     for i in range(4):
@@ -442,11 +445,11 @@
     regions = []
     masks = []
     for b in range(slots):
-        own = jnp.where(table[2 * lines + slots + 2, b] >= 0, table[2 * lines + slots + 2, b], group_first * 8)
+        own = jnp.where(table[after + 2, b] >= 0, table[after + 2, b], group_first * 8)
         octant = own & 7
         bits = ((octant >> 2) & 1, (octant >> 1) & 1, octant & 1)
         brick = jnp.clip((own >> 3) - group_first, 0, LANES * coarse_slots - 1)
-        home = lines + 1 + LANES * coarse_slots + brick
+        home = lines + brick
         steps = [scale * (2 * bit - 1) for scale, bit in zip((9, 3, 1), bits)]
         numbers = [13, 13 + steps[2]]
         numbers += [number + steps[1] for number in numbers]
@@ -506,7 +509,7 @@
     fines = valid_conv(mids, x_pair_weights(w2_ref, width), (even2, odd2), edge, width, DEC_GROUP)
     is_odd = lane_c == 1
     for b in range(slots):
-        value = jnp.where(table[2 * lines + slots + 2, b] >= 0, fines[b], 0.0).reshape(plane * edge, width)
+        value = jnp.where(table[after + 2, b] >= 0, fines[b], 0.0).reshape(plane * edge, width)
         spread[b, pl.ds(0, plane * edge, stride=2), :] = value
         spread[b, pl.ds(1, plane * edge, stride=2), :] = value
         up = spread[b].reshape(half, half, 2 * edge, width)[:, :, :edge]
@@ -514,8 +517,8 @@
         total = base + up[:, None, :, None]
         total = total.reshape(edge, rows, width).astype(BF16)
         out_ref[b] = total
-        last = jnp.where(table[2 * lines + slots, b] == b, total[edge - 1], 0)
-        head = jnp.where(table[2 * lines + slots + 1, b] == b, total[0], 0)
+        last = jnp.where(table[after, b] == b, total[edge - 1], 0)
+        head = jnp.where(table[after + 1, b] == b, total[0], 0)
         near_ref[b] = jnp.where(is_odd, head, last)
         far_ref[b] = jnp.where(is_odd, last, head)
 
@@ -525,7 +528,7 @@
     half = edge // 2
     inside = edge - 2
     total = 4 * (LANES * slots + 1) * half**3
-    lines = 2 * (3 * LANES * coarse_slots + 1) + slots + 4
+    lines = 4 * LANES * coarse_slots + 4
     face = jax.ShapeDtypeStruct((slots, rows, width), BF16)
     return pl.pallas_call(
         functools.partial(coarse_kernel, coarse_slots),

time: 35.6 us -> 35.4 us (level)
  the two profiles are of different devices: /device:TPU:5 before, /device:TPU:21 now
where the time goes in v7:
time: 35.4 us; the launch traced here: 35.3 us
  starting transfers between devices  13.4 us (38%)
  Pallas kernels  12.7 us (36%)
  waiting for transfers between devices  9.03 us (26%)
    ppermute x12, starting transfers between devices, swap(): return lax.ppermute(value, 'gx', pairs)  13.4 us
    ppermute x12, waiting for transfers between devices, swap(): return lax.ppermute(value, 'gx', pairs)  9.03 us
    pallas_call x2, Pallas kernels, inner(): pl.pallas_call(inner_kernel, out_shape=(jax.ShapeDtypeStruct(x.shape, BF1...  5.62 us
    pallas_call x1, Pallas kernels, coarse(): pl.pallas_call(functools.partial(coarse_kernel, coarse_slots), out_shape=...  3.64 us
    pallas_call x1, Pallas kernels, first(): pl.pallas_call(first_kernel, out_shape=(face, face, jax.ShapeDtypeStruct(...  1.56 us
    pallas_call x1, Pallas kernels, outer(): pl.pallas_call(outer_kernel, out_shape=jax.ShapeDtypeStruct(main.shape, B...  1.25 us
  transfers between devices with their start and end apart: 12, of which 7 were waited for; matrix products, arithmetic and copies ran while one was open for 0% of the time, Pallas kernels for 16%

profile of v7, /device:TPU:21, one launch (start us, length us, event | category | flops | bytes accessed | tf_op | source)
XLA Modules:
  0.0 35.3 jit_solution(10371734718351904344)
XLA Ops:
  0.0 1.6 %first.1 = (bf16[4,64,128]{2,1,0:T(8,128)(2,1)S(1)}, bf16[4,64,128]{2,1,0:T(8,128)(2,1)S(1)}, s32[8,128]{1,0:T(8,128)S(1)}, bf16[16,128]{1,0:T(8,128)(2,1)S(1)},...) custom-call(bf16[4,8,64,128]{3,2,1,0:T(8,128)(2,1)} %bitcast.13, ...), custom_call_target="tpu_custom_call" | custom-call | bytes 2097152 | tf_op jit(solution)/shard_map/first/pallas_call | solution.py:123
  1.6 0.7 %collective-permute-start = (bf16[4,64,128]{2,1,0:T(8,128)(2,1)S(1)}, bf16[4,64,128]{2,1,0:T(8,128)(2,1)S(1)}, u32[]{:S(2)}, u32[]{:S(2)}) collective-permute-start(bf16[4,64,128]{2,1,0:T(8,128)(2,1)S(1)} %get-tuple-element.26), channel_id=1, source_target_pairs={{0,1},{1,0},{2,3},{3,2},{4,5},{5,4},{6,7},{7,6},{8,9},{9,8},{10,11... | collective-permute-start | bytes 196616 | tf_op jit(solution)/shard_map/ppermute | solution.py:574
  2.3 3.0 %collective-permute-start.1 = (bf16[4,64,128]{2,1,0:T(8,128)(2,1)S(1)}, bf16[4,64,128]{2,1,0:T(8,128)(2,1)S(1)}, u32[]{:S(2)}, u32[]{:S(2)}) collective-permute-start(bf16[4,64,128]{2,1,0:T(8,128)(2,1)S(1)} %get-tuple-element.27), channel_id=1, source_target_pairs={{1,2},{2,1},{3,4},{4,3},{5,6},{6,5},{7,8},{8,7},{9,10},{10,9},{11,... | collective-permute-start | bytes 196616 | tf_op jit(solution)/shard_map/ppermute | solution.py:574
  5.4 2.8 %inner.2 = (bf16[4,8,64,128]{3,2,1,0:T(8,128)(2,1)S(1)}, f32[4,2,64,128]{3,2,1,0:T(8,128)S(1)}) custom-call(s32[864,128]{1,0:T(8,128)S(1)} %get-tuple-element.23.ids_ref, bf16[4,8,64,128]{3,2,1,0:T(8,128)(2,1)S(1)} %get-tuple-element.28.x_ref, bf16[3456,128]{1,0:T(8,128)(2,1)S(1)} %get-tuple-element.29.w_ref), custom_call_target="tpu_custom_call" | custom-call | flops 1811939328 | bytes 4194304 | tf_op jit(solution)/shard_map/inner/pallas_call | solution.py:200
  8.2 0.0 collective-permute-done.near_ref
  8.2 0.6 %collective-permute-done.1.far_ref = bf16[4,64,128]{2,1,0:T(8,128)(2,1)S(1)} collective-permute-done((bf16[4,64,128]{2,1,0:T(8,128)(2,1)S(1)}, bf16[4,64,128]{2,1,0:T(8,128)(2,1)S(1)}, u32[]{:S(2)}, u32[]{:S(2)}) %collective-permute-start.1) | collective-permute-done | bytes 65568 | tf_op jit(solution)/shard_map/ppermute | solution.py:574
  8.8 0.0 copy-start.1
  8.8 0.0 copy-start.2
  8.8 0.6 %outer_pool.1 = (bf16[4,8,64,128]{3,2,1,0:T(8,128)(2,1)S(1)}, bf16[272,128]{1,0:T(8,128)(2,1)S(1)}, bf16[144,128]{1,0:T(8,128)(2,1)S(1)}) custom-call(s32[864,128]{1,0:T(8,128)S(1)} %get-tuple-element.23.ids_ref, s32[4,128]{1,0:T(4,128)S(1)} %get-tuple-element.25.low_ref, bf16[4,64,128]{2,1,0:T(8,128)(2,1)S(1)} %collective-permute-done.near_ref, ...), custom_call_target="tpu_custom_call" | custom-call | flops 536870912 | bytes 4194304 | tf_op jit(solution)/shard_map/outer_pool/pallas_call | solution.py:322
  9.4 0.1 collective-permute-start.5
  9.5 1.2 %collective-permute-done.5 = bf16[144,128]{1,0:T(8,128)(2,1)S(1)} collective-permute-done((bf16[144,128]{1,0:T(8,128)(2,1)S(1)}, bf16[144,128]{1,0:T(8,128)(2,1)S(1)}, u32[]{:S(2)}, u32[]{:S(2)}) %collective-permute-start.5) | collective-permute-done | bytes 36896 | tf_op jit(solution)/shard_map/ppermute | solution.py:574
  10.7 2.2 %collective-permute-start.6 = (bf16[288,128]{1,0:T(8,128)(2,1)S(1)}, bf16[288,128]{1,0:T(8,128)(2,1)S(1)}, u32[]{:S(2)}, u32[]{:S(2)}) collective-permute-start(bf16[288,128]{1,0:T(8,128)(2,1)S(1)} %pad_maximum_fusion), channel_id=1, source_target_pairs={{1,4},{3,6},{4,1},{5,8},{6,3},{7,10},{8,5},{9,12},{10,7},{11,14},{... | collective-permute-start | bytes 221192 | tf_op jit(solution)/shard_map/ppermute | solution.py:574
  12.9 3.4 %collective-permute-done.6.z_ref = bf16[288,128]{1,0:T(8,128)(2,1)S(1)} collective-permute-done((bf16[288,128]{1,0:T(8,128)(2,1)S(1)}, bf16[288,128]{1,0:T(8,128)(2,1)S(1)}, u32[]{:S(2)}, u32[]{:S(2)}) %collective-permute-start.6) | collective-permute-done | bytes 73760 | tf_op jit(solution)/shard_map/ppermute | solution.py:574
  16.3 0.0 collective-permute-start.7
  16.4 1.4 %collective-permute-start.3 = (bf16[272,128]{1,0:T(8,128)(2,1)S(1)}, bf16[272,128]{1,0:T(8,128)(2,1)S(1)}, u32[]{:S(2)}, u32[]{:S(2)}) collective-permute-start(bf16[272,128]{1,0:T(8,128)(2,1)S(1)} %get-tuple-element.33.own_ref), channel_id=1, source_target_pairs={{0,2},{1,3},{2,0},{3,1},{4,6},{5,7},{6,4},{7,5},{8,10},{9,11},{10,... | collective-permute-start | bytes 208904 | tf_op jit(solution)/shard_map/ppermute | solution.py:574
  17.8 0.7 %collective-permute-start.8 = (bf16[288,128]{1,0:T(8,128)(2,1)S(1)}, bf16[288,128]{1,0:T(8,128)(2,1)S(1)}, u32[]{:S(2)}, u32[]{:S(2)}) collective-permute-start(bf16[288,128]{1,0:T(8,128)(2,1)S(1)} %collective-permute-done.6.z_ref), channel_id=1, source_target_pairs={{0,1},{1,0},{2,3},{3,2},{4,5},{5,4},{6,7},{7,6},{8,9},{9,8},{10,11... | collective-permute-start | bytes 221192 | tf_op jit(solution)/shard_map/ppermute | solution.py:574
  18.5 1.5 %collective-permute-done.7.zy_ref = bf16[288,128]{1,0:T(8,128)(2,1)S(1)} collective-permute-done((bf16[288,128]{1,0:T(8,128)(2,1)S(1)}, bf16[288,128]{1,0:T(8,128)(2,1)S(1)}, u32[]{:S(2)}, u32[]{:S(2)}) %collective-permute-start.7) | collective-permute-done | bytes 73760 | tf_op jit(solution)/shard_map/ppermute | solution.py:574
  20.0 1.6 %collective-permute-start.9 = (bf16[288,128]{1,0:T(8,128)(2,1)S(1)}, bf16[288,128]{1,0:T(8,128)(2,1)S(1)}, u32[]{:S(2)}, u32[]{:S(2)}) collective-permute-start(bf16[288,128]{1,0:T(8,128)(2,1)S(1)} %collective-permute-done.7.zy_ref), channel_id=1, source_target_pairs={{0,1},{1,0},{2,3},{3,2},{4,5},{5,4},{6,7},{7,6},{8,9},{9,8},{10,11... | collective-permute-start | bytes 221192 | tf_op jit(solution)/shard_map/ppermute | solution.py:574
  21.7 0.0 collective-permute-start.2
  21.7 0.0 collective-permute-done.3.y_ref
  21.7 0.9 %collective-permute-start.4 = (bf16[272,128]{1,0:T(8,128)(2,1)S(1)}, bf16[272,128]{1,0:T(8,128)(2,1)S(1)}, u32[]{:S(2)}, u32[]{:S(2)}) collective-permute-start(bf16[272,128]{1,0:T(8,128)(2,1)S(1)} %collective-permute-done.3.y_ref), channel_id=1, source_target_pairs={{0,1},{1,0},{2,3},{3,2},{4,5},{5,4},{6,7},{7,6},{8,9},{9,8},{10,11... | collective-permute-start | bytes 208904 | tf_op jit(solution)/shard_map/ppermute | solution.py:574
  22.5 0.4 %collective-permute-done.2.core_ref = bf16[272,128]{1,0:T(8,128)(2,1)S(1)} collective-permute-done((bf16[272,128]{1,0:T(8,128)(2,1)S(1)}, bf16[272,128]{1,0:T(8,128)(2,1)S(1)}, u32[]{:S(2)}, u32[]{:S(2)}) %collective-permute-start.2) | collective-permute-done | bytes 69664 | tf_op jit(solution)/shard_map/ppermute | solution.py:574
  22.9 0.5 %collective-permute-done.4.yc_ref = bf16[272,128]{1,0:T(8,128)(2,1)S(1)} collective-permute-done((bf16[272,128]{1,0:T(8,128)(2,1)S(1)}, bf16[272,128]{1,0:T(8,128)(2,1)S(1)}, u32[]{:S(2)}, u32[]{:S(2)}) %collective-permute-start.4) | collective-permute-done | bytes 69664 | tf_op jit(solution)/shard_map/ppermute | solution.py:574
  23.4 0.0 collective-permute-done.8.zc_ref
  23.4 0.0 collective-permute-done.9.zyc_ref
  23.4 0.0 copy-done.1
  23.4 0.0 copy-done.2
  23.5 0.0 copy-start
  23.5 3.6 %coarse.1 = (bf16[4,8,64,128]{3,2,1,0:T(8,128)(2,1)S(1)}, bf16[4,64,128]{2,1,0:T(8,128)(2,1)S(1)}, bf16[4,64,128]{2,1,0:T(8,128)(2,1)S(1)}) custom-call(s32[8,128]{1,0:T(8,128)S(1)} %get-tuple-element.24.meta_ref, bf16[272,128]{1,0:T(8,128)(2,1)S(1)} %get-tuple-element.33.own_ref, bf16[272,128]{1,0:T(8,128)(2,1)S(1)} %collective-permute-done.2.core_ref, ...), custom_call_target="tpu_custom_call" | custom-call | flops 2147483648 | bytes 8388608 | tf_op jit(solution)/shard_map/coarse/pallas_call | solution.py:533
  27.1 0.4 %collective-permute-start.10 = (bf16[4,64,128]{2,1,0:T(8,128)(2,1)S(1)}, bf16[4,64,128]{2,1,0:T(8,128)(2,1)S(1)}, u32[]{:S(2)}, u32[]{:S(2)}) collective-permute-start(bf16[4,64,128]{2,1,0:T(8,128)(2,1)S(1)} %get-tuple-element.36), channel_id=1, source_target_pairs={{0,1},{1,0},{2,3},{3,2},{4,5},{5,4},{6,7},{7,6},{8,9},{9,8},{10,11... | collective-permute-start | bytes 196616 | tf_op jit(solution)/shard_map/ppermute | solution.py:574
  27.5 2.2 %collective-permute-start.11 = (bf16[4,64,128]{2,1,0:T(8,128)(2,1)S(1)}, bf16[4,64,128]{2,1,0:T(8,128)(2,1)S(1)}, u32[]{:S(2)}, u32[]{:S(2)}) collective-permute-start(bf16[4,64,128]{2,1,0:T(8,128)(2,1)S(1)} %get-tuple-element.37), channel_id=1, source_target_pairs={{1,2},{2,1},{3,4},{4,3},{5,6},{6,5},{7,8},{8,7},{9,10},{10,9},{11,... | collective-permute-start | bytes 196616 | tf_op jit(solution)/shard_map/ppermute | solution.py:574
  29.8 0.0 copy-done
  29.8 2.8 %inner.3 = (bf16[4,8,64,128]{3,2,1,0:T(8,128)(2,1)S(1)}, f32[4,2,64,128]{3,2,1,0:T(8,128)S(1)}) custom-call(s32[864,128]{1,0:T(8,128)S(1)} %get-tuple-element.23.ids_ref, bf16[4,8,64,128]{3,2,1,0:T(8,128)(2,1)S(1)} %get-tuple-element.38.x_ref, bf16[3456,128]{1,0:T(8,128)(2,1)S(1)} %bitcast.8), custom_call_target="tpu_custom_call" | custom-call | flops 1811939328 | bytes 4194304 | tf_op jit(solution)/shard_map/inner/pallas_call | solution.py:200
  32.6 0.0 collective-permute-done.10.near_ref
  32.6 1.4 %collective-permute-done.11.far_ref = bf16[4,64,128]{2,1,0:T(8,128)(2,1)S(1)} collective-permute-done((bf16[4,64,128]{2,1,0:T(8,128)(2,1)S(1)}, bf16[4,64,128]{2,1,0:T(8,128)(2,1)S(1)}, u32[]{:S(2)}, u32[]{:S(2)}) %collective-permute-start.11) | collective-permute-done | bytes 65568 | tf_op jit(solution)/shard_map/ppermute | solution.py:574
  34.0 1.3 %outer.1 = bf16[4,8,64,128]{3,2,1,0:T(8,128)(2,1)} custom-call(s32[864,128]{1,0:T(8,128)S(1)} %get-tuple-element.23.ids_ref, bf16[4,64,128]{2,1,0:T(8,128)(2,1)S(1)} %collective-permute-done.10.near_ref, bf16[4,64,128]{2,1,0:T(8,128)(2,1)S(1)} %collective-permute-done.11.far_ref, f32[4,2,64,128]{3,2,1,0:T(8,128)S(1)} %get-tuple-element.39.part_ref, ...), custom_call_target="tpu_custom_call" | custom-call | flops 536870912 | bytes 4194304 | tf_op jit(solution)/shard_map/outer/pallas_call | solution.py:281
  (1 shorter events, 0.0 us)
Async XLA Ops:
  1.6 6.6 %collective-permute-start = (bf16[4,64,128]{2,1,0:T(8,128)(2,1)S(1)}, bf16[4,64,128]{2,1,0:T(8,128)(2,1)S(1)}, u32[]{:S(2)}, u32[]{:S(2)}) collective-permute-start(bf16[4,64,128]{2,1,0:T(8,128)(2,1)S(1)} %get-tuple-element.26), channel_id=1, source_target_pairs={{0,1},{1,0},{2,3},{3,2},{4,5},{5,4},{6,7},{7,6},{8,9},{9,8},{10,11... | collective-permute-start | bytes 196616 | tf_op jit(solution)/shard_map/ppermute | solution.py:574
  2.3 6.5 %collective-permute-start.1 = (bf16[4,64,128]{2,1,0:T(8,128)(2,1)S(1)}, bf16[4,64,128]{2,1,0:T(8,128)(2,1)S(1)}, u32[]{:S(2)}, u32[]{:S(2)}) collective-permute-start(bf16[4,64,128]{2,1,0:T(8,128)(2,1)S(1)} %get-tuple-element.27), channel_id=1, source_target_pairs={{1,2},{2,1},{3,4},{4,3},{5,6},{6,5},{7,8},{8,7},{9,10},{10,9},{11,... | collective-permute-start | bytes 196616 | tf_op jit(solution)/shard_map/ppermute | solution.py:574
  8.8 14.7 %copy-start.1 = (bf16[27,128,128]{2,1,0:T(8,128)(2,1)S(1)}, bf16[27,128,128]{2,1,0:T(8,128)(2,1)}, u32[]{:S(2)}) copy-start(bf16[27,128,128]{2,1,0:T(8,128)(2,1)} %param.17) | copy-start | bytes 2654212
  8.8 14.7 %copy-start.2 = (bf16[27,128,128]{2,1,0:T(8,128)(2,1)S(1)}, bf16[27,128,128]{2,1,0:T(8,128)(2,1)}, u32[]{:S(2)}) copy-start(bf16[27,128,128]{2,1,0:T(8,128)(2,1)} %param.18) | copy-start | bytes 2654212
  9.4 1.3 %collective-permute-start.5 = (bf16[144,128]{1,0:T(8,128)(2,1)S(1)}, bf16[144,128]{1,0:T(8,128)(2,1)S(1)}, u32[]{:S(2)}, u32[]{:S(2)}) collective-permute-start(bf16[144,128]{1,0:T(8,128)(2,1)S(1)} %get-tuple-element.34), channel_id=1, source_target_pairs={{0,1},{1,0},{2,3},{3,2},{4,5},{5,4},{6,7},{7,6},{8,9},{9,8},{10,11... | collective-permute-start | bytes 110600 | tf_op jit(solution)/shard_map/ppermute | solution.py:574
  10.7 5.7 %collective-permute-start.6 = (bf16[288,128]{1,0:T(8,128)(2,1)S(1)}, bf16[288,128]{1,0:T(8,128)(2,1)S(1)}, u32[]{:S(2)}, u32[]{:S(2)}) collective-permute-start(bf16[288,128]{1,0:T(8,128)(2,1)S(1)} %pad_maximum_fusion), channel_id=1, source_target_pairs={{1,4},{3,6},{4,1},{5,8},{6,3},{7,10},{8,5},{9,12},{10,7},{11,14},{... | collective-permute-start | bytes 221192 | tf_op jit(solution)/shard_map/ppermute | solution.py:574
  16.3 3.7 %collective-permute-start.7 = (bf16[288,128]{1,0:T(8,128)(2,1)S(1)}, bf16[288,128]{1,0:T(8,128)(2,1)S(1)}, u32[]{:S(2)}, u32[]{:S(2)}) collective-permute-start(bf16[288,128]{1,0:T(8,128)(2,1)S(1)} %collective-permute-done.6.z_ref), channel_id=1, source_target_pairs={{0,2},{1,3},{2,0},{3,1},{4,6},{5,7},{6,4},{7,5},{8,10},{9,11},{10,... | collective-permute-start | bytes 221192 | tf_op jit(solution)/shard_map/ppermute | solution.py:574
  16.4 5.3 %collective-permute-start.3 = (bf16[272,128]{1,0:T(8,128)(2,1)S(1)}, bf16[272,128]{1,0:T(8,128)(2,1)S(1)}, u32[]{:S(2)}, u32[]{:S(2)}) collective-permute-start(bf16[272,128]{1,0:T(8,128)(2,1)S(1)} %get-tuple-element.33.own_ref), channel_id=1, source_target_pairs={{0,2},{1,3},{2,0},{3,1},{4,6},{5,7},{6,4},{7,5},{8,10},{9,11},{10,... | collective-permute-start | bytes 208904 | tf_op jit(solution)/shard_map/ppermute | solution.py:574
  17.8 5.6 %collective-permute-start.8 = (bf16[288,128]{1,0:T(8,128)(2,1)S(1)}, bf16[288,128]{1,0:T(8,128)(2,1)S(1)}, u32[]{:S(2)}, u32[]{:S(2)}) collective-permute-start(bf16[288,128]{1,0:T(8,128)(2,1)S(1)} %collective-permute-done.6.z_ref), channel_id=1, source_target_pairs={{0,1},{1,0},{2,3},{3,2},{4,5},{5,4},{6,7},{7,6},{8,9},{9,8},{10,11... | collective-permute-start | bytes 221192 | tf_op jit(solution)/shard_map/ppermute | solution.py:574
  20.0 3.4 %collective-permute-start.9 = (bf16[288,128]{1,0:T(8,128)(2,1)S(1)}, bf16[288,128]{1,0:T(8,128)(2,1)S(1)}, u32[]{:S(2)}, u32[]{:S(2)}) collective-permute-start(bf16[288,128]{1,0:T(8,128)(2,1)S(1)} %collective-permute-done.7.zy_ref), channel_id=1, source_target_pairs={{0,1},{1,0},{2,3},{3,2},{4,5},{5,4},{6,7},{7,6},{8,9},{9,8},{10,11... | collective-permute-start | bytes 221192 | tf_op jit(solution)/shard_map/ppermute | solution.py:574
  21.7 1.3 %collective-permute-start.2 = (bf16[272,128]{1,0:T(8,128)(2,1)S(1)}, bf16[272,128]{1,0:T(8,128)(2,1)S(1)}, u32[]{:S(2)}, u32[]{:S(2)}) collective-permute-start(bf16[272,128]{1,0:T(8,128)(2,1)S(1)} %get-tuple-element.33.own_ref), channel_id=1, source_target_pairs={{0,1},{1,0},{2,3},{3,2},{4,5},{5,4},{6,7},{7,6},{8,9},{9,8},{10,11... | collective-permute-start | bytes 208904 | tf_op jit(solution)/shard_map/ppermute | solution.py:574
  21.7 1.8 %collective-permute-start.4 = (bf16[272,128]{1,0:T(8,128)(2,1)S(1)}, bf16[272,128]{1,0:T(8,128)(2,1)S(1)}, u32[]{:S(2)}, u32[]{:S(2)}) collective-permute-start(bf16[272,128]{1,0:T(8,128)(2,1)S(1)} %collective-permute-done.3.y_ref), channel_id=1, source_target_pairs={{0,1},{1,0},{2,3},{3,2},{4,5},{5,4},{6,7},{7,6},{8,9},{9,8},{10,11... | collective-permute-start | bytes 208904 | tf_op jit(solution)/shard_map/ppermute | solution.py:574
  23.5 6.3 %copy-start = (bf16[27,128,128]{2,1,0:T(8,128)(2,1)S(1)}, bf16[27,128,128]{2,1,0:T(8,128)(2,1)}, u32[]{:S(2)}) copy-start(bf16[27,128,128]{2,1,0:T(8,128)(2,1)} %param.19) | copy-start | bytes 2654212
  27.1 5.5 %collective-permute-start.10 = (bf16[4,64,128]{2,1,0:T(8,128)(2,1)S(1)}, bf16[4,64,128]{2,1,0:T(8,128)(2,1)S(1)}, u32[]{:S(2)}, u32[]{:S(2)}) collective-permute-start(bf16[4,64,128]{2,1,0:T(8,128)(2,1)S(1)} %get-tuple-element.36), channel_id=1, source_target_pairs={{0,1},{1,0},{2,3},{3,2},{4,5},{5,4},{6,7},{7,6},{8,9},{9,8},{10,11... | collective-permute-start | bytes 196616 | tf_op jit(solution)/shard_map/ppermute | solution.py:574
  27.5 6.5 %collective-permute-start.11 = (bf16[4,64,128]{2,1,0:T(8,128)(2,1)S(1)}, bf16[4,64,128]{2,1,0:T(8,128)(2,1)S(1)}, u32[]{:S(2)}, u32[]{:S(2)}) collective-permute-start(bf16[4,64,128]{2,1,0:T(8,128)(2,1)S(1)} %get-tuple-element.37), channel_id=1, source_target_pairs={{1,2},{2,1},{3,4},{4,3},{5,6},{6,5},{7,8},{8,7},{9,10},{10,9},{11,... | collective-permute-start | bytes 196616 | tf_op jit(solution)/shard_map/ppermute | solution.py:574

commit v8 on v7

--- a/solution.py
+++ b/solution.py
@@ -11,7 +11,7 @@
 LANES = 4
 GROUP = 4
 ENC_GROUP = 1
-DEC_GROUP = 4
+DEC_GROUP = 2
 TILE = 16
 OFFSETS = (-1, 0, 1)
 BF16 = jnp.bfloat16
@@ -151,9 +151,8 @@
     cols[:, :, :, edge + 1] = empty
     for b in range(slots):
         value = x_ref[b].astype(F32).reshape(edge * edge, edge, width)
-        for k, turn in enumerate((1, 0, edge - 1)):
-            moved = pltpu.roll(value, turn, 1) if turn else value
-            stack[k, b] = moved.reshape(edge, edge, edge, width)
+        for k, turn in enumerate((1, edge - 1)):
+            stack[k, b] = pltpu.roll(value, turn, 1).reshape(edge, edge, edge, width)
     weights = pair_weights(w_ref, range(3), width)
     for group in range(0, slots, GROUP):
         bricks = []
@@ -165,11 +164,17 @@
                     ids = ids_ref[line : line + edge][None, None]
                     first, count = {-1: (edge - 1, 1), 0: (0, edge), 1: (0, 1)}[dy]
                     if dy == 0 and k == 1:
-                        value = jnp.where(ids == b, stack[k, b], 0.0)
+                        held = x_ref[b].astype(F32).reshape(edge, edge, edge, width)
+                        value = jnp.where(ids == b, held, 0.0)
                     else:
                         value = jnp.zeros((edge, count, edge, width), F32)
                         for slot in range(slots):
-                            held = stack[k, slot, :, first : first + count]
+                            if k == 1:
+                                row = first // 2 * 2 * edge
+                                held = x_ref[slot, :, row : row + 2 * edge].astype(F32)
+                                held = held.reshape(edge, 2, edge, width)[:, first % 2 : first % 2 + 1]
+                            else:
+                                held = stack[k // 2, slot, :, first : first + count]
                             value = jnp.where(ids == slot, held, value)
                     parts.append(value)
                 full = jnp.concatenate(parts, axis=1)
@@ -207,7 +212,7 @@
         out_specs=(VMEM, VMEM),
         scratch_shapes=[
             pltpu.VMEM((slots, 4, 3, edge + 2, rows // 2, width), BF16),
-            pltpu.VMEM((3, slots, edge, edge, edge, width), F32),
+            pltpu.VMEM((2, slots, edge, edge, edge, width), F32),
         ],
         compiler_params=PARAMS,
         cost_estimate=pl.CostEstimate(

time: 35.4 us -> 35.4 us (level)
  the two profiles are of different devices: /device:TPU:21 before, /device:TPU:15 now
where the time goes in v8:
time: 35.4 us; the launch traced here: 35.2 us
  starting transfers between devices  15.2 us (43%)
  Pallas kernels  12.7 us (36%)
  waiting for transfers between devices  7.19 us (20%)
    ppermute x12, starting transfers between devices, swap(): return lax.ppermute(value, 'gx', pairs)  15.2 us
    ppermute x12, waiting for transfers between devices, swap(): return lax.ppermute(value, 'gx', pairs)  7.19 us
    pallas_call x2, Pallas kernels, inner(): pl.pallas_call(inner_kernel, out_shape=(jax.ShapeDtypeStruct(x.shape, BF1...  5.67 us
    pallas_call x1, Pallas kernels, coarse(): pl.pallas_call(functools.partial(coarse_kernel, coarse_slots), out_shape=...  3.58 us
    pallas_call x1, Pallas kernels, first(): pl.pallas_call(first_kernel, out_shape=(face, face, jax.ShapeDtypeStruct(...  1.56 us
    pallas_call x1, Pallas kernels, outer(): pl.pallas_call(outer_kernel, out_shape=jax.ShapeDtypeStruct(main.shape, B...  1.25 us
  transfers between devices with their start and end apart: 12, of which 7 were waited for; matrix products, arithmetic and copies ran while one was open for 0% of the time, Pallas kernels for 16%

profile of v8, /device:TPU:15, one launch (start us, length us, event | category | flops | bytes accessed | tf_op | source)
XLA Modules:
  0.0 35.2 jit_solution(4658451839581270332)
XLA Ops:
  0.0 1.6 %first.1 = (bf16[4,64,128]{2,1,0:T(8,128)(2,1)S(1)}, bf16[4,64,128]{2,1,0:T(8,128)(2,1)S(1)}, s32[8,128]{1,0:T(8,128)S(1)}, bf16[16,128]{1,0:T(8,128)(2,1)S(1)},...) custom-call(bf16[4,8,64,128]{3,2,1,0:T(8,128)(2,1)} %bitcast.13, ...), custom_call_target="tpu_custom_call" | custom-call | bytes 2097152 | tf_op jit(solution)/shard_map/first/pallas_call | solution.py:123
  1.6 0.7 %collective-permute-start = (bf16[4,64,128]{2,1,0:T(8,128)(2,1)S(1)}, bf16[4,64,128]{2,1,0:T(8,128)(2,1)S(1)}, u32[]{:S(2)}, u32[]{:S(2)}) collective-permute-start(bf16[4,64,128]{2,1,0:T(8,128)(2,1)S(1)} %get-tuple-element.26), channel_id=1, source_target_pairs={{0,1},{1,0},{2,3},{3,2},{4,5},{5,4},{6,7},{7,6},{8,9},{9,8},{10,11... | collective-permute-start | bytes 196616 | tf_op jit(solution)/shard_map/ppermute | solution.py:579
  2.3 3.0 %collective-permute-start.1 = (bf16[4,64,128]{2,1,0:T(8,128)(2,1)S(1)}, bf16[4,64,128]{2,1,0:T(8,128)(2,1)S(1)}, u32[]{:S(2)}, u32[]{:S(2)}) collective-permute-start(bf16[4,64,128]{2,1,0:T(8,128)(2,1)S(1)} %get-tuple-element.27), channel_id=1, source_target_pairs={{1,2},{2,1},{3,4},{4,3},{5,6},{6,5},{7,8},{8,7},{9,10},{10,9},{11,... | collective-permute-start | bytes 196616 | tf_op jit(solution)/shard_map/ppermute | solution.py:579
  5.4 2.8 %inner.2 = (bf16[4,8,64,128]{3,2,1,0:T(8,128)(2,1)S(1)}, f32[4,2,64,128]{3,2,1,0:T(8,128)S(1)}) custom-call(s32[864,128]{1,0:T(8,128)S(1)} %get-tuple-element.23.ids_ref, bf16[4,8,64,128]{3,2,1,0:T(8,128)(2,1)S(1)} %get-tuple-element.28.x_ref, bf16[3456,128]{1,0:T(8,128)(2,1)S(1)} %get-tuple-element.29.w_ref), custom_call_target="tpu_custom_call" | custom-call | flops 1811939328 | bytes 4194304 | tf_op jit(solution)/shard_map/inner/pallas_call | solution.py:205
  8.2 0.0 collective-permute-done.near_ref
  8.2 0.6 %collective-permute-done.1.far_ref = bf16[4,64,128]{2,1,0:T(8,128)(2,1)S(1)} collective-permute-done((bf16[4,64,128]{2,1,0:T(8,128)(2,1)S(1)}, bf16[4,64,128]{2,1,0:T(8,128)(2,1)S(1)}, u32[]{:S(2)}, u32[]{:S(2)}) %collective-permute-start.1) | collective-permute-done | bytes 65568 | tf_op jit(solution)/shard_map/ppermute | solution.py:579
  8.8 0.0 copy-start.1
  8.8 0.0 copy-start.2
  8.8 0.6 %outer_pool.1 = (bf16[4,8,64,128]{3,2,1,0:T(8,128)(2,1)S(1)}, bf16[272,128]{1,0:T(8,128)(2,1)S(1)}, bf16[144,128]{1,0:T(8,128)(2,1)S(1)}) custom-call(s32[864,128]{1,0:T(8,128)S(1)} %get-tuple-element.23.ids_ref, s32[4,128]{1,0:T(4,128)S(1)} %get-tuple-element.25.low_ref, bf16[4,64,128]{2,1,0:T(8,128)(2,1)S(1)} %collective-permute-done.near_ref, ...), custom_call_target="tpu_custom_call" | custom-call | flops 536870912 | bytes 4194304 | tf_op jit(solution)/shard_map/outer_pool/pallas_call | solution.py:327
  9.4 0.1 collective-permute-start.5
  9.5 1.2 %collective-permute-done.5 = bf16[144,128]{1,0:T(8,128)(2,1)S(1)} collective-permute-done((bf16[144,128]{1,0:T(8,128)(2,1)S(1)}, bf16[144,128]{1,0:T(8,128)(2,1)S(1)}, u32[]{:S(2)}, u32[]{:S(2)}) %collective-permute-start.5) | collective-permute-done | bytes 36896 | tf_op jit(solution)/shard_map/ppermute | solution.py:579
  10.7 3.2 %collective-permute-start.6 = (bf16[288,128]{1,0:T(8,128)(2,1)S(1)}, bf16[288,128]{1,0:T(8,128)(2,1)S(1)}, u32[]{:S(2)}, u32[]{:S(2)}) collective-permute-start(bf16[288,128]{1,0:T(8,128)(2,1)S(1)} %pad_maximum_fusion), channel_id=1, source_target_pairs={{1,4},{3,6},{4,1},{5,8},{6,3},{7,10},{8,5},{9,12},{10,7},{11,14},{... | collective-permute-start | bytes 221192 | tf_op jit(solution)/shard_map/ppermute | solution.py:579
  13.9 2.4 %collective-permute-done.6.z_ref = bf16[288,128]{1,0:T(8,128)(2,1)S(1)} collective-permute-done((bf16[288,128]{1,0:T(8,128)(2,1)S(1)}, bf16[288,128]{1,0:T(8,128)(2,1)S(1)}, u32[]{:S(2)}, u32[]{:S(2)}) %collective-permute-start.6) | collective-permute-done | bytes 73760 | tf_op jit(solution)/shard_map/ppermute | solution.py:579
  16.4 0.0 collective-permute-start.7
  16.4 1.4 %collective-permute-start.3 = (bf16[272,128]{1,0:T(8,128)(2,1)S(1)}, bf16[272,128]{1,0:T(8,128)(2,1)S(1)}, u32[]{:S(2)}, u32[]{:S(2)}) collective-permute-start(bf16[272,128]{1,0:T(8,128)(2,1)S(1)} %get-tuple-element.33.own_ref), channel_id=1, source_target_pairs={{0,2},{1,3},{2,0},{3,1},{4,6},{5,7},{6,4},{7,5},{8,10},{9,11},{10,... | collective-permute-start | bytes 208904 | tf_op jit(solution)/shard_map/ppermute | solution.py:579
  17.8 0.7 %collective-permute-start.8 = (bf16[288,128]{1,0:T(8,128)(2,1)S(1)}, bf16[288,128]{1,0:T(8,128)(2,1)S(1)}, u32[]{:S(2)}, u32[]{:S(2)}) collective-permute-start(bf16[288,128]{1,0:T(8,128)(2,1)S(1)} %collective-permute-done.6.z_ref), channel_id=1, source_target_pairs={{0,1},{1,0},{2,3},{3,2},{4,5},{5,4},{6,7},{7,6},{8,9},{9,8},{10,11... | collective-permute-start | bytes 221192 | tf_op jit(solution)/shard_map/ppermute | solution.py:579
  18.5 1.5 %collective-permute-done.7.zy_ref = bf16[288,128]{1,0:T(8,128)(2,1)S(1)} collective-permute-done((bf16[288,128]{1,0:T(8,128)(2,1)S(1)}, bf16[288,128]{1,0:T(8,128)(2,1)S(1)}, u32[]{:S(2)}, u32[]{:S(2)}) %collective-permute-start.7) | collective-permute-done | bytes 73760 | tf_op jit(solution)/shard_map/ppermute | solution.py:579
  20.0 1.6 %collective-permute-start.9 = (bf16[288,128]{1,0:T(8,128)(2,1)S(1)}, bf16[288,128]{1,0:T(8,128)(2,1)S(1)}, u32[]{:S(2)}, u32[]{:S(2)}) collective-permute-start(bf16[288,128]{1,0:T(8,128)(2,1)S(1)} %collective-permute-done.7.zy_ref), channel_id=1, source_target_pairs={{0,1},{1,0},{2,3},{3,2},{4,5},{5,4},{6,7},{7,6},{8,9},{9,8},{10,11... | collective-permute-start | bytes 221192 | tf_op jit(solution)/shard_map/ppermute | solution.py:579
  21.7 0.0 collective-permute-start.2
  21.7 0.0 collective-permute-done.3.y_ref
  21.7 0.9 %collective-permute-start.4 = (bf16[272,128]{1,0:T(8,128)(2,1)S(1)}, bf16[272,128]{1,0:T(8,128)(2,1)S(1)}, u32[]{:S(2)}, u32[]{:S(2)}) collective-permute-start(bf16[272,128]{1,0:T(8,128)(2,1)S(1)} %collective-permute-done.3.y_ref), channel_id=1, source_target_pairs={{0,1},{1,0},{2,3},{3,2},{4,5},{5,4},{6,7},{7,6},{8,9},{9,8},{10,11... | collective-permute-start | bytes 208904 | tf_op jit(solution)/shard_map/ppermute | solution.py:579
  22.5 0.4 %collective-permute-done.2.core_ref = bf16[272,128]{1,0:T(8,128)(2,1)S(1)} collective-permute-done((bf16[272,128]{1,0:T(8,128)(2,1)S(1)}, bf16[272,128]{1,0:T(8,128)(2,1)S(1)}, u32[]{:S(2)}, u32[]{:S(2)}) %collective-permute-start.2) | collective-permute-done | bytes 69664 | tf_op jit(solution)/shard_map/ppermute | solution.py:579
  22.9 0.5 %collective-permute-done.4.yc_ref = bf16[272,128]{1,0:T(8,128)(2,1)S(1)} collective-permute-done((bf16[272,128]{1,0:T(8,128)(2,1)S(1)}, bf16[272,128]{1,0:T(8,128)(2,1)S(1)}, u32[]{:S(2)}, u32[]{:S(2)}) %collective-permute-start.4) | collective-permute-done | bytes 69664 | tf_op jit(solution)/shard_map/ppermute | solution.py:579
  23.4 0.0 collective-permute-done.8.zc_ref
  23.4 0.0 collective-permute-done.9.zyc_ref
  23.4 0.0 copy-done.1
  23.4 0.0 copy-done.2
  23.5 0.0 copy-start
  23.5 3.6 %coarse.1 = (bf16[4,8,64,128]{3,2,1,0:T(8,128)(2,1)S(1)}, bf16[4,64,128]{2,1,0:T(8,128)(2,1)S(1)}, bf16[4,64,128]{2,1,0:T(8,128)(2,1)S(1)}) custom-call(s32[8,128]{1,0:T(8,128)S(1)} %get-tuple-element.24.meta_ref, bf16[272,128]{1,0:T(8,128)(2,1)S(1)} %get-tuple-element.33.own_ref, bf16[272,128]{1,0:T(8,128)(2,1)S(1)} %collective-permute-done.2.core_ref, ...), custom_call_target="tpu_custom_call" | custom-call | flops 2147483648 | bytes 8388608 | tf_op jit(solution)/shard_map/coarse/pallas_call | solution.py:538
  27.1 0.4 %collective-permute-start.10 = (bf16[4,64,128]{2,1,0:T(8,128)(2,1)S(1)}, bf16[4,64,128]{2,1,0:T(8,128)(2,1)S(1)}, u32[]{:S(2)}, u32[]{:S(2)}) collective-permute-start(bf16[4,64,128]{2,1,0:T(8,128)(2,1)S(1)} %get-tuple-element.36), channel_id=1, source_target_pairs={{0,1},{1,0},{2,3},{3,2},{4,5},{5,4},{6,7},{7,6},{8,9},{9,8},{10,11... | collective-permute-start | bytes 196616 | tf_op jit(solution)/shard_map/ppermute | solution.py:579
  27.5 3.0 %collective-permute-start.11 = (bf16[4,64,128]{2,1,0:T(8,128)(2,1)S(1)}, bf16[4,64,128]{2,1,0:T(8,128)(2,1)S(1)}, u32[]{:S(2)}, u32[]{:S(2)}) collective-permute-start(bf16[4,64,128]{2,1,0:T(8,128)(2,1)S(1)} %get-tuple-element.37), channel_id=1, source_target_pairs={{1,2},{2,1},{3,4},{4,3},{5,6},{6,5},{7,8},{8,7},{9,10},{10,9},{11,... | collective-permute-start | bytes 196616 | tf_op jit(solution)/shard_map/ppermute | solution.py:579
  30.5 0.0 copy-done
  30.5 2.8 %inner.3 = (bf16[4,8,64,128]{3,2,1,0:T(8,128)(2,1)S(1)}, f32[4,2,64,128]{3,2,1,0:T(8,128)S(1)}) custom-call(s32[864,128]{1,0:T(8,128)S(1)} %get-tuple-element.23.ids_ref, bf16[4,8,64,128]{3,2,1,0:T(8,128)(2,1)S(1)} %get-tuple-element.38.x_ref, bf16[3456,128]{1,0:T(8,128)(2,1)S(1)} %bitcast.8), custom_call_target="tpu_custom_call" | custom-call | flops 1811939328 | bytes 4194304 | tf_op jit(solution)/shard_map/inner/pallas_call | solution.py:205
  33.3 0.0 collective-permute-done.10.near_ref
  33.3 0.6 %collective-permute-done.11.far_ref = bf16[4,64,128]{2,1,0:T(8,128)(2,1)S(1)} collective-permute-done((bf16[4,64,128]{2,1,0:T(8,128)(2,1)S(1)}, bf16[4,64,128]{2,1,0:T(8,128)(2,1)S(1)}, u32[]{:S(2)}, u32[]{:S(2)}) %collective-permute-start.11) | collective-permute-done | bytes 65568 | tf_op jit(solution)/shard_map/ppermute | solution.py:579
  34.0 1.2 %outer.1 = bf16[4,8,64,128]{3,2,1,0:T(8,128)(2,1)} custom-call(s32[864,128]{1,0:T(8,128)S(1)} %get-tuple-element.23.ids_ref, bf16[4,64,128]{2,1,0:T(8,128)(2,1)S(1)} %collective-permute-done.10.near_ref, bf16[4,64,128]{2,1,0:T(8,128)(2,1)S(1)} %collective-permute-done.11.far_ref, f32[4,2,64,128]{3,2,1,0:T(8,128)S(1)} %get-tuple-element.39.part_ref, ...), custom_call_target="tpu_custom_call" | custom-call | flops 536870912 | bytes 4194304 | tf_op jit(solution)/shard_map/outer/pallas_call | solution.py:286
  (1 shorter events, 0.0 us)
Async XLA Ops:
  1.6 6.6 %collective-permute-start = (bf16[4,64,128]{2,1,0:T(8,128)(2,1)S(1)}, bf16[4,64,128]{2,1,0:T(8,128)(2,1)S(1)}, u32[]{:S(2)}, u32[]{:S(2)}) collective-permute-start(bf16[4,64,128]{2,1,0:T(8,128)(2,1)S(1)} %get-tuple-element.26), channel_id=1, source_target_pairs={{0,1},{1,0},{2,3},{3,2},{4,5},{5,4},{6,7},{7,6},{8,9},{9,8},{10,11... | collective-permute-start | bytes 196616 | tf_op jit(solution)/shard_map/ppermute | solution.py:579
  2.3 6.5 %collective-permute-start.1 = (bf16[4,64,128]{2,1,0:T(8,128)(2,1)S(1)}, bf16[4,64,128]{2,1,0:T(8,128)(2,1)S(1)}, u32[]{:S(2)}, u32[]{:S(2)}) collective-permute-start(bf16[4,64,128]{2,1,0:T(8,128)(2,1)S(1)} %get-tuple-element.27), channel_id=1, source_target_pairs={{1,2},{2,1},{3,4},{4,3},{5,6},{6,5},{7,8},{8,7},{9,10},{10,9},{11,... | collective-permute-start | bytes 196616 | tf_op jit(solution)/shard_map/ppermute | solution.py:579
  8.8 14.7 %copy-start.1 = (bf16[27,128,128]{2,1,0:T(8,128)(2,1)S(1)}, bf16[27,128,128]{2,1,0:T(8,128)(2,1)}, u32[]{:S(2)}) copy-start(bf16[27,128,128]{2,1,0:T(8,128)(2,1)} %param.17) | copy-start | bytes 2654212
  8.8 14.7 %copy-start.2 = (bf16[27,128,128]{2,1,0:T(8,128)(2,1)S(1)}, bf16[27,128,128]{2,1,0:T(8,128)(2,1)}, u32[]{:S(2)}) copy-start(bf16[27,128,128]{2,1,0:T(8,128)(2,1)} %param.18) | copy-start | bytes 2654212
  9.4 1.3 %collective-permute-start.5 = (bf16[144,128]{1,0:T(8,128)(2,1)S(1)}, bf16[144,128]{1,0:T(8,128)(2,1)S(1)}, u32[]{:S(2)}, u32[]{:S(2)}) collective-permute-start(bf16[144,128]{1,0:T(8,128)(2,1)S(1)} %get-tuple-element.34), channel_id=1, source_target_pairs={{0,1},{1,0},{2,3},{3,2},{4,5},{5,4},{6,7},{7,6},{8,9},{9,8},{10,11... | collective-permute-start | bytes 110600 | tf_op jit(solution)/shard_map/ppermute | solution.py:579
  10.7 5.7 %collective-permute-start.6 = (bf16[288,128]{1,0:T(8,128)(2,1)S(1)}, bf16[288,128]{1,0:T(8,128)(2,1)S(1)}, u32[]{:S(2)}, u32[]{:S(2)}) collective-permute-start(bf16[288,128]{1,0:T(8,128)(2,1)S(1)} %pad_maximum_fusion), channel_id=1, source_target_pairs={{1,4},{3,6},{4,1},{5,8},{6,3},{7,10},{8,5},{9,12},{10,7},{11,14},{... | collective-permute-start | bytes 221192 | tf_op jit(solution)/shard_map/ppermute | solution.py:579
  16.4 3.7 %collective-permute-start.7 = (bf16[288,128]{1,0:T(8,128)(2,1)S(1)}, bf16[288,128]{1,0:T(8,128)(2,1)S(1)}, u32[]{:S(2)}, u32[]{:S(2)}) collective-permute-start(bf16[288,128]{1,0:T(8,128)(2,1)S(1)} %collective-permute-done.6.z_ref), channel_id=1, source_target_pairs={{0,2},{1,3},{2,0},{3,1},{4,6},{5,7},{6,4},{7,5},{8,10},{9,11},{10,... | collective-permute-start | bytes 221192 | tf_op jit(solution)/shard_map/ppermute | solution.py:579
  16.4 5.3 %collective-permute-start.3 = (bf16[272,128]{1,0:T(8,128)(2,1)S(1)}, bf16[272,128]{1,0:T(8,128)(2,1)S(1)}, u32[]{:S(2)}, u32[]{:S(2)}) collective-permute-start(bf16[272,128]{1,0:T(8,128)(2,1)S(1)} %get-tuple-element.33.own_ref), channel_id=1, source_target_pairs={{0,2},{1,3},{2,0},{3,1},{4,6},{5,7},{6,4},{7,5},{8,10},{9,11},{10,... | collective-permute-start | bytes 208904 | tf_op jit(solution)/shard_map/ppermute | solution.py:579
  17.8 5.6 %collective-permute-start.8 = (bf16[288,128]{1,0:T(8,128)(2,1)S(1)}, bf16[288,128]{1,0:T(8,128)(2,1)S(1)}, u32[]{:S(2)}, u32[]{:S(2)}) collective-permute-start(bf16[288,128]{1,0:T(8,128)(2,1)S(1)} %collective-permute-done.6.z_ref), channel_id=1, source_target_pairs={{0,1},{1,0},{2,3},{3,2},{4,5},{5,4},{6,7},{7,6},{8,9},{9,8},{10,11... | collective-permute-start | bytes 221192 | tf_op jit(solution)/shard_map/ppermute | solution.py:579
  20.0 3.4 %collective-permute-start.9 = (bf16[288,128]{1,0:T(8,128)(2,1)S(1)}, bf16[288,128]{1,0:T(8,128)(2,1)S(1)}, u32[]{:S(2)}, u32[]{:S(2)}) collective-permute-start(bf16[288,128]{1,0:T(8,128)(2,1)S(1)} %collective-permute-done.7.zy_ref), channel_id=1, source_target_pairs={{0,1},{1,0},{2,3},{3,2},{4,5},{5,4},{6,7},{7,6},{8,9},{9,8},{10,11... | collective-permute-start | bytes 221192 | tf_op jit(solution)/shard_map/ppermute | solution.py:579
  21.7 1.3 %collective-permute-start.2 = (bf16[272,128]{1,0:T(8,128)(2,1)S(1)}, bf16[272,128]{1,0:T(8,128)(2,1)S(1)}, u32[]{:S(2)}, u32[]{:S(2)}) collective-permute-start(bf16[272,128]{1,0:T(8,128)(2,1)S(1)} %get-tuple-element.33.own_ref), channel_id=1, source_target_pairs={{0,1},{1,0},{2,3},{3,2},{4,5},{5,4},{6,7},{7,6},{8,9},{9,8},{10,11... | collective-permute-start | bytes 208904 | tf_op jit(solution)/shard_map/ppermute | solution.py:579
  21.7 1.8 %collective-permute-start.4 = (bf16[272,128]{1,0:T(8,128)(2,1)S(1)}, bf16[272,128]{1,0:T(8,128)(2,1)S(1)}, u32[]{:S(2)}, u32[]{:S(2)}) collective-permute-start(bf16[272,128]{1,0:T(8,128)(2,1)S(1)} %collective-permute-done.3.y_ref), channel_id=1, source_target_pairs={{0,1},{1,0},{2,3},{3,2},{4,5},{5,4},{6,7},{7,6},{8,9},{9,8},{10,11... | collective-permute-start | bytes 208904 | tf_op jit(solution)/shard_map/ppermute | solution.py:579
  23.5 7.0 %copy-start = (bf16[27,128,128]{2,1,0:T(8,128)(2,1)S(1)}, bf16[27,128,128]{2,1,0:T(8,128)(2,1)}, u32[]{:S(2)}) copy-start(bf16[27,128,128]{2,1,0:T(8,128)(2,1)} %param.19) | copy-start | bytes 2654212
  27.1 6.3 %collective-permute-start.10 = (bf16[4,64,128]{2,1,0:T(8,128)(2,1)S(1)}, bf16[4,64,128]{2,1,0:T(8,128)(2,1)S(1)}, u32[]{:S(2)}, u32[]{:S(2)}) collective-permute-start(bf16[4,64,128]{2,1,0:T(8,128)(2,1)S(1)} %get-tuple-element.36), channel_id=1, source_target_pairs={{0,1},{1,0},{2,3},{3,2},{4,5},{5,4},{6,7},{7,6},{8,9},{9,8},{10,11... | collective-permute-start | bytes 196616 | tf_op jit(solution)/shard_map/ppermute | solution.py:579
  27.5 6.5 %collective-permute-start.11 = (bf16[4,64,128]{2,1,0:T(8,128)(2,1)S(1)}, bf16[4,64,128]{2,1,0:T(8,128)(2,1)S(1)}, u32[]{:S(2)}, u32[]{:S(2)}) collective-permute-start(bf16[4,64,128]{2,1,0:T(8,128)(2,1)S(1)} %get-tuple-element.37), channel_id=1, source_target_pairs={{1,2},{2,1},{3,4},{4,3},{5,6},{6,5},{7,8},{8,7},{9,10},{10,9},{11,... | collective-permute-start | bytes 196616 | tf_op jit(solution)/shard_map/ppermute | solution.py:579
